TPU v7x, 256 devices: a whole 4x4x8 slice. The times are simulated.
256 devices in a mesh: seq: 32 (over y_lo, z, core), fsdp: 8 (over y_hi, x).
Axes of the slice: x: 4, y: 4 (y_hi: 2, y_lo: 2; y = y_hi * 2 + y_lo), z: 8, core: 2. Of those that a mesh axis runs over, the one named last changes fastest.
Arguments:
- tokens: bfloat16 [8, 32768, 1024], P('fsdp', 'seq'), may hold values from -6 to 6
- qkv_base: bfloat16 [1024, 3072], P('fsdp'), may hold values from -1 to 1
- qkv_dir: bfloat16 [1024, 3072], P('fsdp'), may hold values from -0.1875 to 0.1875
- out_base: bfloat16 [1024, 1024], P('fsdp'), may hold values from -0.1875 to 0.1875
- out_dir: bfloat16 [1024, 1024], P('fsdp'), may hold values from -0.1875 to 0.1875
- alpha_index: int32 [1], replicated, may hold values from 0 to 1023
Outputs:
- attn_delta: bfloat16 [8, 32768, 1024], P('fsdp', 'seq')
All inputs are finite; a program needn't handle non-finite values.
Results may differ from a plain program's by a relative error of at most 0.011.
Values may be sent and summed in bfloat16 or wider, within the bound.
No kernel may reach another device: no remote copies, remote signals or barrier semaphores. Data moves between devices by JAX's collectives and lax.ppermute only.
A program may use at most 192 MiB of HBM per device.

v0:
```python
import functools
import math

import jax
import jax.numpy as jnp
from jax import lax
from jax.experimental import pallas as pl
from jax.experimental.pallas import tpu as pltpu
from jax.sharding import PartitionSpec as P

D = 1024
HEADS = 16
STRIDE = 1024
NALPHA = 1024
HEAD_DIM = D // HEADS
HALF = D // 2
PAIR = 2 * HEAD_DIM
COLS_AT, ROWS_AT, OUT_AT = 0, 768, 1536
SLAB = 2048
F32, BF16 = jnp.float32, jnp.bfloat16
LOG2_SCALE = math.log2(math.e) / math.sqrt(HEAD_DIM)
BOTH = ("seq", "fsdp")


def split_index(i):
    s, f = divmod(i, 8)
    return s // 16, (s // 2) % 8, s % 2, f // 4, f % 4


def pairs(move):
    out = []
    for i in range(256):
        yl, z, c, yh, x = move(*split_index(i))
        out.append((i, ((yl * 8 + z) * 2 + c) * 8 + yh * 4 + x))
    return out


X_UP = pairs(lambda yl, z, c, yh, x: (yl, z, c, yh, (x + 1) % 4))
X_DOWN = pairs(lambda yl, z, c, yh, x: (yl, z, c, yh, (x - 1) % 4))
Y_NEAR = pairs(lambda yl, z, c, yh, x: (1 - yl, z, c, 1 - yh, x))
CORE = pairs(lambda yl, z, c, yh, x: (yl, z, 1 - c, yh, x))


def send(value, where):
    return lax.ppermute(value, BOTH, where)


def normalized(rows):
    mean_square = jnp.mean(rows * rows, axis=-1, keepdims=True)
    return (rows * lax.rsqrt(mean_square + 1e-06)).astype(BF16)


def fetch_weights(slabs, first, width, dest, sems):
    core = lax.axis_index("seq") % 2
    mine = lax.axis_index("fsdp")
    copies = []
    for n, slab in enumerate(slabs):
        half = core if n < 2 else 1 - core
        y_hi = mine // 4 if n % 2 == 0 else 1 - mine // 4
        for k in range(4):
            feature = pl.multiple_of((y_hi * 4 + (mine % 4 - k + 4) % 4) * 128, 128)
            copy = pltpu.make_async_copy(
                slab.at[k, :, pl.ds(first, width)],
                dest.at[half, pl.ds(feature, 128), :],
                sems.at[n * 4 + k],
            )
            copy.start()
            copies.append(copy)
    return copies


def soft_average(queries, keys, values_ones, mask):
    scores = lax.dot_general(queries, keys, (((1,), (1,)), ((), ())), preferred_element_type=F32)
    if mask is not None:
        width = mask.shape[1]
        last = scores[:, -width:] + mask
        scores = last if width == scores.shape[1] else jnp.concatenate([scores[:, :-width], last], 1)
    peak = jnp.max(scores, axis=-1, keepdims=True)
    weights = jnp.exp2((scores - peak) * LOG2_SCALE).astype(BF16)
    both = jnp.dot(weights, values_ones, preferred_element_type=F32)
    return both[:, :PAIR] / both[:, PAIR:]


def pair_attend(q, k, v, mask):
    rows = q.shape[0]
    first = lax.broadcasted_iota(jnp.int32, (rows, PAIR), 1) < HEAD_DIM
    nothing = jnp.zeros_like(q)
    values_ones = jnp.concatenate([v, jnp.ones_like(v)], 1)
    even = soft_average(jnp.where(first, q, nothing), k, values_ones, mask)
    odd = soft_average(jnp.where(first, nothing, q), k, values_ones, mask)
    return jnp.where(first, even, odd).astype(BF16)


def row_kernel(x_ref, s0, s1, s2, s3, o_ref, w, qkv, mask_ref, sems):
    copies = fetch_weights((s0, s1, s2, s3), ROWS_AT, 768, w, sems)
    block = 256
    row = lax.broadcasted_iota(jnp.int32, (block, block), 0)
    col = lax.broadcasted_iota(jnp.int32, (block, block), 1)
    mask_ref[...] = jnp.where(col <= row, 0.0, -jnp.inf)
    for copy in copies:
        copy.wait()

    def project(i, _):
        at = pl.ds(pl.multiple_of(i * block, block), block)
        normed = normalized(x_ref[at, :].astype(F32))
        for half in range(2):
            made = jnp.dot(normed, w[half], preferred_element_type=F32).astype(BF16)
            for which in range(3):
                for p in range(2):
                    lane = which * 256 + p * PAIR
                    qkv[which, half * 2 + p, at, :] = made[:, lane : lane + PAIR]
        return 0

    lax.fori_loop(0, STRIDE // block, project, 0)

    for p in range(4):
        for i in range(STRIDE // block):
            upto = (i + 1) * block
            o_ref[i * block : upto, p * PAIR : (p + 1) * PAIR] = pair_attend(
                qkv[0, p, i * block : upto, :],
                qkv[1, p, :upto, :],
                qkv[2, p, :upto, :],
                mask_ref[...],
            )


def col_kernel(x_ref, s0, s1, s2, s3, o_ref, w, mask_ref, sems):
    copies = fetch_weights((s0, s1, s2, s3), COLS_AT, 768, w, sems)
    rows = x_ref.shape[0]
    size = rows * 8
    at = lax.broadcasted_iota(jnp.int32, (size, size), 0)
    to = lax.broadcasted_iota(jnp.int32, (size, size), 1)
    meets = jnp.logical_and(at % 8 == to % 8, to <= at)
    mask_ref[...] = jnp.where(meets, 0.0, -jnp.inf)
    for copy in copies:
        copy.wait()
    for wide in range(x_ref.shape[1] // 16):
        taken = x_ref[:, wide * 16 : (wide + 1) * 16, :].astype(F32)
        parts = []
        for part in range(2):
            normed = normalized(taken[:, part * 8 : (part + 1) * 8, :].reshape(size, D))
            done = []
            for half in range(2):
                made = jnp.dot(normed, w[half], preferred_element_type=F32).astype(BF16)
                for p in range(2):
                    q, k, v = (
                        made[:, which * 256 + p * PAIR : which * 256 + (p + 1) * PAIR]
                        for which in range(3)
                    )
                    done.append(pair_attend(q, k, v, mask_ref[...]))
            parts.append(jnp.concatenate(done, 1).astype(F32).reshape(rows, 8, HALF))
        o_ref[:, wide * 16 : (wide + 1) * 16, :] = jnp.concatenate(parts, 1).astype(BF16)


def out_kernel(row_ref, col_ref, s0, s1, s2, s3, o_ref, w, sems):
    @pl.when(pl.program_id(0) == 0)
    def _():
        for copy in fetch_weights((s0, s1, s2, s3), OUT_AT, 512, w, sems):
            copy.wait()

    for half in range(2):
        total = jnp.dot(row_ref[...], w[half, :HALF, :], preferred_element_type=F32)
        total += jnp.dot(col_ref[...], w[half, HALF:, :], preferred_element_type=F32)
        o_ref[:, half * 512 : (half + 1) * 512] = total.astype(BF16)


ANY = pl.BlockSpec(memory_space=pl.ANY)
WHOLE = pl.BlockSpec(memory_space=pltpu.VMEM)
LIMIT = 48 << 20


def row_heads(sequence, slabs):
    return pl.pallas_call(
        row_kernel,
        out_shape=jax.ShapeDtypeStruct((STRIDE, HALF), BF16),
        in_specs=[WHOLE] + [ANY] * 4,
        out_specs=WHOLE,
        scratch_shapes=[
            pltpu.VMEM((2, D, 768), BF16),
            pltpu.VMEM((3, 4, STRIDE, PAIR), BF16),
            pltpu.VMEM((256, 256), F32),
            pltpu.SemaphoreType.DMA((16,)),
        ],
        compiler_params=pltpu.CompilerParams(vmem_limit_bytes=LIMIT),
        cost_estimate=pl.CostEstimate(
            flops=6_000_000_000, bytes_accessed=6 << 20, transcendentals=5_000_000
        ),
        name="row_heads",
    )(sequence, *slabs)


def col_heads(columns, slabs):
    rows, cols = columns.shape[:2]
    return pl.pallas_call(
        col_kernel,
        out_shape=jax.ShapeDtypeStruct((rows, cols, HALF), BF16),
        in_specs=[WHOLE] + [ANY] * 4,
        out_specs=WHOLE,
        scratch_shapes=[
            pltpu.VMEM((2, D, 768), BF16),
            pltpu.VMEM((rows * 8, rows * 8), F32),
            pltpu.SemaphoreType.DMA((16,)),
        ],
        compiler_params=pltpu.CompilerParams(vmem_limit_bytes=LIMIT),
        cost_estimate=pl.CostEstimate(
            flops=4_000_000_000, bytes_accessed=6 << 20, transcendentals=2_000_000
        ),
        name="col_heads",
    )(columns, *slabs)


def project_out(row_out, col_out, slabs):
    block = 256
    return pl.pallas_call(
        out_kernel,
        out_shape=jax.ShapeDtypeStruct((STRIDE, D), BF16),
        grid=(STRIDE // block,),
        in_specs=[pl.BlockSpec((block, HALF), lambda i: (i, 0))] * 2 + [ANY] * 4,
        out_specs=pl.BlockSpec((block, D), lambda i: (i, 0)),
        scratch_shapes=[pltpu.VMEM((2, D, 512), BF16), pltpu.SemaphoreType.DMA((16,))],
        compiler_params=pltpu.CompilerParams(vmem_limit_bytes=LIMIT),
        cost_estimate=pl.CostEstimate(
            flops=2_000_000_000, bytes_accessed=6 << 20, transcendentals=0
        ),
        name="project_out",
    )(row_out, col_out, *slabs)


def rebuild(base_part, direction, step_alpha):
    return (base_part.astype(F32) + step_alpha * direction.astype(F32)).astype(BF16)


def core_half(qkv, out, core):
    picked = lax.dynamic_index_in_dim(qkv.reshape(-1, 3, 2, 2, 256), core, 3, keepdims=False)
    parts = [picked[:, which, kind] for kind in (1, 0) for which in range(3)]
    parts.append(lax.dynamic_slice_in_dim(out, core * 512, 512, 1))
    return jnp.concatenate(parts, 1)


def shards(tokens, qkv_base, qkv_dir, out_base, out_dir, alpha_index):
    step_alpha = (alpha_index[0].astype(F32) + NALPHA) / (2.0 * NALPHA)
    core = lax.axis_index("seq") % 2
    sequence = tokens[0]
    columns = lax.all_to_all(
        sequence.reshape(32, 32, D), "seq", split_axis=0, concat_axis=0, tiled=True
    )
    own = rebuild(
        core_half(qkv_base, out_base, core), core_half(qkv_dir, out_dir, core), step_alpha
    )

    def around(piece):
        below, above = send(piece, X_UP), send(piece, X_DOWN)
        far = jnp.concatenate(
            [send(below[:, : SLAB // 2], X_UP), send(above[:, SLAB // 2 :], X_DOWN)], 1
        )
        return jnp.stack([piece, below, far, above])

    other = send(own, Y_NEAR)
    near_slab = around(own)
    far_slab = around(other)
    slabs = (near_slab, far_slab, send(near_slab, CORE), send(far_slab, CORE))
    attended = col_heads(columns, slabs)
    col_out = lax.all_to_all(attended, "seq", split_axis=0, concat_axis=0, tiled=True)
    row_out = row_heads(sequence, slabs)
    return project_out(row_out, col_out.reshape(STRIDE, HALF), slabs)[None]


def solution(mesh):
    in_specs = (
        P("fsdp", "seq", None),
        P("fsdp", None),
        P("fsdp", None),
        P("fsdp", None),
        P("fsdp", None),
        P(),
    )
    out_specs = P("fsdp", "seq", None)
    return jax.shard_map(shards, mesh=mesh, in_specs=in_specs, out_specs=out_specs, check_vma=False)
```

profile of v0, /device:TPU:1, one launch (start us, length us, event | category | flops | bytes accessed | tf_op | source)
XLA Modules:
  0.0 125.3 jit_solution(2302788514826438184)
XLA Ops:
  0.7 2.6 %reshape.223 = bf16[128,3,2,2,256]{4,3,2,1,0:T(2,128)(2,1)S(1)} reshape(bf16[128,3072]{1,0:T(8,128)(2,1)} %param.7) | data formatting | bytes 1572864 | tf_op jit(solution)/shard_map/reshape | solution.py:234
  3.3 0.0 copy-done.5
  3.3 0.6 reshape.224
  3.9 1.6 %constant_dynamic-slice_fusion = (bf16[128,3,2,1,256]{4,3,2,1,0:T(2,128)(2,1)S(1)}, bf16[128,3,2,1,256]{4,3,2,1,0:T(2,128)(2,1)S(1)}) fusion(bf16[128,3,2,2,256]{4,3,2,1,0:T(2,128)(2,1)S(1)} %reshape.224, s32[]{:T(128)S(6)} %select_n.17, bf16[128,3,2,2,256]{4,3,2,1,0:T(2,128)(2,1)S(1)} %reshape.223), kind=kLoop, calls=%fused_computation.36 | loop fusion | bytes 1572868 | tf_op jit(solution)/shard_map/jit(dynamic_index_in_dim)/dynamic_slice | solution.py:234
  5.5 0.0 copy-start.6
  5.5 0.0 copy-start.7
  5.5 0.1 copy.13
  5.6 0.1 copy.14
  5.9 0.6 copy-done.6
  6.5 0.1 copy-done.7
  6.6 1.0 add_convert_fusion
  7.5 3.6 %collective-permute-start.4 = (bf16[128,2048]{1,0:T(8,128)(2,1)}, bf16[128,2048]{1,0:T(8,128)(2,1)}, u32[]{:S(2)}, u32[]{:S(2)}) collective-permute-start(bf16[128,2048]{1,0:T(8,128)(2,1)} %add_convert_fusion), channel_id=1, source_target_pairs={{0,132},{1,133},{2,134},{3,135},{4,128},{5,129},{6,130},{7,131},{8... | collective-permute-start | bytes 1572872 | tf_op jit(solution)/shard_map/ppermute | solution.py:45
  11.1 2.5 %collective-permute-start.2 = (bf16[128,2048]{1,0:T(8,128)(2,1)}, bf16[128,2048]{1,0:T(8,128)(2,1)S(1)}, u32[]{:S(2)}, u32[]{:S(2)}) collective-permute-start(bf16[128,2048]{1,0:T(8,128)(2,1)} %add_convert_fusion), channel_id=1, source_target_pairs={{0,3},{1,0},{2,1},{3,2},{4,7},{5,4},{6,5},{7,6},{8,11},{9,8},{10,9... | collective-permute-start | bytes 1572872 | tf_op jit(solution)/shard_map/ppermute | solution.py:45
  13.6 0.0 collective-permute-start
  13.6 9.9 %all-to-all-start = ((bf16[32,32,1024]{2,1,0:T(8,128)(2,1)}), bf16[32,32,1024]{2,1,0:T(8,128)(2,1)}, u32[]{:S(2)}, u32[]{:S(2)}) async-start(bf16[32,32,1024]{2,1,0:T(8,128)(2,1)} %bitcast.37), calls=%async_computation | async-start | bytes 4194304 | tf_op jit(solution)/shard_map/all_to_all | solution.py:244
  23.7 0.4 collective-permute-done.2
  24.2 3.4 %collective-permute-start.3 = (bf16[128,1024]{1,0:T(8,128)(2,1)S(1)}, bf16[128,1024]{1,0:T(8,128)(2,1)S(1)}, u32[]{:S(2)}, u32[]{:S(2)}) collective-permute-start(bf16[128,1024]{1,0:T(8,128)(2,1)S(1)} %slice.77), channel_id=1, source_target_pairs={{0,3},{1,0},{2,1},{3,2},{4,7},{5,4},{6,5},{7,6},{8,11},{9,8},{10,9... | collective-permute-start | bytes 786440 | tf_op jit(solution)/shard_map/ppermute | solution.py:45
  27.6 0.0 collective-permute-done
  27.6 0.1 collective-permute-start.1
  27.7 0.0 collective-permute-done.4
  27.7 2.7 %collective-permute-start.7 = (bf16[128,2048]{1,0:T(8,128)(2,1)}, bf16[128,2048]{1,0:T(8,128)(2,1)S(1)}, u32[]{:S(2)}, u32[]{:S(2)}) collective-permute-start(bf16[128,2048]{1,0:T(8,128)(2,1)} %collective-permute-done.4), channel_id=1, source_target_pairs={{0,3},{1,0},{2,1},{3,2},{4,7},{5,4},{6,5},{7,6},{8,11},{9,8},{10,9... | collective-permute-start | bytes 1572872 | tf_op jit(solution)/shard_map/ppermute | solution.py:45
  30.4 0.0 collective-permute-start.5
  30.4 0.2 add_convert_fusion.1
  30.5 0.8 collective-permute-done.3
  31.3 3.3 %collective-permute-done.1 = bf16[128,1024]{1,0:T(8,128)(2,1)S(1)} collective-permute-done((bf16[128,1024]{1,0:T(8,128)(2,1)S(1)}, bf16[128,1024]{1,0:T(8,128)(2,1)S(1)}, u32[]{:S(2)}, u32[]{:S(2)}) %collective-permute-start.1) | collective-permute-done | bytes 262176 | tf_op jit(solution)/shard_map/ppermute | solution.py:45
  34.7 8.0 %collective-permute-done.7 = bf16[128,2048]{1,0:T(8,128)(2,1)S(1)} collective-permute-done((bf16[128,2048]{1,0:T(8,128)(2,1)}, bf16[128,2048]{1,0:T(8,128)(2,1)S(1)}, u32[]{:S(2)}, u32[]{:S(2)}) %collective-permute-start.7) | collective-permute-done | bytes 524320 | tf_op jit(solution)/shard_map/ppermute | solution.py:45
  42.7 3.4 %collective-permute-start.8 = (bf16[128,1024]{1,0:T(8,128)(2,1)S(1)}, bf16[128,1024]{1,0:T(8,128)(2,1)S(1)}, u32[]{:S(2)}, u32[]{:S(2)}) collective-permute-start(bf16[128,1024]{1,0:T(8,128)(2,1)S(1)} %slice.79), channel_id=1, source_target_pairs={{0,3},{1,0},{2,1},{3,2},{4,7},{5,4},{6,5},{7,6},{8,11},{9,8},{10,9... | collective-permute-start | bytes 786440 | tf_op jit(solution)/shard_map/ppermute | solution.py:45
  46.0 0.0 collective-permute-done.5
  46.1 0.3 collective-permute-start.6
  46.3 0.3 pad_maximum_fusion.s0
  46.6 3.2 %collective-permute-start.9 = (bf16[4,128,2048]{2,1,0:T(8,128)(2,1)S(1)}, bf16[4,128,2048]{2,1,0:T(8,128)(2,1)S(1)}, u32[]{:S(2)}, u32[]{:S(2)}) collective-permute-start(bf16[4,128,2048]{2,1,0:T(8,128)(2,1)S(1)} %pad_maximum_fusion.s0), channel_id=1, source_target_pairs={{0,8},{1,9},{2,10},{3,11},{4,12},{5,13},{6,14},{7,15},{8,0},{9,1},... | collective-permute-start | bytes 6291464 | tf_op jit(solution)/shard_map/ppermute | solution.py:45
  49.8 0.0 collective-permute-done.8
  49.8 3.4 %collective-permute-done.6 = bf16[128,1024]{1,0:T(8,128)(2,1)S(1)} collective-permute-done((bf16[128,1024]{1,0:T(8,128)(2,1)S(1)}, bf16[128,1024]{1,0:T(8,128)(2,1)S(1)}, u32[]{:S(2)}, u32[]{:S(2)}) %collective-permute-start.6) | collective-permute-done | bytes 262176 | tf_op jit(solution)/shard_map/ppermute | solution.py:45
  53.2 1.3 %pad_maximum_fusion.1.s1 = bf16[4,128,2048]{2,1,0:T(8,128)(2,1)S(1)} fusion(bf16[1,128,2048]{2,1,0:T(8,128)(2,1)S(1)} %bitcast.99, bf16[1,128,2048]{2,1,0:T(8,128)(2,1)S(1)} %maximum_bitcast_fusion.1, bf16[1,128,2048]{2,1,0:T(8,128)(2,1)S(1)} %bitcast.100, bf16[1,128,2048]{2,1,0:T(8,128)(2,1)} %bitcast.33), kind=kLoop, calls=%fused_computation.1 | loop fusion | flops 3145728 | bytes 4194304 | tf_op jit(solution)/shard_map/stack | solution.py:256
  54.5 3.9 %collective-permute-start.10 = (bf16[4,128,2048]{2,1,0:T(8,128)(2,1)S(1)}, bf16[4,128,2048]{2,1,0:T(8,128)(2,1)}, u32[]{:S(2)}, u32[]{:S(2)}) collective-permute-start(bf16[4,128,2048]{2,1,0:T(8,128)(2,1)S(1)} %pad_maximum_fusion.1.s1), channel_id=1, source_target_pairs={{0,8},{1,9},{2,10},{3,11},{4,12},{5,13},{6,14},{7,15},{8,0},{9,1},... | collective-permute-start | bytes 6291464 | tf_op jit(solution)/shard_map/ppermute | solution.py:45
  58.4 0.0 collective-permute-done.9.s2
  58.4 1.3 %copy-done.4 = bf16[4,128,2048]{2,1,0:T(8,128)(2,1)} copy-done((bf16[4,128,2048]{2,1,0:T(8,128)(2,1)}, bf16[4,128,2048]{2,1,0:T(8,128)(2,1)S(1)}, u32[]{:S(2)}) %copy-start.4) | copy-done | bytes 2097176
  59.8 2.6 %collective-permute-done.10.s3 = bf16[4,128,2048]{2,1,0:T(8,128)(2,1)} collective-permute-done((bf16[4,128,2048]{2,1,0:T(8,128)(2,1)S(1)}, bf16[4,128,2048]{2,1,0:T(8,128)(2,1)}, u32[]{:S(2)}, u32[]{:S(2)}) %collective-permute-start.10) | collective-permute-done | bytes 2097184 | tf_op jit(solution)/shard_map/ppermute | solution.py:45
  62.3 10.6 %all-to-all-done.x_ref = bf16[32,32,1024]{2,1,0:T(8,128)(2,1)} async-done(((bf16[32,32,1024]{2,1,0:T(8,128)(2,1)}), bf16[32,32,1024]{2,1,0:T(8,128)(2,1)}, u32[]{:S(2)}, u32[]{:S(2)}) %all-to-all-start) | async-done | bytes 2097184 | tf_op jit(solution)/shard_map/all_to_all | solution.py:244
  72.9 12.6 %col_heads.1 = bf16[32,32,512]{2,1,0:T(8,128)(2,1)S(1)} custom-call(bf16[32,32,1024]{2,1,0:T(8,128)(2,1)} %all-to-all-done.x_ref, bf16[4,128,2048]{2,1,0:T(8,128)(2,1)S(1)} %pad_maximum_fusion.s0, bf16[4,128,2048]{2,1,0:T(8,128)(2,1)} %copy-done.3, bf16[4,128,2048]{2,1,0:T(8,128)(2,1)} %copy-done.4, bf16[4,128,2048]{2,1,0:T(8,128)(2,1)} %collective-permute-done.10.s3), custom_call_target="tpu_custom_call" | custom-call | flops 4000000000 | bytes 6291456 | tf_op jit(solution)/shard_map/col_heads/pallas_call | solution.py:194
  85.6 1.0 copy-done.2
  86.6 5.5 %all-to-all-start.1 = ((bf16[32,32,512]{2,1,0:T(8,128)(2,1)}), bf16[32,32,512]{2,1,0:T(8,128)(2,1)S(1)}, u32[]{:S(2)}, u32[]{:S(2)}) async-start(bf16[32,32,512]{2,1,0:T(8,128)(2,1)} %copy-done.2), calls=%async_computation.1 | async-start | bytes 2097152 | tf_op jit(solution)/shard_map/all_to_all | solution.py:263
  92.1 16.7 %row_heads.1.row_ref = bf16[1024,512]{1,0:T(8,128)(2,1)S(1)} custom-call(bf16[1024,1024]{1,0:T(8,128)(2,1)} %bitcast.x_ref, bf16[4,128,2048]{2,1,0:T(8,128)(2,1)S(1)} %pad_maximum_fusion.s0, bf16[4,128,2048]{2,1,0:T(8,128)(2,1)} %copy-done.3, bf16[4,128,2048]{2,1,0:T(8,128)(2,1)} %copy-done.4, bf16[4,128,2048]{2,1,0:T(8,128)(2,1)} %collective-permute-done.10.s3), custom_call_target="tpu_custom_call" | custom-call | flops 6000000000 | bytes 6291456 | tf_op jit(solution)/shard_map/row_heads/pallas_call | solution.py:173
  108.8 0.0 copy-start
  108.8 1.0 copy-done
  109.8 8.7 %all-to-all-done.1 = bf16[32,32,512]{2,1,0:T(8,128)(2,1)S(1)} async-done(((bf16[32,32,512]{2,1,0:T(8,128)(2,1)}), bf16[32,32,512]{2,1,0:T(8,128)(2,1)S(1)}, u32[]{:S(2)}, u32[]{:S(2)}) %all-to-all-start.1) | async-done | bytes 1048608 | tf_op jit(solution)/shard_map/all_to_all | solution.py:263
  118.4 1.2 copy-done.1
  119.7 5.4 %project_out.1 = bf16[1024,1024]{1,0:T(8,128)(2,1)} custom-call(bf16[1024,512]{1,0:T(8,128)(2,1)S(1)} %copy-done.1, bf16[1024,512]{1,0:T(8,128)(2,1)S(1)} %bitcast.72, bf16[4,128,2048]{2,1,0:T(8,128)(2,1)S(1)} %pad_maximum_fusion.s0, bf16[4,128,2048]{2,1,0:T(8,128)(2,1)} %copy-done.3, bf16[4,128,2048]{2,1,0:T(8,128)(2,1)} %copy-done.4, ...), custom_call_target="tpu_custom_call" | custom-call | flops 2000000000 | bytes 6291456 | tf_op jit(solution)/shard_map/project_out/pallas_call | solution.py:214
  (40 shorter events, 0.4 us)
Async XLA Ops:
  0.0 3.3 %copy-start.5 = (bf16[128,3072]{1,0:T(8,128)(2,1)S(1)}, bf16[128,3072]{1,0:T(8,128)(2,1)}, u32[]{:S(2)}) copy-start(bf16[128,3072]{1,0:T(8,128)(2,1)} %param.8) | copy-start | bytes 2359300
  5.5 1.0 copy-start.6
  5.5 1.0 copy-start.7
  7.5 20.2 %collective-permute-start.4 = (bf16[128,2048]{1,0:T(8,128)(2,1)}, bf16[128,2048]{1,0:T(8,128)(2,1)}, u32[]{:S(2)}, u32[]{:S(2)}) collective-permute-start(bf16[128,2048]{1,0:T(8,128)(2,1)} %add_convert_fusion), channel_id=1, source_target_pairs={{0,132},{1,133},{2,134},{3,135},{4,128},{5,129},{6,130},{7,131},{8... | collective-permute-start | bytes 1572872 | tf_op jit(solution)/shard_map/ppermute | solution.py:45
  11.1 13.1 %collective-permute-start.2 = (bf16[128,2048]{1,0:T(8,128)(2,1)}, bf16[128,2048]{1,0:T(8,128)(2,1)S(1)}, u32[]{:S(2)}, u32[]{:S(2)}) collective-permute-start(bf16[128,2048]{1,0:T(8,128)(2,1)} %add_convert_fusion), channel_id=1, source_target_pairs={{0,3},{1,0},{2,1},{3,2},{4,7},{5,4},{6,5},{7,6},{8,11},{9,8},{10,9... | collective-permute-start | bytes 1572872 | tf_op jit(solution)/shard_map/ppermute | solution.py:45
  13.6 14.0 %collective-permute-start = (bf16[128,2048]{1,0:T(8,128)(2,1)}, bf16[128,2048]{1,0:T(8,128)(2,1)S(1)}, u32[]{:S(2)}, u32[]{:S(2)}) collective-permute-start(bf16[128,2048]{1,0:T(8,128)(2,1)} %add_convert_fusion), channel_id=1, source_target_pairs={{0,1},{1,2},{2,3},{3,0},{4,5},{5,6},{6,7},{7,4},{8,9},{9,10},{10,1... | collective-permute-start | bytes 1572872 | tf_op jit(solution)/shard_map/ppermute | solution.py:45
  13.6 59.4 %all-to-all-start = ((bf16[32,32,1024]{2,1,0:T(8,128)(2,1)}), bf16[32,32,1024]{2,1,0:T(8,128)(2,1)}, u32[]{:S(2)}, u32[]{:S(2)}) async-start(bf16[32,32,1024]{2,1,0:T(8,128)(2,1)} %bitcast.37), calls=%async_computation | async-start | bytes 4194304 | tf_op jit(solution)/shard_map/all_to_all | solution.py:244
  24.2 7.1 %collective-permute-start.3 = (bf16[128,1024]{1,0:T(8,128)(2,1)S(1)}, bf16[128,1024]{1,0:T(8,128)(2,1)S(1)}, u32[]{:S(2)}, u32[]{:S(2)}) collective-permute-start(bf16[128,1024]{1,0:T(8,128)(2,1)S(1)} %slice.77), channel_id=1, source_target_pairs={{0,3},{1,0},{2,1},{3,2},{4,7},{5,4},{6,5},{7,6},{8,11},{9,8},{10,9... | collective-permute-start | bytes 786440 | tf_op jit(solution)/shard_map/ppermute | solution.py:45
  27.6 7.0 %collective-permute-start.1 = (bf16[128,1024]{1,0:T(8,128)(2,1)S(1)}, bf16[128,1024]{1,0:T(8,128)(2,1)S(1)}, u32[]{:S(2)}, u32[]{:S(2)}) collective-permute-start(bf16[128,1024]{1,0:T(8,128)(2,1)S(1)} %slice.76), channel_id=1, source_target_pairs={{0,1},{1,2},{2,3},{3,0},{4,5},{5,6},{6,7},{7,4},{8,9},{9,10},{10,1... | collective-permute-start | bytes 786440 | tf_op jit(solution)/shard_map/ppermute | solution.py:45
  27.7 14.9 %collective-permute-start.7 = (bf16[128,2048]{1,0:T(8,128)(2,1)}, bf16[128,2048]{1,0:T(8,128)(2,1)S(1)}, u32[]{:S(2)}, u32[]{:S(2)}) collective-permute-start(bf16[128,2048]{1,0:T(8,128)(2,1)} %collective-permute-done.4), channel_id=1, source_target_pairs={{0,3},{1,0},{2,1},{3,2},{4,7},{5,4},{6,5},{7,6},{8,11},{9,8},{10,9... | collective-permute-start | bytes 1572872 | tf_op jit(solution)/shard_map/ppermute | solution.py:45
  30.4 15.7 %collective-permute-start.5 = (bf16[128,2048]{1,0:T(8,128)(2,1)}, bf16[128,2048]{1,0:T(8,128)(2,1)S(1)}, u32[]{:S(2)}, u32[]{:S(2)}) collective-permute-start(bf16[128,2048]{1,0:T(8,128)(2,1)} %collective-permute-done.4), channel_id=1, source_target_pairs={{0,1},{1,2},{2,3},{3,0},{4,5},{5,6},{6,7},{7,4},{8,9},{9,10},{10,1... | collective-permute-start | bytes 1572872 | tf_op jit(solution)/shard_map/ppermute | solution.py:45
  42.7 7.1 %collective-permute-start.8 = (bf16[128,1024]{1,0:T(8,128)(2,1)S(1)}, bf16[128,1024]{1,0:T(8,128)(2,1)S(1)}, u32[]{:S(2)}, u32[]{:S(2)}) collective-permute-start(bf16[128,1024]{1,0:T(8,128)(2,1)S(1)} %slice.79), channel_id=1, source_target_pairs={{0,3},{1,0},{2,1},{3,2},{4,7},{5,4},{6,5},{7,6},{8,11},{9,8},{10,9... | collective-permute-start | bytes 786440 | tf_op jit(solution)/shard_map/ppermute | solution.py:45
  46.1 7.1 %collective-permute-start.6 = (bf16[128,1024]{1,0:T(8,128)(2,1)S(1)}, bf16[128,1024]{1,0:T(8,128)(2,1)S(1)}, u32[]{:S(2)}, u32[]{:S(2)}) collective-permute-start(bf16[128,1024]{1,0:T(8,128)(2,1)S(1)} %slice.78), channel_id=1, source_target_pairs={{0,1},{1,2},{2,3},{3,0},{4,5},{5,6},{6,7},{7,4},{8,9},{9,10},{10,1... | collective-permute-start | bytes 786440 | tf_op jit(solution)/shard_map/ppermute | solution.py:45
  46.6 11.8 %collective-permute-start.9 = (bf16[4,128,2048]{2,1,0:T(8,128)(2,1)S(1)}, bf16[4,128,2048]{2,1,0:T(8,128)(2,1)S(1)}, u32[]{:S(2)}, u32[]{:S(2)}) collective-permute-start(bf16[4,128,2048]{2,1,0:T(8,128)(2,1)S(1)} %pad_maximum_fusion.s0), channel_id=1, source_target_pairs={{0,8},{1,9},{2,10},{3,11},{4,12},{5,13},{6,14},{7,15},{8,0},{9,1},... | collective-permute-start | bytes 6291464 | tf_op jit(solution)/shard_map/ppermute | solution.py:45
  54.5 3.9 %copy-start.3 = (bf16[4,128,2048]{2,1,0:T(8,128)(2,1)}, bf16[4,128,2048]{2,1,0:T(8,128)(2,1)S(1)}, u32[]{:S(2)}) copy-start(bf16[4,128,2048]{2,1,0:T(8,128)(2,1)S(1)} %pad_maximum_fusion.1.s1) | copy-start | bytes 6291460
  54.5 7.8 %collective-permute-start.10 = (bf16[4,128,2048]{2,1,0:T(8,128)(2,1)S(1)}, bf16[4,128,2048]{2,1,0:T(8,128)(2,1)}, u32[]{:S(2)}, u32[]{:S(2)}) collective-permute-start(bf16[4,128,2048]{2,1,0:T(8,128)(2,1)S(1)} %pad_maximum_fusion.1.s1), channel_id=1, source_target_pairs={{0,8},{1,9},{2,10},{3,11},{4,12},{5,13},{6,14},{7,15},{8,0},{9,1},... | collective-permute-start | bytes 6291464 | tf_op jit(solution)/shard_map/ppermute | solution.py:45
  58.4 1.3 %copy-start.4 = (bf16[4,128,2048]{2,1,0:T(8,128)(2,1)}, bf16[4,128,2048]{2,1,0:T(8,128)(2,1)S(1)}, u32[]{:S(2)}) copy-start(bf16[4,128,2048]{2,1,0:T(8,128)(2,1)S(1)} %collective-permute-done.9.s2) | copy-start | bytes 6291460
  85.6 1.0 copy-start.2
  86.6 31.9 %all-to-all-start.1 = ((bf16[32,32,512]{2,1,0:T(8,128)(2,1)}), bf16[32,32,512]{2,1,0:T(8,128)(2,1)S(1)}, u32[]{:S(2)}, u32[]{:S(2)}) async-start(bf16[32,32,512]{2,1,0:T(8,128)(2,1)} %copy-done.2), calls=%async_computation.1 | async-start | bytes 2097152 | tf_op jit(solution)/shard_map/all_to_all | solution.py:263
  108.8 1.0 copy-start
  118.4 1.2 copy-start.1
where the time goes:
time: 128 us; the launch traced here: 125 us
  starting transfers between devices  38.3 us (30%)
  waiting for transfers between devices  37.8 us (30%)
  Pallas kernels  34.7 us (27%)
  local copies, waits for them, and re-layouts  10.4 us (8%)
  other arithmetic  2.76 us (2%)
  between operations  1.33 us (1%)
    ppermute x11, starting transfers between devices, send(): return lax.ppermute(value, BOTH, where)  22.9 us
    ppermute x11, waiting for transfers between devices, send(): return lax.ppermute(value, BOTH, where)  18.5 us
    pallas_call x1, Pallas kernels, row_heads(): pl.pallas_call(row_kernel, out_shape=jax.ShapeDtypeStruct((STRIDE, HALF),...  16.7 us
    pallas_call x1, Pallas kernels, col_heads(): pl.pallas_call(col_kernel, out_shape=jax.ShapeDtypeStruct((rows, cols, HA...  12.6 us
    all_to_all x1, waiting for transfers between devices, shards(): lax.all_to_all(sequence.reshape(32, 32, D), 'seq', split_axis=0, concat_a...  10.6 us
    all_to_all x1, starting transfers between devices, shards(): lax.all_to_all(sequence.reshape(32, 32, D), 'seq', split_axis=0, concat_a...  9.91 us
    all_to_all x1, waiting for transfers between devices, shards(): lax.all_to_all(attended, 'seq', split_axis=0, concat_axis=0, tiled=True)  8.66 us
    all_to_all x1, starting transfers between devices, shards(): lax.all_to_all(attended, 'seq', split_axis=0, concat_axis=0, tiled=True)  5.53 us
  transfers between devices with their start and end apart: 13, of which 8 were waited for; matrix products, arithmetic and copies ran while one was open for 2% of the time, Pallas kernels for 13%

commit v1 on v0

v1 whole, which is shorter than its diff:
```python
import math

import jax
import jax.numpy as jnp
from jax import lax
from jax.experimental import pallas as pl
from jax.experimental.pallas import tpu as pltpu
from jax.sharding import PartitionSpec as P

D = 1024
HEADS = 16
STRIDE = 1024
NALPHA = 1024
HEAD_DIM = D // HEADS
HALF = D // 2
PAIR = 2 * HEAD_DIM
COLS_AT, ROWS_AT, OUT_AT = 0, 768, 1536
SLAB = 2048
F32, BF16 = jnp.float32, jnp.bfloat16
LOG2_SCALE = math.log2(math.e) / math.sqrt(HEAD_DIM)
BOTH = ("seq", "fsdp")


def split_index(i):
    s, f = divmod(i, 8)
    return s // 16, (s // 2) % 8, s % 2, f // 4, f % 4


def pairs(move):
    out = []
    for i in range(256):
        yl, z, c, yh, x = move(*split_index(i))
        out.append((i, ((yl * 8 + z) * 2 + c) * 8 + yh * 4 + x))
    return out


X_UP = pairs(lambda yl, z, c, yh, x: (yl, z, c, yh, (x + 1) % 4))
X_DOWN = pairs(lambda yl, z, c, yh, x: (yl, z, c, yh, (x - 1) % 4))
Y_NEAR = pairs(lambda yl, z, c, yh, x: (1 - yl, z, c, 1 - yh, x))
CORE = pairs(lambda yl, z, c, yh, x: (yl, z, 1 - c, yh, x))


def send(value, where):
    return lax.ppermute(value, BOTH, where)


def normalized(rows):
    mean_square = jnp.mean(rows * rows, axis=-1, keepdims=True)
    return (rows * lax.rsqrt(mean_square + 1e-06)).astype(BF16)


def fetch_weights(slabs, first, width, dest, sems):
    core = lax.axis_index("seq") % 2
    mine = lax.axis_index("fsdp")
    copies = []
    for n, slab in enumerate(slabs):
        half = core if n < 2 else 1 - core
        y_hi = mine // 4 if n % 2 == 0 else 1 - mine // 4
        for k in range(4):
            feature = pl.multiple_of((y_hi * 4 + (mine % 4 - k + 4) % 4) * 128, 128)
            copy = pltpu.make_async_copy(
                slab.at[k, :, pl.ds(first, width)],
                dest.at[half, pl.ds(feature, 128), :],
                sems.at[n * 4 + k],
            )
            copy.start()
            copies.append(copy)
    return copies


def prep_kernel(alpha_ref, qb_ref, qd_ref, ob_ref, od_ref, o_ref):
    core = lax.axis_index("seq") % 2
    step_alpha = (alpha_ref[0].astype(F32) + NALPHA) / (2.0 * NALPHA)
    at = 0
    for kind in (1, 0):
        for which in range(3):
            lanes = pl.ds(pl.multiple_of(which * D + kind * HALF + core * 256, 256), 256)
            rebuilt = qb_ref[:, lanes].astype(F32) + step_alpha * qd_ref[:, lanes].astype(F32)
            o_ref[:, at : at + 256] = rebuilt.astype(BF16)
            at += 256
    lanes = pl.ds(pl.multiple_of(core * 512, 512), 512)
    rebuilt = ob_ref[:, lanes].astype(F32) + step_alpha * od_ref[:, lanes].astype(F32)
    o_ref[:, at:] = rebuilt.astype(BF16)


def soft_average(queries, keys, values_ones, mask):
    scores = lax.dot_general(queries, keys, (((1,), (1,)), ((), ())), preferred_element_type=F32)
    width = mask.shape[1]
    last = scores[:, -width:] + mask
    scores = last if width == scores.shape[1] else jnp.concatenate([scores[:, :-width], last], 1)
    peak = jnp.max(scores, axis=-1, keepdims=True)
    weights = jnp.exp2((scores - peak) * LOG2_SCALE).astype(BF16)
    both = jnp.dot(weights, values_ones, preferred_element_type=F32)
    return both[:, :PAIR] / both[:, PAIR:]


def lanes_of_first(rows):
    return lax.broadcasted_iota(jnp.int32, (rows, PAIR), 1) < HEAD_DIM


def pair_attend(q, k, v, mask):
    first = lanes_of_first(q.shape[0])
    nothing = jnp.zeros_like(q)
    values_ones = jnp.concatenate([v, jnp.ones_like(v)], 1)
    even = soft_average(jnp.where(first, q, nothing), k, values_ones, mask)
    odd = soft_average(jnp.where(first, nothing, q), k, values_ones, mask)
    return jnp.where(first, even, odd).astype(BF16)


def block_attend(q, k, v, mask):
    first = lanes_of_first(q.shape[0])
    nothing, one = jnp.zeros_like(q), jnp.ones_like(q)
    keys = jnp.concatenate([jnp.where(first, k, nothing), jnp.where(first, nothing, k)], 0)
    scores = lax.dot_general(q, keys, (((1,), (1,)), ((), ())), preferred_element_type=F32)
    weights = []
    for head in range(2):
        own = scores[:, head * 128 : (head + 1) * 128] + mask
        peak = jnp.max(own, axis=-1, keepdims=True)
        weights.append(jnp.exp2((own - peak) * LOG2_SCALE).astype(BF16))
    values = jnp.concatenate(
        [
            jnp.concatenate([jnp.where(first, v, nothing), jnp.where(first, one, nothing)], 1),
            jnp.concatenate([jnp.where(first, nothing, v), jnp.where(first, nothing, one)], 1),
        ],
        0,
    )
    both = jnp.dot(jnp.concatenate(weights, 1), values, preferred_element_type=F32)
    return (both[:, :PAIR] / both[:, PAIR:]).astype(BF16)


def row_kernel(x_ref, s0, s1, s2, s3, part_hbm, wc_hbm, w, wo, qkv, attended, mask_ref, part, sems, sems_o, sems_part):
    slabs = (s0, s1, s2, s3)
    copies = fetch_weights(slabs, ROWS_AT, 768, w, sems)
    copies_out = fetch_weights(slabs, OUT_AT, 512, wo, sems_o)
    block = 256
    row = lax.broadcasted_iota(jnp.int32, (block, block), 0)
    col = lax.broadcasted_iota(jnp.int32, (block, block), 1)
    mask_ref[...] = jnp.where(col <= row, 0.0, -jnp.inf)
    for copy in copies:
        copy.wait()

    def project(i, _):
        at = pl.ds(pl.multiple_of(i * block, block), block)
        normed = normalized(x_ref[at, :].astype(F32))
        for half in range(2):
            made = jnp.dot(normed, w[half], preferred_element_type=F32).astype(BF16)
            for which in range(3):
                for p in range(2):
                    lane = which * 256 + p * PAIR
                    qkv[which, half * 2 + p, at, :] = made[:, lane : lane + PAIR]
        return 0

    lax.fori_loop(0, STRIDE // block, project, 0)

    for p in range(4):
        for i in range(STRIDE // block):
            upto = (i + 1) * block
            attended[i * block : upto, p * PAIR : (p + 1) * PAIR] = pair_attend(
                qkv[0, p, i * block : upto, :],
                qkv[1, p, :upto, :],
                qkv[2, p, :upto, :],
                mask_ref[...],
            )
    for copy in copies_out:
        copy.wait()

    copies = [pltpu.make_async_copy(wo.at[:, pl.ds(HALF, HALF), :], wc_hbm, sems.at[0])]
    copies[0].start()
    for i in range(STRIDE // block):
        at = slice(i * block, (i + 1) * block)
        for half in range(2):
            part[at, half * 512 : (half + 1) * 512] = jnp.dot(
                attended[at, :], wo[half, :HALF, :], preferred_element_type=F32
            )
        copies.append(pltpu.make_async_copy(part.at[at, :], part_hbm.at[at, :], sems_part.at[i]))
        copies[-1].start()
    for copy in copies:
        copy.wait()


def sequence_row(place):
    z = place // 4
    z = (z % 2) * 4 + (z // 2 % 2) * 2 + z // 4
    return (place // 2 % 2) * 16 + z * 2 + place % 2


def col_kernel(x_hbm, s0, s1, s2, s3, o_hbm, x, w, out, mask_ref, sort_ref, sems, sems_x, sems_o):
    wide = 16
    steps = x.shape[1] // wide
    arrive, leave = [], []
    for i in range(steps):
        at = pl.ds(i * wide, wide)
        arrive.append(pltpu.make_async_copy(x_hbm.at[:, at, :], x.at[:, at, :], sems_x.at[i]))
        leave.append(pltpu.make_async_copy(out.at[:, at, :], o_hbm.at[:, at, :], sems_o.at[i]))
    arrive[0].start()
    weights = fetch_weights((s0, s1, s2, s3), COLS_AT, 768, w, sems)
    for copy in arrive[1:]:
        copy.start()
    size = 256
    at = lax.broadcasted_iota(jnp.int32, (128, 128), 0)
    to = lax.broadcasted_iota(jnp.int32, (128, 128), 1)
    meets = jnp.logical_and(at // 32 == to // 32, to <= at)
    mask_ref[...] = jnp.where(meets, 0.0, -jnp.inf)
    new = lax.broadcasted_iota(jnp.int32, (size, size), 0)
    old = lax.broadcasted_iota(jnp.int32, (size, size), 1)
    moves = jnp.logical_and(new // 32 == old % 8, new % 32 == sequence_row(old // 8))
    sort_ref[...] = jnp.where(moves, 1.0, 0.0).astype(BF16)

    for i in range(steps):
        arrive[i].wait()
        taken = x[:, i * wide : (i + 1) * wide, :].astype(F32)
        sorted_parts = []
        for part in range(2):
            normed = normalized(taken[:, part * 8 : (part + 1) * 8, :].reshape(size, D))
            sorted_parts.append(
                jnp.dot(sort_ref[...], normed, preferred_element_type=F32).astype(BF16)
            )
        if i == 0:
            for copy in weights:
                copy.wait()
        backs = []
        for normed in sorted_parts:
            done = []
            for half in range(2):
                made = jnp.dot(normed, w[half], preferred_element_type=F32).astype(BF16)
                for p in range(2):
                    q, k, v = (
                        made[:, which * 256 + p * PAIR : which * 256 + (p + 1) * PAIR]
                        for which in range(3)
                    )
                    blocks = [
                        block_attend(q[n : n + 128], k[n : n + 128], v[n : n + 128], mask_ref[...])
                        for n in (0, 128)
                    ]
                    done.append(jnp.concatenate(blocks, 0))
            back = lax.dot_general(
                sort_ref[...],
                jnp.concatenate(done, 1),
                (((0,), (0,)), ((), ())),
                preferred_element_type=F32,
            )
            backs.append(back.reshape(32, 8, HALF))
        out[:, i * wide : (i + 1) * wide, :] = jnp.concatenate(backs, 1).astype(BF16)
        leave[i].start()
    for copy in leave:
        copy.wait()


def out_kernel(part_hbm, col_hbm, w_hbm, o_hbm, part, col, w, out, sem_w, sems_p, sems_c, sems_o):
    block = 256
    weights = pltpu.make_async_copy(w_hbm, w, sem_w.at[0])
    weights.start()
    parts, cols, outs = [], [], []
    for i in range(STRIDE // block):
        at = pl.ds(i * block, block)
        parts.append(pltpu.make_async_copy(part_hbm.at[at, :], part.at[at, :], sems_p.at[i]))
        cols.append(pltpu.make_async_copy(col_hbm.at[at, :], col.at[at, :], sems_c.at[i]))
        outs.append(pltpu.make_async_copy(out.at[at, :], o_hbm.at[at, :], sems_o.at[i]))
        cols[i].start()
        parts[i].start()
    weights.wait()
    for i in range(STRIDE // block):
        at = slice(i * block, (i + 1) * block)
        cols[i].wait()
        parts[i].wait()
        for half in range(2):
            lanes = slice(half * 512, (half + 1) * 512)
            total = part[at, lanes] + jnp.dot(
                col[at, :], w[half], preferred_element_type=F32
            )
            out[at, lanes] = total.astype(BF16)
        outs[i].start()
    for copy in outs:
        copy.wait()


ANY = pl.BlockSpec(memory_space=pl.ANY)
WHOLE = pl.BlockSpec(memory_space=pltpu.VMEM)
FAR = pl.BlockSpec(memory_space=pltpu.HBM)
DMA = pltpu.SemaphoreType.DMA


def limit(mib):
    return pltpu.CompilerParams(vmem_limit_bytes=mib << 20)


def rebuilt_half(alpha_index, *parts):
    return pl.pallas_call(
        prep_kernel,
        out_shape=jax.ShapeDtypeStruct((parts[0].shape[0], SLAB), BF16),
        in_specs=[pl.BlockSpec(memory_space=pltpu.SMEM)] + [WHOLE] * 4,
        out_specs=WHOLE,
        compiler_params=limit(16),
        name="rebuilt_half",
    )(alpha_index, *parts)


def row_heads(sequence, slabs):
    return pl.pallas_call(
        row_kernel,
        out_shape=(
            jax.ShapeDtypeStruct((STRIDE, D), F32),
            jax.ShapeDtypeStruct((2, HALF, 512), BF16),
        ),
        in_specs=[WHOLE] + [ANY] * 4,
        out_specs=(FAR, FAR),
        scratch_shapes=[
            pltpu.VMEM((2, D, 768), BF16),
            pltpu.VMEM((2, D, 512), BF16),
            pltpu.VMEM((3, 4, STRIDE, PAIR), BF16),
            pltpu.VMEM((STRIDE, HALF), BF16),
            pltpu.VMEM((256, 256), F32),
            pltpu.VMEM((STRIDE, D), F32),
            DMA((16,)),
            DMA((16,)),
            DMA((4,)),
        ],
        compiler_params=limit(63),
        cost_estimate=pl.CostEstimate(
            flops=7_000_000_000, bytes_accessed=12 << 20, transcendentals=5_000_000
        ),
        name="row_heads",
    )(sequence, *slabs)


def col_heads(columns, slabs):
    rows, cols = columns.shape[:2]
    return pl.pallas_call(
        col_kernel,
        out_shape=jax.ShapeDtypeStruct((rows, cols, HALF), BF16),
        in_specs=[FAR] + [ANY] * 4,
        out_specs=FAR,
        scratch_shapes=[
            pltpu.VMEM((rows, cols, D), BF16),
            pltpu.VMEM((2, D, 768), BF16),
            pltpu.VMEM((rows, cols, HALF), BF16),
            pltpu.VMEM((128, 128), F32),
            pltpu.VMEM((256, 256), BF16),
            DMA((16,)),
            DMA((cols // 16,)),
            DMA((cols // 16,)),
        ],
        compiler_params=limit(63),
        cost_estimate=pl.CostEstimate(
            flops=4_000_000_000, bytes_accessed=6 << 20, transcendentals=1_000_000
        ),
        name="col_heads",
    )(columns, *slabs)


def project_out(row_part, col_out, weights):
    return pl.pallas_call(
        out_kernel,
        out_shape=jax.ShapeDtypeStruct((STRIDE, D), BF16),
        in_specs=[FAR] * 3,
        out_specs=FAR,
        scratch_shapes=[
            pltpu.VMEM((STRIDE, D), F32),
            pltpu.VMEM((STRIDE, HALF), BF16),
            pltpu.VMEM((2, HALF, 512), BF16),
            pltpu.VMEM((STRIDE, D), BF16),
            DMA((1,)),
            DMA((4,)),
            DMA((4,)),
            DMA((4,)),
        ],
        compiler_params=limit(63),
        cost_estimate=pl.CostEstimate(
            flops=1_000_000_000, bytes_accessed=8 << 20, transcendentals=0
        ),
        name="project_out",
    )(row_part, col_out, weights)


ORDER = [sequence_row(place) for place in range(32)]


def exchange(blocks):
    return lax.all_to_all(
        blocks, "seq", split_axis=0, concat_axis=0, tiled=True, axis_index_groups=[ORDER]
    )


def shards(tokens, qkv_base, qkv_dir, out_base, out_dir, alpha_index):
    sequence = tokens[0]
    columns = exchange(sequence.reshape(32, 32, D))
    own = rebuilt_half(alpha_index, qkv_base, qkv_dir, out_base, out_dir)

    def around(piece):
        below, above = send(piece, X_UP), send(piece, X_DOWN)
        far = jnp.concatenate(
            [send(below[:, : SLAB // 2], X_UP), send(above[:, SLAB // 2 :], X_DOWN)], 1
        )
        return jnp.stack([piece, below, far, above])

    other = send(own, Y_NEAR)
    near_slab = around(own)
    far_slab = around(other)
    slabs = (near_slab, far_slab, send(near_slab, CORE), send(far_slab, CORE))
    attended = col_heads(columns, slabs)
    col_out = exchange(attended)
    row_part, weights = row_heads(sequence, slabs)
    return project_out(row_part, col_out.reshape(STRIDE, HALF), weights)[None]


def solution(mesh):
    in_specs = (
        P("fsdp", "seq", None),
        P("fsdp", None),
        P("fsdp", None),
        P("fsdp", None),
        P("fsdp", None),
        P(),
    )
    out_specs = P("fsdp", "seq", None)
    return jax.shard_map(shards, mesh=mesh, in_specs=in_specs, out_specs=out_specs, check_vma=False)
```

time: 128 us -> 119 us (0.930); the launches traced: 125 us -> 119 us
  local copies, waits for them, and re-layouts: 10.4 us -> 1.46 us
  Pallas kernels: 34.7 us -> 41.4 us
  starting transfers between devices: 38.3 us -> 36.1 us
  other arithmetic: 2.76 us -> 0.6 us
    ppermute x11, waiting for transfers between devices: 18.5 us -> 31.4 us  [send(): return lax.ppermute(value, BOTH, where)]
    all_to_all x2, waiting for transfers between devices: 19.3 us -> 7.09 us  [exchange(): lax.all_to_all(blocks, 'seq', split_axis=0, concat_axis=0, tiled=True, ax...]
    ppermute x11, starting transfers between devices: 22.9 us -> 18 us  [send(): return lax.ppermute(value, BOTH, where)]
    unnamed x42 -> x14, local copies, waits for them, and re-layouts: 5.49 us -> 1.39 us
    pallas_call x1, Pallas kernels: 12.6 us -> 16.2 us  [col_heads(): pl.pallas_call(col_kernel, out_shape=jax.ShapeDtypeStruct((rows, cols, HA...]
    pallas_call x1 -> x2, Pallas kernels: 16.7 us -> 20.1 us  [the longest x1 19.9 us: row_heads(): pl.pallas_call(row_kernel, out_shape=(jax.ShapeDtypeStruct((STRIDE, D), F...]
    reshape x2 -> x0, local copies, waits for them, and re-layouts: 3.14 us -> none  [core_half(): qkv.reshape(-1, 3, 2, 2, 256)]
    all_to_all x2, starting transfers between devices: 15.4 us -> 18.1 us  [exchange(): lax.all_to_all(blocks, 'seq', split_axis=0, concat_axis=0, tiled=True, ax...]
  transfers between devices with their start and end apart: 13 -> 13, of which waited for: 8 -> 7; matrix products, arithmetic and copies ran while one was open for 2% -> 1% of each run, Pallas kernels for 13% -> 17%
where the time goes in v1:
time: 119 us
  Pallas kernels  41.4 us (35%)
  waiting for transfers between devices  38.4 us (32%)
  starting transfers between devices  36.1 us (30%)
  local copies, waits for them, and re-layouts  1.46 us (1%)
    ppermute x11, waiting for transfers between devices, send(): return lax.ppermute(value, BOTH, where)  31.4 us
    pallas_call x1, Pallas kernels, row_heads(): pl.pallas_call(row_kernel, out_shape=(jax.ShapeDtypeStruct((STRIDE, D), F...  19.9 us
    all_to_all x2, starting transfers between devices, exchange(): lax.all_to_all(blocks, 'seq', split_axis=0, concat_axis=0, tiled=True, ax...  18.1 us
    ppermute x11, starting transfers between devices, send(): return lax.ppermute(value, BOTH, where)  18 us
    pallas_call x1, Pallas kernels, col_heads(): pl.pallas_call(col_kernel, out_shape=jax.ShapeDtypeStruct((rows, cols, HA...  16.2 us
    all_to_all x2, waiting for transfers between devices, exchange(): lax.all_to_all(blocks, 'seq', split_axis=0, concat_axis=0, tiled=True, ax...  7.09 us
    pallas_call x1, Pallas kernels, project_out(): pl.pallas_call(out_kernel, out_shape=jax.ShapeDtypeStruct((STRIDE, D), BF...  5.13 us
  transfers between devices with their start and end apart: 13, of which 7 were waited for; matrix products, arithmetic and copies ran while one was open for 1% of the time, Pallas kernels for 17%

profile of v1, /device:TPU:1, one launch (start us, length us, event | category | flops | bytes accessed | tf_op | source)
XLA Modules:
  0.0 119.0 jit_solution(13476529577280833514)
XLA Ops:
  0.0 0.0 copy-start
  0.0 0.0 copy-start.1
  0.0 0.0 copy-start.2
  0.0 0.0 copy-start.3
  0.0 11.3 %all-to-all-start = ((bf16[32,32,1024]{2,1,0:T(8,128)(2,1)}), bf16[32,32,1024]{2,1,0:T(8,128)(2,1)}, u32[]{:S(2)}, u32[]{:S(2)}) async-start(bf16[32,32,1024]{2,1,0:T(8,128)(2,1)} %bitcast.15), calls=%async_computation | async-start | bytes 4194304 | tf_op jit(solution)/shard_map/all_to_all | solution.py:379
  12.0 0.0 copy-done
  12.0 0.0 copy-done.1
  12.0 0.0 copy-done.2
  12.0 0.0 copy-done.3
  12.0 0.2 rebuilt_half.1
  12.2 2.9 %collective-permute-start.4 = (bf16[128,2048]{1,0:T(8,128)(2,1)S(1)}, bf16[128,2048]{1,0:T(8,128)(2,1)S(1)}, u32[]{:S(2)}, u32[]{:S(2)}) collective-permute-start(bf16[128,2048]{1,0:T(8,128)(2,1)S(1)} %rebuilt_half.1), channel_id=1, source_target_pairs={{0,132},{1,133},{2,134},{3,135},{4,128},{5,129},{6,130},{7,131},{8... | collective-permute-start | bytes 1572872 | tf_op jit(solution)/shard_map/ppermute | solution.py:44
  15.1 2.5 %collective-permute-start.2 = (bf16[128,2048]{1,0:T(8,128)(2,1)S(1)}, bf16[128,2048]{1,0:T(8,128)(2,1)S(1)}, u32[]{:S(2)}, u32[]{:S(2)}) collective-permute-start(bf16[128,2048]{1,0:T(8,128)(2,1)S(1)} %rebuilt_half.1), channel_id=1, source_target_pairs={{0,3},{1,0},{2,1},{3,2},{4,7},{5,4},{6,5},{7,6},{8,11},{9,8},{10,9... | collective-permute-start | bytes 1572872 | tf_op jit(solution)/shard_map/ppermute | solution.py:44
  17.6 0.0 collective-permute-start
  17.6 9.5 %collective-permute-done.4 = bf16[128,2048]{1,0:T(8,128)(2,1)S(1)} collective-permute-done((bf16[128,2048]{1,0:T(8,128)(2,1)S(1)}, bf16[128,2048]{1,0:T(8,128)(2,1)S(1)}, u32[]{:S(2)}, u32[]{:S(2)}) %collective-permute-start.4) | collective-permute-done | bytes 524320 | tf_op jit(solution)/shard_map/ppermute | solution.py:44
  27.2 2.5 %collective-permute-start.7 = (bf16[128,2048]{1,0:T(8,128)(2,1)S(1)}, bf16[128,2048]{1,0:T(8,128)(2,1)S(1)}, u32[]{:S(2)}, u32[]{:S(2)}) collective-permute-start(bf16[128,2048]{1,0:T(8,128)(2,1)S(1)} %collective-permute-done.4), channel_id=1, source_target_pairs={{0,3},{1,0},{2,1},{3,2},{4,7},{5,4},{6,5},{7,6},{8,11},{9,8},{10,9... | collective-permute-start | bytes 1572872 | tf_op jit(solution)/shard_map/ppermute | solution.py:44
  29.6 0.0 collective-permute-start.5
  29.6 0.0 collective-permute-done.2
  29.7 2.8 %collective-permute-start.3 = (bf16[128,1024]{1,0:T(8,128)(2,1)S(1)}, bf16[128,1024]{1,0:T(8,128)(2,1)S(1)}, u32[]{:S(2)}, u32[]{:S(2)}) collective-permute-start(bf16[128,1024]{1,0:T(8,128)(2,1)S(1)} %slice.17), channel_id=1, source_target_pairs={{0,3},{1,0},{2,1},{3,2},{4,7},{5,4},{6,5},{7,6},{8,11},{9,8},{10,9... | collective-permute-start | bytes 786440 | tf_op jit(solution)/shard_map/ppermute | solution.py:44
  32.4 0.0 collective-permute-done
  32.5 0.1 collective-permute-start.1
  32.5 13.1 %collective-permute-done.3 = bf16[128,1024]{1,0:T(8,128)(2,1)S(1)} collective-permute-done((bf16[128,1024]{1,0:T(8,128)(2,1)S(1)}, bf16[128,1024]{1,0:T(8,128)(2,1)S(1)}, u32[]{:S(2)}, u32[]{:S(2)}) %collective-permute-start.3) | collective-permute-done | bytes 262176 | tf_op jit(solution)/shard_map/ppermute | solution.py:44
  45.6 3.2 %collective-permute-done.1 = bf16[128,1024]{1,0:T(8,128)(2,1)S(1)} collective-permute-done((bf16[128,1024]{1,0:T(8,128)(2,1)S(1)}, bf16[128,1024]{1,0:T(8,128)(2,1)S(1)}, u32[]{:S(2)}, u32[]{:S(2)}) %collective-permute-start.1) | collective-permute-done | bytes 262176 | tf_op jit(solution)/shard_map/ppermute | solution.py:44
  48.9 0.0 collective-permute-done.7
  48.9 0.3 collective-permute-start.8
  49.2 0.0 collective-permute-done.5
  49.2 1.3 %collective-permute-start.6 = (bf16[128,1024]{1,0:T(8,128)(2,1)S(1)}, bf16[128,1024]{1,0:T(8,128)(2,1)S(1)}, u32[]{:S(2)}, u32[]{:S(2)}) collective-permute-start(bf16[128,1024]{1,0:T(8,128)(2,1)S(1)} %slice.18), channel_id=1, source_target_pairs={{0,1},{1,2},{2,3},{3,0},{4,5},{5,6},{6,7},{7,4},{8,9},{9,10},{10,1... | collective-permute-start | bytes 786440 | tf_op jit(solution)/shard_map/ppermute | solution.py:44
  50.6 0.3 pad_maximum_fusion.s0
  50.8 0.0 copy-start.4
  50.9 2.6 %collective-permute-start.9 = (bf16[4,128,2048]{2,1,0:T(8,128)(2,1)S(1)}, bf16[4,128,2048]{2,1,0:T(8,128)(2,1)S(1)}, u32[]{:S(2)}, u32[]{:S(2)}) collective-permute-start(bf16[4,128,2048]{2,1,0:T(8,128)(2,1)S(1)} %pad_maximum_fusion.s0), channel_id=1, source_target_pairs={{0,8},{1,9},{2,10},{3,11},{4,12},{5,13},{6,14},{7,15},{8,0},{9,1},... | collective-permute-start | bytes 6291464 | tf_op jit(solution)/shard_map/ppermute | solution.py:44
  53.5 1.5 %collective-permute-done.8 = bf16[128,1024]{1,0:T(8,128)(2,1)S(1)} collective-permute-done((bf16[128,1024]{1,0:T(8,128)(2,1)S(1)}, bf16[128,1024]{1,0:T(8,128)(2,1)S(1)}, u32[]{:S(2)}, u32[]{:S(2)}) %collective-permute-start.8) | collective-permute-done | bytes 262176 | tf_op jit(solution)/shard_map/ppermute | solution.py:44
  55.0 1.4 %collective-permute-done.6 = bf16[128,1024]{1,0:T(8,128)(2,1)S(1)} collective-permute-done((bf16[128,1024]{1,0:T(8,128)(2,1)S(1)}, bf16[128,1024]{1,0:T(8,128)(2,1)S(1)}, u32[]{:S(2)}, u32[]{:S(2)}) %collective-permute-start.6) | collective-permute-done | bytes 262176 | tf_op jit(solution)/shard_map/ppermute | solution.py:44
  56.4 0.3 pad_maximum_fusion.1.s1
  56.7 0.0 copy-done.4
  56.7 0.0 copy-start.5
  56.7 3.1 %collective-permute-start.10 = (bf16[4,128,2048]{2,1,0:T(8,128)(2,1)S(1)}, bf16[4,128,2048]{2,1,0:T(8,128)(2,1)}, u32[]{:S(2)}, u32[]{:S(2)}) collective-permute-start(bf16[4,128,2048]{2,1,0:T(8,128)(2,1)S(1)} %pad_maximum_fusion.1.s1), channel_id=1, source_target_pairs={{0,8},{1,9},{2,10},{3,11},{4,12},{5,13},{6,14},{7,15},{8,0},{9,1},... | collective-permute-start | bytes 6291464 | tf_op jit(solution)/shard_map/ppermute | solution.py:44
  59.8 0.0 collective-permute-done.9.s2
  59.9 0.0 copy-done.5
  59.9 0.0 copy-start.6
  59.9 1.4 %copy-done.6 = bf16[4,128,2048]{2,1,0:T(8,128)(2,1)} copy-done((bf16[4,128,2048]{2,1,0:T(8,128)(2,1)}, bf16[4,128,2048]{2,1,0:T(8,128)(2,1)S(1)}, u32[]{:S(2)}) %copy-start.6) | copy-done | bytes 2097176
  61.2 2.5 %collective-permute-done.10.s3 = bf16[4,128,2048]{2,1,0:T(8,128)(2,1)} collective-permute-done((bf16[4,128,2048]{2,1,0:T(8,128)(2,1)S(1)}, bf16[4,128,2048]{2,1,0:T(8,128)(2,1)}, u32[]{:S(2)}, u32[]{:S(2)}) %collective-permute-start.10) | collective-permute-done | bytes 2097184 | tf_op jit(solution)/shard_map/ppermute | solution.py:44
  63.8 0.0 all-to-all-done.x_hbm
  63.8 16.2 %col_heads.1 = bf16[32,32,512]{2,1,0:T(8,128)(2,1)} custom-call(bf16[32,32,1024]{2,1,0:T(8,128)(2,1)} %all-to-all-done.x_hbm, bf16[4,128,2048]{2,1,0:T(8,128)(2,1)} %copy-done.4, bf16[4,128,2048]{2,1,0:T(8,128)(2,1)} %copy-done.5, bf16[4,128,2048]{2,1,0:T(8,128)(2,1)} %copy-done.6, bf16[4,128,2048]{2,1,0:T(8,128)(2,1)} %collective-permute-done.10.s3), custom_call_target="tpu_custom_call" | custom-call | flops 4000000000 | bytes 6291456 | tf_op jit(solution)/shard_map/col_heads/pallas_call | solution.py:328
  79.9 6.7 %all-to-all-start.1 = ((bf16[32,32,512]{2,1,0:T(8,128)(2,1)}), bf16[32,32,512]{2,1,0:T(8,128)(2,1)}, u32[]{:S(2)}, u32[]{:S(2)}) async-start(bf16[32,32,512]{2,1,0:T(8,128)(2,1)} %col_heads.1), calls=%async_computation.1 | async-start | bytes 2097152 | tf_op jit(solution)/shard_map/all_to_all | solution.py:379
  86.7 19.9 %row_heads.1 = (f32[1024,1024]{1,0:T(8,128)}, bf16[2,512,512]{2,1,0:T(8,128)(2,1)}) custom-call(bf16[1024,1024]{1,0:T(8,128)(2,1)} %bitcast.16, bf16[4,128,2048]{2,1,0:T(8,128)(2,1)} %copy-done.4, bf16[4,128,2048]{2,1,0:T(8,128)(2,1)} %copy-done.5, bf16[4,128,2048]{2,1,0:T(8,128)(2,1)} %copy-done.6, bf16[4,128,2048]{2,1,0:T(8,128)(2,1)} %collective-permute-done.10.s3), custom_call_target="tpu_custom_call" | custom-call | flops 7000000000 | bytes 12582912 | tf_op jit(solution)/shard_map/row_heads/pallas_call | solution.py:299
  106.6 7.1 %all-to-all-done.1 = bf16[32,32,512]{2,1,0:T(8,128)(2,1)} async-done(((bf16[32,32,512]{2,1,0:T(8,128)(2,1)}), bf16[32,32,512]{2,1,0:T(8,128)(2,1)}, u32[]{:S(2)}, u32[]{:S(2)}) %all-to-all-start.1) | async-done | bytes 1048608 | tf_op jit(solution)/shard_map/all_to_all | solution.py:379
  113.7 5.1 %project_out.1 = bf16[1024,1024]{1,0:T(8,128)(2,1)} custom-call(f32[1024,1024]{1,0:T(8,128)} %get-tuple-element.7.part_hbm, bf16[1024,512]{1,0:T(8,128)(2,1)} %bitcast.10.col_hbm, bf16[2,512,512]{2,1,0:T(8,128)(2,1)} %get-tuple-element.8.w_hbm), custom_call_target="tpu_custom_call" | custom-call | flops 1000000000 | bytes 8388608 | tf_op jit(solution)/shard_map/project_out/pallas_call | solution.py:352
  (6 shorter events, 0.1 us)
Async XLA Ops:
  0.0 12.0 %copy-start = (bf16[128,3072]{1,0:T(8,128)(2,1)S(1)}, bf16[128,3072]{1,0:T(8,128)(2,1)}, u32[]{:S(2)}) copy-start(bf16[128,3072]{1,0:T(8,128)(2,1)} %qb_ref.1) | copy-start | bytes 2359300
  0.0 12.0 %copy-start.1 = (bf16[128,3072]{1,0:T(8,128)(2,1)S(1)}, bf16[128,3072]{1,0:T(8,128)(2,1)}, u32[]{:S(2)}) copy-start(bf16[128,3072]{1,0:T(8,128)(2,1)} %qd_ref.1) | copy-start | bytes 2359300
  0.0 12.0 %copy-start.2 = (bf16[128,1024]{1,0:T(8,128)(2,1)S(1)}, bf16[128,1024]{1,0:T(8,128)(2,1)}, u32[]{:S(2)}) copy-start(bf16[128,1024]{1,0:T(8,128)(2,1)} %ob_ref.1) | copy-start | bytes 786436
  0.0 12.0 %copy-start.3 = (bf16[128,1024]{1,0:T(8,128)(2,1)S(1)}, bf16[128,1024]{1,0:T(8,128)(2,1)}, u32[]{:S(2)}) copy-start(bf16[128,1024]{1,0:T(8,128)(2,1)} %od_ref.1) | copy-start | bytes 786436
  0.0 63.7 %all-to-all-start = ((bf16[32,32,1024]{2,1,0:T(8,128)(2,1)}), bf16[32,32,1024]{2,1,0:T(8,128)(2,1)}, u32[]{:S(2)}, u32[]{:S(2)}) async-start(bf16[32,32,1024]{2,1,0:T(8,128)(2,1)} %bitcast.15), calls=%async_computation | async-start | bytes 4194304 | tf_op jit(solution)/shard_map/all_to_all | solution.py:379
  12.2 14.9 %collective-permute-start.4 = (bf16[128,2048]{1,0:T(8,128)(2,1)S(1)}, bf16[128,2048]{1,0:T(8,128)(2,1)S(1)}, u32[]{:S(2)}, u32[]{:S(2)}) collective-permute-start(bf16[128,2048]{1,0:T(8,128)(2,1)S(1)} %rebuilt_half.1), channel_id=1, source_target_pairs={{0,132},{1,133},{2,134},{3,135},{4,128},{5,129},{6,130},{7,131},{8... | collective-permute-start | bytes 1572872 | tf_op jit(solution)/shard_map/ppermute | solution.py:44
  15.1 14.5 %collective-permute-start.2 = (bf16[128,2048]{1,0:T(8,128)(2,1)S(1)}, bf16[128,2048]{1,0:T(8,128)(2,1)S(1)}, u32[]{:S(2)}, u32[]{:S(2)}) collective-permute-start(bf16[128,2048]{1,0:T(8,128)(2,1)S(1)} %rebuilt_half.1), channel_id=1, source_target_pairs={{0,3},{1,0},{2,1},{3,2},{4,7},{5,4},{6,5},{7,6},{8,11},{9,8},{10,9... | collective-permute-start | bytes 1572872 | tf_op jit(solution)/shard_map/ppermute | solution.py:44
  17.6 14.8 %collective-permute-start = (bf16[128,2048]{1,0:T(8,128)(2,1)S(1)}, bf16[128,2048]{1,0:T(8,128)(2,1)S(1)}, u32[]{:S(2)}, u32[]{:S(2)}) collective-permute-start(bf16[128,2048]{1,0:T(8,128)(2,1)S(1)} %rebuilt_half.1), channel_id=1, source_target_pairs={{0,1},{1,2},{2,3},{3,0},{4,5},{5,6},{6,7},{7,4},{8,9},{9,10},{10,1... | collective-permute-start | bytes 1572872 | tf_op jit(solution)/shard_map/ppermute | solution.py:44
  27.2 21.7 %collective-permute-start.7 = (bf16[128,2048]{1,0:T(8,128)(2,1)S(1)}, bf16[128,2048]{1,0:T(8,128)(2,1)S(1)}, u32[]{:S(2)}, u32[]{:S(2)}) collective-permute-start(bf16[128,2048]{1,0:T(8,128)(2,1)S(1)} %collective-permute-done.4), channel_id=1, source_target_pairs={{0,3},{1,0},{2,1},{3,2},{4,7},{5,4},{6,5},{7,6},{8,11},{9,8},{10,9... | collective-permute-start | bytes 1572872 | tf_op jit(solution)/shard_map/ppermute | solution.py:44
  29.6 19.6 %collective-permute-start.5 = (bf16[128,2048]{1,0:T(8,128)(2,1)S(1)}, bf16[128,2048]{1,0:T(8,128)(2,1)S(1)}, u32[]{:S(2)}, u32[]{:S(2)}) collective-permute-start(bf16[128,2048]{1,0:T(8,128)(2,1)S(1)} %collective-permute-done.4), channel_id=1, source_target_pairs={{0,1},{1,2},{2,3},{3,0},{4,5},{5,6},{6,7},{7,4},{8,9},{9,10},{10,1... | collective-permute-start | bytes 1572872 | tf_op jit(solution)/shard_map/ppermute | solution.py:44
  29.7 16.0 %collective-permute-start.3 = (bf16[128,1024]{1,0:T(8,128)(2,1)S(1)}, bf16[128,1024]{1,0:T(8,128)(2,1)S(1)}, u32[]{:S(2)}, u32[]{:S(2)}) collective-permute-start(bf16[128,1024]{1,0:T(8,128)(2,1)S(1)} %slice.17), channel_id=1, source_target_pairs={{0,3},{1,0},{2,1},{3,2},{4,7},{5,4},{6,5},{7,6},{8,11},{9,8},{10,9... | collective-permute-start | bytes 786440 | tf_op jit(solution)/shard_map/ppermute | solution.py:44
  32.5 16.4 %collective-permute-start.1 = (bf16[128,1024]{1,0:T(8,128)(2,1)S(1)}, bf16[128,1024]{1,0:T(8,128)(2,1)S(1)}, u32[]{:S(2)}, u32[]{:S(2)}) collective-permute-start(bf16[128,1024]{1,0:T(8,128)(2,1)S(1)} %slice.16), channel_id=1, source_target_pairs={{0,1},{1,2},{2,3},{3,0},{4,5},{5,6},{6,7},{7,4},{8,9},{9,10},{10,1... | collective-permute-start | bytes 786440 | tf_op jit(solution)/shard_map/ppermute | solution.py:44
  48.9 6.0 %collective-permute-start.8 = (bf16[128,1024]{1,0:T(8,128)(2,1)S(1)}, bf16[128,1024]{1,0:T(8,128)(2,1)S(1)}, u32[]{:S(2)}, u32[]{:S(2)}) collective-permute-start(bf16[128,1024]{1,0:T(8,128)(2,1)S(1)} %slice.19), channel_id=1, source_target_pairs={{0,3},{1,0},{2,1},{3,2},{4,7},{5,4},{6,5},{7,6},{8,11},{9,8},{10,9... | collective-permute-start | bytes 786440 | tf_op jit(solution)/shard_map/ppermute | solution.py:44
  49.2 7.2 %collective-permute-start.6 = (bf16[128,1024]{1,0:T(8,128)(2,1)S(1)}, bf16[128,1024]{1,0:T(8,128)(2,1)S(1)}, u32[]{:S(2)}, u32[]{:S(2)}) collective-permute-start(bf16[128,1024]{1,0:T(8,128)(2,1)S(1)} %slice.18), channel_id=1, source_target_pairs={{0,1},{1,2},{2,3},{3,0},{4,5},{5,6},{6,7},{7,4},{8,9},{9,10},{10,1... | collective-permute-start | bytes 786440 | tf_op jit(solution)/shard_map/ppermute | solution.py:44
  50.8 5.9 %copy-start.4 = (bf16[4,128,2048]{2,1,0:T(8,128)(2,1)}, bf16[4,128,2048]{2,1,0:T(8,128)(2,1)S(1)}, u32[]{:S(2)}) copy-start(bf16[4,128,2048]{2,1,0:T(8,128)(2,1)S(1)} %pad_maximum_fusion.s0) | copy-start | bytes 6291460
  50.9 9.0 %collective-permute-start.9 = (bf16[4,128,2048]{2,1,0:T(8,128)(2,1)S(1)}, bf16[4,128,2048]{2,1,0:T(8,128)(2,1)S(1)}, u32[]{:S(2)}, u32[]{:S(2)}) collective-permute-start(bf16[4,128,2048]{2,1,0:T(8,128)(2,1)S(1)} %pad_maximum_fusion.s0), channel_id=1, source_target_pairs={{0,8},{1,9},{2,10},{3,11},{4,12},{5,13},{6,14},{7,15},{8,0},{9,1},... | collective-permute-start | bytes 6291464 | tf_op jit(solution)/shard_map/ppermute | solution.py:44
  56.7 3.1 %copy-start.5 = (bf16[4,128,2048]{2,1,0:T(8,128)(2,1)}, bf16[4,128,2048]{2,1,0:T(8,128)(2,1)S(1)}, u32[]{:S(2)}) copy-start(bf16[4,128,2048]{2,1,0:T(8,128)(2,1)S(1)} %pad_maximum_fusion.1.s1) | copy-start | bytes 6291460
  56.7 7.0 %collective-permute-start.10 = (bf16[4,128,2048]{2,1,0:T(8,128)(2,1)S(1)}, bf16[4,128,2048]{2,1,0:T(8,128)(2,1)}, u32[]{:S(2)}, u32[]{:S(2)}) collective-permute-start(bf16[4,128,2048]{2,1,0:T(8,128)(2,1)S(1)} %pad_maximum_fusion.1.s1), channel_id=1, source_target_pairs={{0,8},{1,9},{2,10},{3,11},{4,12},{5,13},{6,14},{7,15},{8,0},{9,1},... | collective-permute-start | bytes 6291464 | tf_op jit(solution)/shard_map/ppermute | solution.py:44
  59.9 1.4 %copy-start.6 = (bf16[4,128,2048]{2,1,0:T(8,128)(2,1)}, bf16[4,128,2048]{2,1,0:T(8,128)(2,1)S(1)}, u32[]{:S(2)}) copy-start(bf16[4,128,2048]{2,1,0:T(8,128)(2,1)S(1)} %collective-permute-done.9.s2) | copy-start | bytes 6291460
  79.9 33.7 %all-to-all-start.1 = ((bf16[32,32,512]{2,1,0:T(8,128)(2,1)}), bf16[32,32,512]{2,1,0:T(8,128)(2,1)}, u32[]{:S(2)}, u32[]{:S(2)}) async-start(bf16[32,32,512]{2,1,0:T(8,128)(2,1)} %col_heads.1), calls=%async_computation.1 | async-start | bytes 2097152 | tf_op jit(solution)/shard_map/all_to_all | solution.py:379

commit v2 on v1

--- a/solution.py
+++ b/solution.py
@@ -14,8 +14,7 @@
 HEAD_DIM = D // HEADS
 HALF = D // 2
 PAIR = 2 * HEAD_DIM
-COLS_AT, ROWS_AT, OUT_AT = 0, 768, 1536
-SLAB = 2048
+COLS, REST = 768, 1280
 F32, BF16 = jnp.float32, jnp.bfloat16
 LOG2_SCALE = math.log2(math.e) / math.sqrt(HEAD_DIM)
 BOTH = ("seq", "fsdp")
@@ -34,9 +33,13 @@
     return out
 
 
-X_UP = pairs(lambda yl, z, c, yh, x: (yl, z, c, yh, (x + 1) % 4))
-X_DOWN = pairs(lambda yl, z, c, yh, x: (yl, z, c, yh, (x - 1) % 4))
-Y_NEAR = pairs(lambda yl, z, c, yh, x: (1 - yl, z, c, 1 - yh, x))
+def hop(other_y, dx):
+    return pairs(
+        lambda yl, z, c, yh, x: (yl ^ other_y, z, c, yh ^ other_y, (x + dx) % 4)
+    )
+
+
+HOPS = [hop(other_y, dx) for other_y in range(2) for dx in range(4)]
 CORE = pairs(lambda yl, z, c, yh, x: (yl, z, 1 - c, yh, x))
 
 
@@ -54,33 +57,31 @@
     mine = lax.axis_index("fsdp")
     copies = []
     for n, slab in enumerate(slabs):
-        half = core if n < 2 else 1 - core
-        y_hi = mine // 4 if n % 2 == 0 else 1 - mine // 4
-        for k in range(4):
-            feature = pl.multiple_of((y_hi * 4 + (mine % 4 - k + 4) % 4) * 128, 128)
+        half = core if n == 0 else 1 - core
+        for k in range(8):
+            y_hi = mine // 4 if k % 2 == 0 else 1 - mine // 4
+            feature = pl.multiple_of((y_hi * 4 + (mine % 4 - k // 2 + 4) % 4) * 128, 128)
             copy = pltpu.make_async_copy(
                 slab.at[k, :, pl.ds(first, width)],
                 dest.at[half, pl.ds(feature, 128), :],
-                sems.at[n * 4 + k],
+                sems.at[n * 8 + k],
             )
             copy.start()
             copies.append(copy)
     return copies
 
 
-def prep_kernel(alpha_ref, qb_ref, qd_ref, ob_ref, od_ref, o_ref):
+def prep_kernel(alpha_ref, qb_ref, qd_ref, ob_ref, od_ref, cols_ref, rest_ref):
     core = lax.axis_index("seq") % 2
     step_alpha = (alpha_ref[0].astype(F32) + NALPHA) / (2.0 * NALPHA)
-    at = 0
-    for kind in (1, 0):
+    for kind, to_ref in ((1, cols_ref), (0, rest_ref)):
         for which in range(3):
             lanes = pl.ds(pl.multiple_of(which * D + kind * HALF + core * 256, 256), 256)
             rebuilt = qb_ref[:, lanes].astype(F32) + step_alpha * qd_ref[:, lanes].astype(F32)
-            o_ref[:, at : at + 256] = rebuilt.astype(BF16)
-            at += 256
+            to_ref[:, which * 256 : (which + 1) * 256] = rebuilt.astype(BF16)
     lanes = pl.ds(pl.multiple_of(core * 512, 512), 512)
     rebuilt = ob_ref[:, lanes].astype(F32) + step_alpha * od_ref[:, lanes].astype(F32)
-    o_ref[:, at:] = rebuilt.astype(BF16)
+    rest_ref[:, 768:] = rebuilt.astype(BF16)
 
 
 def soft_average(queries, keys, values_ones, mask):
@@ -107,16 +108,25 @@
     return jnp.where(first, even, odd).astype(BF16)
 
 
-def block_attend(q, k, v, mask):
+def block_scores(q, k):
     first = lanes_of_first(q.shape[0])
-    nothing, one = jnp.zeros_like(q), jnp.ones_like(q)
+    nothing = jnp.zeros_like(q)
     keys = jnp.concatenate([jnp.where(first, k, nothing), jnp.where(first, nothing, k)], 0)
-    scores = lax.dot_general(q, keys, (((1,), (1,)), ((), ())), preferred_element_type=F32)
+    return lax.dot_general(q, keys, (((1,), (1,)), ((), ())), preferred_element_type=F32)
+
+
+def block_weights(scores, mask):
     weights = []
     for head in range(2):
         own = scores[:, head * 128 : (head + 1) * 128] + mask
         peak = jnp.max(own, axis=-1, keepdims=True)
         weights.append(jnp.exp2((own - peak) * LOG2_SCALE).astype(BF16))
+    return jnp.concatenate(weights, 1)
+
+
+def block_average(weights, v):
+    first = lanes_of_first(v.shape[0])
+    nothing, one = jnp.zeros_like(v), jnp.ones_like(v)
     values = jnp.concatenate(
         [
             jnp.concatenate([jnp.where(first, v, nothing), jnp.where(first, one, nothing)], 1),
@@ -124,14 +134,14 @@
         ],
         0,
     )
-    both = jnp.dot(jnp.concatenate(weights, 1), values, preferred_element_type=F32)
+    both = jnp.dot(weights, values, preferred_element_type=F32)
     return (both[:, :PAIR] / both[:, PAIR:]).astype(BF16)
 
 
-def row_kernel(x_ref, s0, s1, s2, s3, part_hbm, wc_hbm, w, wo, qkv, attended, mask_ref, part, sems, sems_o, sems_part):
-    slabs = (s0, s1, s2, s3)
-    copies = fetch_weights(slabs, ROWS_AT, 768, w, sems)
-    copies_out = fetch_weights(slabs, OUT_AT, 512, wo, sems_o)
+def row_kernel(x_ref, s0, s1, part_hbm, wc_hbm, w, wo, qkv, attended, mask_ref, part, sems, sems_o, sems_part):
+    slabs = (s0, s1)
+    copies = fetch_weights(slabs, 0, 768, w, sems)
+    copies_out = fetch_weights(slabs, 768, 512, wo, sems_o)
     block = 256
     row = lax.broadcasted_iota(jnp.int32, (block, block), 0)
     col = lax.broadcasted_iota(jnp.int32, (block, block), 1)
@@ -179,68 +189,82 @@
 
 
 def sequence_row(place):
-    z = place // 4
-    z = (z % 2) * 4 + (z // 2 % 2) * 2 + z // 4
-    return (place // 2 % 2) * 16 + z * 2 + place % 2
-
-
-def col_kernel(x_hbm, s0, s1, s2, s3, o_hbm, x, w, out, mask_ref, sort_ref, sems, sems_x, sems_o):
-    wide = 16
-    steps = x.shape[1] // wide
+    z = ((place >> 2) & 1) * 4 + ((place >> 3) & 1) * 2 + (place >> 4)
+    return ((place >> 1) & 1) * 16 + z * 2 + (place & 1)
+
+
+def place_of(row):
+    z = ((row >> 1) & 1) * 4 + ((row >> 2) & 1) * 2 + ((row >> 3) & 1)
+    return z * 4 + (row >> 4) * 2 + (row & 1)
+
+
+WIDE = 16
+STEP = 32 * WIDE
+
+
+def one_hot(ref, lane_of):
+    wanted = lane_of(lax.broadcasted_iota(jnp.int32, (STEP, 128), 0))
+    lane = lax.broadcasted_iota(jnp.int32, (STEP, 128), 1)
+    for at in range(0, STEP, 128):
+        ref[:, at : at + 128] = jnp.where(wanted == lane + at, 1.0, 0.0).astype(BF16)
+
+
+def col_kernel(
+    x_hbm, s0, s1, o_hbm, x, w, out, mask_ref, sort_ref, back_ref, normed_ref, sems, sems_x, sems_o
+):
+    steps = x.shape[1] // WIDE
     arrive, leave = [], []
     for i in range(steps):
-        at = pl.ds(i * wide, wide)
+        at = pl.ds(i * WIDE, WIDE)
         arrive.append(pltpu.make_async_copy(x_hbm.at[:, at, :], x.at[:, at, :], sems_x.at[i]))
         leave.append(pltpu.make_async_copy(out.at[:, at, :], o_hbm.at[:, at, :], sems_o.at[i]))
-    arrive[0].start()
-    weights = fetch_weights((s0, s1, s2, s3), COLS_AT, 768, w, sems)
-    for copy in arrive[1:]:
-        copy.start()
-    size = 256
+        arrive[i].start()
+    weights = fetch_weights((s0, s1), 0, 768, w, sems)
     at = lax.broadcasted_iota(jnp.int32, (128, 128), 0)
     to = lax.broadcasted_iota(jnp.int32, (128, 128), 1)
     meets = jnp.logical_and(at // 32 == to // 32, to <= at)
     mask_ref[...] = jnp.where(meets, 0.0, -jnp.inf)
-    new = lax.broadcasted_iota(jnp.int32, (size, size), 0)
-    old = lax.broadcasted_iota(jnp.int32, (size, size), 1)
-    moves = jnp.logical_and(new // 32 == old % 8, new % 32 == sequence_row(old // 8))
-    sort_ref[...] = jnp.where(moves, 1.0, 0.0).astype(BF16)
-
+    one_hot(sort_ref, lambda new: place_of(new & 31) * WIDE + (new >> 5))
+    one_hot(back_ref, lambda old: (old & (WIDE - 1)) * 32 + sequence_row(old >> 4))
     for i in range(steps):
         arrive[i].wait()
-        taken = x[:, i * wide : (i + 1) * wide, :].astype(F32)
-        sorted_parts = []
-        for part in range(2):
-            normed = normalized(taken[:, part * 8 : (part + 1) * 8, :].reshape(size, D))
-            sorted_parts.append(
-                jnp.dot(sort_ref[...], normed, preferred_element_type=F32).astype(BF16)
-            )
-        if i == 0:
-            for copy in weights:
-                copy.wait()
-        backs = []
-        for normed in sorted_parts:
-            done = []
-            for half in range(2):
-                made = jnp.dot(normed, w[half], preferred_element_type=F32).astype(BF16)
+        taken = x[:, i * WIDE : (i + 1) * WIDE, :].reshape(STEP, D)
+        for half in range(2):
+            rows = slice(half * 256, half * 256 + 256)
+            ordered = jnp.dot(sort_ref[rows, :], taken, preferred_element_type=F32)
+            normed_ref[i * STEP + half * 256 : i * STEP + half * 256 + 256, :] = normalized(ordered)
+    for copy in weights:
+        copy.wait()
+    for i in range(steps):
+        attended = []
+        for group in range(STEP // 256):
+            start = i * STEP + group * 256
+            parts = [
+                jnp.dot(
+                    normed_ref[start : start + 256, :], w[half], preferred_element_type=F32
+                ).astype(BF16)
+                for half in range(2)
+            ]
+            blocks = []
+            for made in parts:
                 for p in range(2):
-                    q, k, v = (
-                        made[:, which * 256 + p * PAIR : which * 256 + (p + 1) * PAIR]
-                        for which in range(3)
-                    )
-                    blocks = [
-                        block_attend(q[n : n + 128], k[n : n + 128], v[n : n + 128], mask_ref[...])
-                        for n in (0, 128)
-                    ]
-                    done.append(jnp.concatenate(blocks, 0))
-            back = lax.dot_general(
-                sort_ref[...],
-                jnp.concatenate(done, 1),
-                (((0,), (0,)), ((), ())),
-                preferred_element_type=F32,
-            )
-            backs.append(back.reshape(32, 8, HALF))
-        out[:, i * wide : (i + 1) * wide, :] = jnp.concatenate(backs, 1).astype(BF16)
+                    for n in (0, 128):
+                        blocks.append(
+                            [
+                                made[n : n + 128, which * 256 + p * PAIR : which * 256 + (p + 1) * PAIR]
+                                for which in range(3)
+                            ]
+                        )
+            scores = [block_scores(q, k) for q, k, _ in blocks]
+            shares = [block_weights(score, mask_ref[...]) for score in scores]
+            done = [block_average(share, v) for share, (_, _, v) in zip(shares, blocks)]
+            attended.append(jnp.concatenate(
+                [jnp.concatenate(done[n::2], 1) for n in range(2)], 0
+            ))
+        back = jnp.dot(
+            back_ref[...], jnp.concatenate(attended, 0), preferred_element_type=F32
+        ).astype(BF16)
+        out[:, i * WIDE : (i + 1) * WIDE, :] = back.reshape(32, WIDE, HALF)
         leave[i].start()
     for copy in leave:
         copy.wait()
@@ -287,9 +311,11 @@
 def rebuilt_half(alpha_index, *parts):
     return pl.pallas_call(
         prep_kernel,
-        out_shape=jax.ShapeDtypeStruct((parts[0].shape[0], SLAB), BF16),
+        out_shape=[
+            jax.ShapeDtypeStruct((parts[0].shape[0], width), BF16) for width in (COLS, REST)
+        ],
         in_specs=[pl.BlockSpec(memory_space=pltpu.SMEM)] + [WHOLE] * 4,
-        out_specs=WHOLE,
+        out_specs=[WHOLE] * 2,
         compiler_params=limit(16),
         name="rebuilt_half",
     )(alpha_index, *parts)
@@ -302,7 +328,7 @@
             jax.ShapeDtypeStruct((STRIDE, D), F32),
             jax.ShapeDtypeStruct((2, HALF, 512), BF16),
         ),
-        in_specs=[WHOLE] + [ANY] * 4,
+        in_specs=[WHOLE] + [ANY] * 2,
         out_specs=(FAR, FAR),
         scratch_shapes=[
             pltpu.VMEM((2, D, 768), BF16),
@@ -328,17 +354,19 @@
     return pl.pallas_call(
         col_kernel,
         out_shape=jax.ShapeDtypeStruct((rows, cols, HALF), BF16),
-        in_specs=[FAR] + [ANY] * 4,
+        in_specs=[FAR] + [ANY] * 2,
         out_specs=FAR,
         scratch_shapes=[
             pltpu.VMEM((rows, cols, D), BF16),
             pltpu.VMEM((2, D, 768), BF16),
             pltpu.VMEM((rows, cols, HALF), BF16),
             pltpu.VMEM((128, 128), F32),
-            pltpu.VMEM((256, 256), BF16),
+            pltpu.VMEM((STEP, STEP), BF16),
+            pltpu.VMEM((STEP, STEP), BF16),
+            pltpu.VMEM((rows * cols, D), BF16),
             DMA((16,)),
-            DMA((cols // 16,)),
-            DMA((cols // 16,)),
+            DMA((cols // WIDE,)),
+            DMA((cols // WIDE,)),
         ],
         compiler_params=limit(63),
         cost_estimate=pl.CostEstimate(
@@ -381,25 +409,21 @@
     )
 
 
+def gathered(own):
+    both = jnp.stack([own, send(own, HOPS[4])])
+    slab = jnp.concatenate([both] + [send(both, where) for where in HOPS[1:4]])
+    return slab, send(slab, CORE)
+
+
 def shards(tokens, qkv_base, qkv_dir, out_base, out_dir, alpha_index):
     sequence = tokens[0]
     columns = exchange(sequence.reshape(32, 32, D))
-    own = rebuilt_half(alpha_index, qkv_base, qkv_dir, out_base, out_dir)
-
-    def around(piece):
-        below, above = send(piece, X_UP), send(piece, X_DOWN)
-        far = jnp.concatenate(
-            [send(below[:, : SLAB // 2], X_UP), send(above[:, SLAB // 2 :], X_DOWN)], 1
-        )
-        return jnp.stack([piece, below, far, above])
-
-    other = send(own, Y_NEAR)
-    near_slab = around(own)
-    far_slab = around(other)
-    slabs = (near_slab, far_slab, send(near_slab, CORE), send(far_slab, CORE))
-    attended = col_heads(columns, slabs)
+    own_cols, own_rest = rebuilt_half(alpha_index, qkv_base, qkv_dir, out_base, out_dir)
+    col_slabs = gathered(own_cols)
+    rest_slabs = gathered(own_rest)
+    attended = col_heads(columns, col_slabs)
     col_out = exchange(attended)
-    row_part, weights = row_heads(sequence, slabs)
+    row_part, weights = row_heads(sequence, rest_slabs)
     return project_out(row_part, col_out.reshape(STRIDE, HALF), weights)[None]
 
 

time: 119 us -> 125 us (1.050)
  waiting for transfers between devices: 38.4 us -> 45.4 us
  Pallas kernels: 41.4 us -> 35.9 us
  local copies, waits for them, and re-layouts: 1.46 us -> 4.39 us
  starting transfers between devices: 36.1 us -> 38.2 us
    ppermute x11 -> x10, waiting for transfers between devices: 31.4 us -> 38.3 us  [send(): return lax.ppermute(value, BOTH, where)]
    pallas_call x1, Pallas kernels: 16.2 us -> 10.7 us  [col_heads(): pl.pallas_call(col_kernel, out_shape=jax.ShapeDtypeStruct((rows, cols, HA...]
    unnamed x14 -> x18, local copies, waits for them, and re-layouts: 1.39 us -> 3.45 us
    ppermute x11 -> x10, starting transfers between devices: 18 us -> 20 us  [send(): return lax.ppermute(value, BOTH, where)]
  transfers between devices with their start and end apart: 13 -> 12, of which waited for: 7 -> 5; matrix products, arithmetic and copies ran while one was open for 1% -> 4% of each run, Pallas kernels for 17% -> 25%
where the time goes in v2:
time: 125 us
  waiting for transfers between devices  45.4 us (36%)
  starting transfers between devices  38.2 us (31%)
  Pallas kernels  35.9 us (29%)
  local copies, waits for them, and re-layouts  4.39 us (4%)
    ppermute x10, waiting for transfers between devices, send(): return lax.ppermute(value, BOTH, where)  38.3 us
    ppermute x10, starting transfers between devices, send(): return lax.ppermute(value, BOTH, where)  20 us
    pallas_call x1, Pallas kernels, row_heads(): pl.pallas_call(row_kernel, out_shape=(jax.ShapeDtypeStruct((STRIDE, D), F...  19.9 us
    all_to_all x2, starting transfers between devices, exchange(): lax.all_to_all(blocks, 'seq', split_axis=0, concat_axis=0, tiled=True, ax...  18.1 us
    pallas_call x1, Pallas kernels, col_heads(): pl.pallas_call(col_kernel, out_shape=jax.ShapeDtypeStruct((rows, cols, HA...  10.7 us
    all_to_all x2, waiting for transfers between devices, exchange(): lax.all_to_all(blocks, 'seq', split_axis=0, concat_axis=0, tiled=True, ax...  7.09 us
    pallas_call x1, Pallas kernels, project_out(): pl.pallas_call(out_kernel, out_shape=jax.ShapeDtypeStruct((STRIDE, D), BF...  5.09 us
    unnamed x18, local copies, waits for them, and re-layouts  3.45 us
  transfers between devices with their start and end apart: 12, of which 5 were waited for; matrix products, arithmetic and copies ran while one was open for 4% of the time, Pallas kernels for 25%

profile of v2, /device:TPU:1, one launch (start us, length us, event | category | flops | bytes accessed | tf_op | source)
XLA Modules:
  0.0 124.9 jit_solution(13387263577643900555)
XLA Ops:
  0.0 0.0 copy-start
  0.0 0.0 copy-start.1
  0.0 0.0 copy-start.2
  0.0 0.0 copy-start.3
  0.0 11.3 %all-to-all-start = ((bf16[32,32,1024]{2,1,0:T(8,128)(2,1)}), bf16[32,32,1024]{2,1,0:T(8,128)(2,1)}, u32[]{:S(2)}, u32[]{:S(2)}) async-start(bf16[32,32,1024]{2,1,0:T(8,128)(2,1)} %bitcast.14), calls=%async_computation | async-start | bytes 4194304 | tf_op jit(solution)/shard_map/all_to_all | solution.py:407
  12.0 0.0 copy-done
  12.0 0.0 copy-done.1
  12.0 0.0 copy-done.2
  12.0 0.0 copy-done.3
  12.0 0.2 rebuilt_half.1
  12.2 2.9 %collective-permute-start.5 = (bf16[128,768]{1,0:T(8,128)(2,1)S(1)}, bf16[128,768]{1,0:T(8,128)(2,1)S(1)}, u32[]{:S(2)}, u32[]{:S(2)}) collective-permute-start(bf16[128,768]{1,0:T(8,128)(2,1)S(1)} %get-tuple-element.11), channel_id=1, source_target_pairs={{0,132},{1,133},{2,134},{3,135},{4,128},{5,129},{6,130},{7,131},{8... | collective-permute-start | bytes 589832 | tf_op jit(solution)/shard_map/ppermute | solution.py:47
  15.1 0.1 collective-permute-start
  15.2 0.8 constant_dynamic-update-slice_fusion.4
  16.0 4.1 %collective-permute-done.5 = bf16[128,768]{1,0:T(8,128)(2,1)S(1)} collective-permute-done((bf16[128,768]{1,0:T(8,128)(2,1)S(1)}, bf16[128,768]{1,0:T(8,128)(2,1)S(1)}, u32[]{:S(2)}, u32[]{:S(2)}) %collective-permute-start.5) | collective-permute-done | bytes 196640 | tf_op jit(solution)/shard_map/ppermute | solution.py:47
  20.2 2.6 %collective-permute-start.8 = (bf16[2,128,768]{2,1,0:T(8,128)(2,1)S(1)}, bf16[2,128,768]{2,1,0:T(8,128)(2,1)S(1)}, u32[]{:S(2)}, u32[]{:S(2)}) collective-permute-start(bf16[2,128,768]{2,1,0:T(8,128)(2,1)S(1)} %pad_maximum_fusion.1), channel_id=1, source_target_pairs={{0,3},{1,0},{2,1},{3,2},{4,7},{5,4},{6,5},{7,6},{8,11},{9,8},{10,9... | collective-permute-start | bytes 1179656 | tf_op jit(solution)/shard_map/ppermute | solution.py:47
  22.7 0.5 collective-permute-start.7
  23.3 0.6 collective-permute-start.6
  23.9 3.3 %collective-permute-done = bf16[128,1280]{1,0:T(8,128)(2,1)S(1)} collective-permute-done((bf16[128,1280]{1,0:T(8,128)(2,1)S(1)}, bf16[128,1280]{1,0:T(8,128)(2,1)S(1)}, u32[]{:S(2)}, u32[]{:S(2)}) %collective-permute-start) | collective-permute-done | bytes 327712 | tf_op jit(solution)/shard_map/ppermute | solution.py:47
  27.2 0.1 pad_maximum_fusion
  27.2 2.8 %collective-permute-start.2 = (bf16[2,128,1280]{2,1,0:T(8,128)(2,1)S(1)}, bf16[2,128,1280]{2,1,0:T(8,128)(2,1)S(1)}, u32[]{:S(2)}, u32[]{:S(2)}) collective-permute-start(bf16[2,128,1280]{2,1,0:T(8,128)(2,1)S(1)} %pad_maximum_fusion), channel_id=1, source_target_pairs={{0,2},{1,3},{2,0},{3,1},{4,6},{5,7},{6,4},{7,5},{8,10},{9,11},{10,... | collective-permute-start | bytes 1966088 | tf_op jit(solution)/shard_map/ppermute | solution.py:47
  30.1 0.3 collective-permute-start.1
  30.4 0.7 constant_dynamic-update-slice_fusion.3
  31.1 14.7 %collective-permute-done.6 = bf16[2,128,768]{2,1,0:T(8,128)(2,1)S(1)} collective-permute-done((bf16[2,128,768]{2,1,0:T(8,128)(2,1)S(1)}, bf16[2,128,768]{2,1,0:T(8,128)(2,1)S(1)}, u32[]{:S(2)}, u32[]{:S(2)}) %collective-permute-start.6) | collective-permute-done | bytes 393248 | tf_op jit(solution)/shard_map/ppermute | solution.py:47
  45.8 0.0 collective-permute-start.3
  45.9 0.0 collective-permute-done.7
  45.9 0.0 collective-permute-done.8
  46.0 0.0 copy-start.4
  46.0 9.7 %collective-permute-start.9 = (bf16[8,128,768]{2,1,0:T(8,128)(2,1)S(1)}, bf16[8,128,768]{2,1,0:T(8,128)(2,1)}, u32[]{:S(2)}, u32[]{:S(2)}) collective-permute-start(bf16[8,128,768]{2,1,0:T(8,128)(2,1)S(1)} %constant_dynamic-update-slice_fusion.5.s0), channel_id=1, source_target_pairs={{0,8},{1,9},{2,10},{3,11},{4,12},{5,13},{6,14},{7,15},{8,0},{9,1},... | collective-permute-start | bytes 4718600 | tf_op jit(solution)/shard_map/ppermute | solution.py:47
  55.7 16.1 %collective-permute-done.1 = bf16[2,128,1280]{2,1,0:T(8,128)(2,1)S(1)} collective-permute-done((bf16[2,128,1280]{2,1,0:T(8,128)(2,1)S(1)}, bf16[2,128,1280]{2,1,0:T(8,128)(2,1)S(1)}, u32[]{:S(2)}, u32[]{:S(2)}) %collective-permute-start.1) | collective-permute-done | bytes 655392 | tf_op jit(solution)/shard_map/ppermute | solution.py:47
  71.8 0.9 constant_dynamic-update-slice_fusion.2
  72.7 0.0 collective-permute-done.2
  72.7 0.9 constant_dynamic-update-slice_fusion.1
  73.6 0.0 collective-permute-done.3
  73.7 0.9 constant_dynamic-update-slice_fusion.s0
  74.6 0.0 copy-done.4
  74.6 0.5 collective-permute-start.4
  75.1 0.0 collective-permute-done.9.s1
  75.1 0.0 all-to-all-done.x_hbm
  75.1 10.7 %col_heads.1 = bf16[32,32,512]{2,1,0:T(8,128)(2,1)} custom-call(bf16[32,32,1024]{2,1,0:T(8,128)(2,1)} %all-to-all-done.x_hbm, bf16[8,128,768]{2,1,0:T(8,128)(2,1)} %copy-done.4, bf16[8,128,768]{2,1,0:T(8,128)(2,1)} %collective-permute-done.9.s1), custom_call_target="tpu_custom_call" | custom-call | flops 4000000000 | bytes 6291456 | tf_op jit(solution)/shard_map/col_heads/pallas_call | solution.py:354
  85.8 6.8 %all-to-all-start.1 = ((bf16[32,32,512]{2,1,0:T(8,128)(2,1)}), bf16[32,32,512]{2,1,0:T(8,128)(2,1)}, u32[]{:S(2)}, u32[]{:S(2)}) async-start(bf16[32,32,512]{2,1,0:T(8,128)(2,1)} %col_heads.1), calls=%async_computation.1 | async-start | bytes 2097152 | tf_op jit(solution)/shard_map/all_to_all | solution.py:407
  92.6 0.0 collective-permute-done.4.s1
  92.6 19.9 %row_heads.1 = (f32[1024,1024]{1,0:T(8,128)}, bf16[2,512,512]{2,1,0:T(8,128)(2,1)}) custom-call(bf16[1024,1024]{1,0:T(8,128)(2,1)} %bitcast.15, bf16[8,128,1280]{2,1,0:T(8,128)(2,1)} %constant_dynamic-update-slice_fusion.s0, bf16[8,128,1280]{2,1,0:T(8,128)(2,1)} %collective-permute-done.4.s1), custom_call_target="tpu_custom_call" | custom-call | flops 7000000000 | bytes 12582912 | tf_op jit(solution)/shard_map/row_heads/pallas_call | solution.py:325
  112.5 7.1 %all-to-all-done.1 = bf16[32,32,512]{2,1,0:T(8,128)(2,1)} async-done(((bf16[32,32,512]{2,1,0:T(8,128)(2,1)}), bf16[32,32,512]{2,1,0:T(8,128)(2,1)}, u32[]{:S(2)}, u32[]{:S(2)}) %all-to-all-start.1) | async-done | bytes 1048608 | tf_op jit(solution)/shard_map/all_to_all | solution.py:407
  119.6 5.1 %project_out.1 = bf16[1024,1024]{1,0:T(8,128)(2,1)} custom-call(f32[1024,1024]{1,0:T(8,128)} %get-tuple-element.10.part_hbm, bf16[1024,512]{1,0:T(8,128)(2,1)} %bitcast.6.col_hbm, bf16[2,512,512]{2,1,0:T(8,128)(2,1)} %get-tuple-element.12.w_hbm), custom_call_target="tpu_custom_call" | custom-call | flops 1000000000 | bytes 8388608 | tf_op jit(solution)/shard_map/project_out/pallas_call | solution.py:380
  (6 shorter events, 0.1 us)
Async XLA Ops:
  0.0 12.0 %copy-start = (bf16[128,3072]{1,0:T(8,128)(2,1)S(1)}, bf16[128,3072]{1,0:T(8,128)(2,1)}, u32[]{:S(2)}) copy-start(bf16[128,3072]{1,0:T(8,128)(2,1)} %qb_ref.1) | copy-start | bytes 2359300
  0.0 12.0 %copy-start.1 = (bf16[128,3072]{1,0:T(8,128)(2,1)S(1)}, bf16[128,3072]{1,0:T(8,128)(2,1)}, u32[]{:S(2)}) copy-start(bf16[128,3072]{1,0:T(8,128)(2,1)} %qd_ref.1) | copy-start | bytes 2359300
  0.0 12.0 %copy-start.2 = (bf16[128,1024]{1,0:T(8,128)(2,1)S(1)}, bf16[128,1024]{1,0:T(8,128)(2,1)}, u32[]{:S(2)}) copy-start(bf16[128,1024]{1,0:T(8,128)(2,1)} %ob_ref.1) | copy-start | bytes 786436
  0.0 12.0 %copy-start.3 = (bf16[128,1024]{1,0:T(8,128)(2,1)S(1)}, bf16[128,1024]{1,0:T(8,128)(2,1)}, u32[]{:S(2)}) copy-start(bf16[128,1024]{1,0:T(8,128)(2,1)} %od_ref.1) | copy-start | bytes 786436
  0.0 75.1 %all-to-all-start = ((bf16[32,32,1024]{2,1,0:T(8,128)(2,1)}), bf16[32,32,1024]{2,1,0:T(8,128)(2,1)}, u32[]{:S(2)}, u32[]{:S(2)}) async-start(bf16[32,32,1024]{2,1,0:T(8,128)(2,1)} %bitcast.14), calls=%async_computation | async-start | bytes 4194304 | tf_op jit(solution)/shard_map/all_to_all | solution.py:407
  12.2 7.9 %collective-permute-start.5 = (bf16[128,768]{1,0:T(8,128)(2,1)S(1)}, bf16[128,768]{1,0:T(8,128)(2,1)S(1)}, u32[]{:S(2)}, u32[]{:S(2)}) collective-permute-start(bf16[128,768]{1,0:T(8,128)(2,1)S(1)} %get-tuple-element.11), channel_id=1, source_target_pairs={{0,132},{1,133},{2,134},{3,135},{4,128},{5,129},{6,130},{7,131},{8... | collective-permute-start | bytes 589832 | tf_op jit(solution)/shard_map/ppermute | solution.py:47
  15.1 12.0 %collective-permute-start = (bf16[128,1280]{1,0:T(8,128)(2,1)S(1)}, bf16[128,1280]{1,0:T(8,128)(2,1)S(1)}, u32[]{:S(2)}, u32[]{:S(2)}) collective-permute-start(bf16[128,1280]{1,0:T(8,128)(2,1)S(1)} %get-tuple-element.9), channel_id=1, source_target_pairs={{0,132},{1,133},{2,134},{3,135},{4,128},{5,129},{6,130},{7,131},{8... | collective-permute-start | bytes 983048 | tf_op jit(solution)/shard_map/ppermute | solution.py:47
  20.2 25.7 %collective-permute-start.8 = (bf16[2,128,768]{2,1,0:T(8,128)(2,1)S(1)}, bf16[2,128,768]{2,1,0:T(8,128)(2,1)S(1)}, u32[]{:S(2)}, u32[]{:S(2)}) collective-permute-start(bf16[2,128,768]{2,1,0:T(8,128)(2,1)S(1)} %pad_maximum_fusion.1), channel_id=1, source_target_pairs={{0,3},{1,0},{2,1},{3,2},{4,7},{5,4},{6,5},{7,6},{8,11},{9,8},{10,9... | collective-permute-start | bytes 1179656 | tf_op jit(solution)/shard_map/ppermute | solution.py:47
  22.7 23.1 %collective-permute-start.7 = (bf16[2,128,768]{2,1,0:T(8,128)(2,1)S(1)}, bf16[2,128,768]{2,1,0:T(8,128)(2,1)S(1)}, u32[]{:S(2)}, u32[]{:S(2)}) collective-permute-start(bf16[2,128,768]{2,1,0:T(8,128)(2,1)S(1)} %pad_maximum_fusion.1), channel_id=1, source_target_pairs={{0,2},{1,3},{2,0},{3,1},{4,6},{5,7},{6,4},{7,5},{8,10},{9,11},{10,... | collective-permute-start | bytes 1179656 | tf_op jit(solution)/shard_map/ppermute | solution.py:47
  23.3 22.6 %collective-permute-start.6 = (bf16[2,128,768]{2,1,0:T(8,128)(2,1)S(1)}, bf16[2,128,768]{2,1,0:T(8,128)(2,1)S(1)}, u32[]{:S(2)}, u32[]{:S(2)}) collective-permute-start(bf16[2,128,768]{2,1,0:T(8,128)(2,1)S(1)} %pad_maximum_fusion.1), channel_id=1, source_target_pairs={{0,1},{1,2},{2,3},{3,0},{4,5},{5,6},{6,7},{7,4},{8,9},{9,10},{10,1... | collective-permute-start | bytes 1179656 | tf_op jit(solution)/shard_map/ppermute | solution.py:47
  27.2 45.5 %collective-permute-start.2 = (bf16[2,128,1280]{2,1,0:T(8,128)(2,1)S(1)}, bf16[2,128,1280]{2,1,0:T(8,128)(2,1)S(1)}, u32[]{:S(2)}, u32[]{:S(2)}) collective-permute-start(bf16[2,128,1280]{2,1,0:T(8,128)(2,1)S(1)} %pad_maximum_fusion), channel_id=1, source_target_pairs={{0,2},{1,3},{2,0},{3,1},{4,6},{5,7},{6,4},{7,5},{8,10},{9,11},{10,... | collective-permute-start | bytes 1966088 | tf_op jit(solution)/shard_map/ppermute | solution.py:47
  30.1 41.7 %collective-permute-start.1 = (bf16[2,128,1280]{2,1,0:T(8,128)(2,1)S(1)}, bf16[2,128,1280]{2,1,0:T(8,128)(2,1)S(1)}, u32[]{:S(2)}, u32[]{:S(2)}) collective-permute-start(bf16[2,128,1280]{2,1,0:T(8,128)(2,1)S(1)} %pad_maximum_fusion), channel_id=1, source_target_pairs={{0,1},{1,2},{2,3},{3,0},{4,5},{5,6},{6,7},{7,4},{8,9},{9,10},{10,1... | collective-permute-start | bytes 1966088 | tf_op jit(solution)/shard_map/ppermute | solution.py:47
  45.8 27.8 %collective-permute-start.3 = (bf16[2,128,1280]{2,1,0:T(8,128)(2,1)S(1)}, bf16[2,128,1280]{2,1,0:T(8,128)(2,1)S(1)}, u32[]{:S(2)}, u32[]{:S(2)}) collective-permute-start(bf16[2,128,1280]{2,1,0:T(8,128)(2,1)S(1)} %pad_maximum_fusion), channel_id=1, source_target_pairs={{0,3},{1,0},{2,1},{3,2},{4,7},{5,4},{6,5},{7,6},{8,11},{9,8},{10,9... | collective-permute-start | bytes 1966088 | tf_op jit(solution)/shard_map/ppermute | solution.py:47
  46.0 28.6 %copy-start.4 = (bf16[8,128,768]{2,1,0:T(8,128)(2,1)}, bf16[8,128,768]{2,1,0:T(8,128)(2,1)S(1)}, u32[]{:S(2)}) copy-start(bf16[8,128,768]{2,1,0:T(8,128)(2,1)S(1)} %constant_dynamic-update-slice_fusion.5.s0) | copy-start | bytes 4718596
  46.0 29.1 %collective-permute-start.9 = (bf16[8,128,768]{2,1,0:T(8,128)(2,1)S(1)}, bf16[8,128,768]{2,1,0:T(8,128)(2,1)}, u32[]{:S(2)}, u32[]{:S(2)}) collective-permute-start(bf16[8,128,768]{2,1,0:T(8,128)(2,1)S(1)} %constant_dynamic-update-slice_fusion.5.s0), channel_id=1, source_target_pairs={{0,8},{1,9},{2,10},{3,11},{4,12},{5,13},{6,14},{7,15},{8,0},{9,1},... | collective-permute-start | bytes 4718600 | tf_op jit(solution)/shard_map/ppermute | solution.py:47
  74.6 18.1 %collective-permute-start.4 = (bf16[8,128,1280]{2,1,0:T(8,128)(2,1)}, bf16[8,128,1280]{2,1,0:T(8,128)(2,1)}, u32[]{:S(2)}, u32[]{:S(2)}) collective-permute-start(bf16[8,128,1280]{2,1,0:T(8,128)(2,1)} %constant_dynamic-update-slice_fusion.s0), channel_id=1, source_target_pairs={{0,8},{1,9},{2,10},{3,11},{4,12},{5,13},{6,14},{7,15},{8,0},{9,1},... | collective-permute-start | bytes 7864328 | tf_op jit(solution)/shard_map/ppermute | solution.py:47
  85.8 33.8 %all-to-all-start.1 = ((bf16[32,32,512]{2,1,0:T(8,128)(2,1)}), bf16[32,32,512]{2,1,0:T(8,128)(2,1)}, u32[]{:S(2)}, u32[]{:S(2)}) async-start(bf16[32,32,512]{2,1,0:T(8,128)(2,1)} %col_heads.1), calls=%async_computation.1 | async-start | bytes 2097152 | tf_op jit(solution)/shard_map/all_to_all | solution.py:407

commit v3 on v2

--- a/solution.py
+++ b/solution.py
@@ -39,7 +39,6 @@
     )
 
 
-HOPS = [hop(other_y, dx) for other_y in range(2) for dx in range(4)]
 CORE = pairs(lambda yl, z, c, yh, x: (yl, z, 1 - c, yh, x))
 
 
@@ -57,14 +56,14 @@
     mine = lax.axis_index("fsdp")
     copies = []
     for n, slab in enumerate(slabs):
-        half = core if n == 0 else 1 - core
-        for k in range(8):
-            y_hi = mine // 4 if k % 2 == 0 else 1 - mine // 4
-            feature = pl.multiple_of((y_hi * 4 + (mine % 4 - k // 2 + 4) % 4) * 128, 128)
+        half = core if n < 4 else 1 - core
+        for k in range(2):
+            y_hi = mine // 4 if k == 0 else 1 - mine // 4
+            feature = pl.multiple_of((y_hi * 4 + (mine % 4 - n % 4 + 4) % 4) * 128, 128)
             copy = pltpu.make_async_copy(
                 slab.at[k, :, pl.ds(first, width)],
                 dest.at[half, pl.ds(feature, 128), :],
-                sems.at[n * 8 + k],
+                sems.at[n * 2 + k],
             )
             copy.start()
             copies.append(copy)
@@ -138,8 +137,9 @@
     return (both[:, :PAIR] / both[:, PAIR:]).astype(BF16)
 
 
-def row_kernel(x_ref, s0, s1, part_hbm, wc_hbm, w, wo, qkv, attended, mask_ref, part, sems, sems_o, sems_part):
-    slabs = (s0, s1)
+def row_kernel(x_ref, *refs):
+    slabs = refs[:8]
+    part_hbm, wc_hbm, w, wo, qkv, attended, mask_ref, part, sems, sems_o, sems_part = refs[8:]
     copies = fetch_weights(slabs, 0, 768, w, sems)
     copies_out = fetch_weights(slabs, 768, 512, wo, sems_o)
     block = 256
@@ -209,9 +209,8 @@
         ref[:, at : at + 128] = jnp.where(wanted == lane + at, 1.0, 0.0).astype(BF16)
 
 
-def col_kernel(
-    x_hbm, s0, s1, o_hbm, x, w, out, mask_ref, sort_ref, back_ref, normed_ref, sems, sems_x, sems_o
-):
+def col_kernel(x_hbm, *refs):
+    o_hbm, x, w, out, mask_ref, sort_ref, back_ref, normed_ref, sems, sems_x, sems_o = refs[8:]
     steps = x.shape[1] // WIDE
     arrive, leave = [], []
     for i in range(steps):
@@ -219,7 +218,7 @@
         arrive.append(pltpu.make_async_copy(x_hbm.at[:, at, :], x.at[:, at, :], sems_x.at[i]))
         leave.append(pltpu.make_async_copy(out.at[:, at, :], o_hbm.at[:, at, :], sems_o.at[i]))
         arrive[i].start()
-    weights = fetch_weights((s0, s1), 0, 768, w, sems)
+    weights = fetch_weights(refs[:8], 0, 768, w, sems)
     at = lax.broadcasted_iota(jnp.int32, (128, 128), 0)
     to = lax.broadcasted_iota(jnp.int32, (128, 128), 1)
     meets = jnp.logical_and(at // 32 == to // 32, to <= at)
@@ -328,7 +327,7 @@
             jax.ShapeDtypeStruct((STRIDE, D), F32),
             jax.ShapeDtypeStruct((2, HALF, 512), BF16),
         ),
-        in_specs=[WHOLE] + [ANY] * 2,
+        in_specs=[WHOLE] + [ANY] * 8,
         out_specs=(FAR, FAR),
         scratch_shapes=[
             pltpu.VMEM((2, D, 768), BF16),
@@ -354,7 +353,7 @@
     return pl.pallas_call(
         col_kernel,
         out_shape=jax.ShapeDtypeStruct((rows, cols, HALF), BF16),
-        in_specs=[FAR] + [ANY] * 2,
+        in_specs=[FAR] + [ANY] * 8,
         out_specs=FAR,
         scratch_shapes=[
             pltpu.VMEM((rows, cols, D), BF16),
@@ -409,21 +408,29 @@
     )
 
 
-def gathered(own):
-    both = jnp.stack([own, send(own, HOPS[4])])
-    slab = jnp.concatenate([both] + [send(both, where) for where in HOPS[1:4]])
-    return slab, send(slab, CORE)
+def with_far_y(own):
+    return jnp.stack([own, send(own, hop(1, 0))])
+
+
+def along_x(both):
+    return [both] + [send(both, hop(0, dx)) for dx in range(1, 4)]
+
+
+def both_cores(pieces):
+    return pieces + [send(piece, CORE) for piece in pieces]
 
 
 def shards(tokens, qkv_base, qkv_dir, out_base, out_dir, alpha_index):
     sequence = tokens[0]
     columns = exchange(sequence.reshape(32, 32, D))
     own_cols, own_rest = rebuilt_half(alpha_index, qkv_base, qkv_dir, out_base, out_dir)
-    col_slabs = gathered(own_cols)
-    rest_slabs = gathered(own_rest)
-    attended = col_heads(columns, col_slabs)
+    col_pieces = along_x(with_far_y(own_cols))
+    rest_both, col_pieces = lax.optimization_barrier((with_far_y(own_rest), col_pieces))
+    rest_pieces = along_x(rest_both)
+    attended = col_heads(columns, both_cores(col_pieces))
     col_out = exchange(attended)
-    row_part, weights = row_heads(sequence, rest_slabs)
+    rest_pieces, attended = lax.optimization_barrier((rest_pieces, attended))
+    row_part, weights = row_heads(sequence, both_cores(rest_pieces))
     return project_out(row_part, col_out.reshape(STRIDE, HALF), weights)[None]
 
 

time: 125 us -> 143 us (1.14)
  waiting for transfers between devices: 45.4 us -> 75 us
  starting transfers between devices: 38.2 us -> 29.3 us
  local copies, waits for them, and re-layouts: 4.39 us -> 1.65 us
    ppermute x10 -> x16, waiting for transfers between devices: 38.3 us -> 62.2 us  [send(): return lax.ppermute(value, BOTH, where)]
    ppermute x10 -> x16, starting transfers between devices: 20 us -> 12.5 us  [send(): return lax.ppermute(value, BOTH, where)]
    all_to_all x2, waiting for transfers between devices: 7.09 us -> 12.9 us  [exchange(): lax.all_to_all(blocks, 'seq', split_axis=0, concat_axis=0, tiled=True, ax...]
    unnamed x18 -> x38, local copies, waits for them, and re-layouts: 3.45 us -> 1.65 us
  transfers between devices with their start and end apart: 12 -> 18, of which waited for: 5 -> 15; matrix products, arithmetic and copies ran while one was open for 4% -> 0% of each run, Pallas kernels for 25% -> 14%
where the time goes in v3:
time: 143 us
  waiting for transfers between devices  75 us (52%)
  Pallas kernels  35.9 us (25%)
  starting transfers between devices  29.3 us (20%)
  local copies, waits for them, and re-layouts  1.65 us (1%)
    ppermute x16, waiting for transfers between devices, send(): return lax.ppermute(value, BOTH, where)  62.2 us
    pallas_call x1, Pallas kernels, row_heads(): pl.pallas_call(row_kernel, out_shape=(jax.ShapeDtypeStruct((STRIDE, D), F...  19.9 us
    all_to_all x2, starting transfers between devices, exchange(): lax.all_to_all(blocks, 'seq', split_axis=0, concat_axis=0, tiled=True, ax...  16.8 us
    all_to_all x2, waiting for transfers between devices, exchange(): lax.all_to_all(blocks, 'seq', split_axis=0, concat_axis=0, tiled=True, ax...  12.9 us
    ppermute x16, starting transfers between devices, send(): return lax.ppermute(value, BOTH, where)  12.5 us
    pallas_call x1, Pallas kernels, col_heads(): pl.pallas_call(col_kernel, out_shape=jax.ShapeDtypeStruct((rows, cols, HA...  10.7 us
    pallas_call x1, Pallas kernels, project_out(): pl.pallas_call(out_kernel, out_shape=jax.ShapeDtypeStruct((STRIDE, D), BF...  5.1 us
  transfers between devices with their start and end apart: 18, of which 15 were waited for; matrix products, arithmetic and copies ran while one was open for 0% of the time, Pallas kernels for 14%

profile of v3, /device:TPU:1, one launch (start us, length us, event | category | flops | bytes accessed | tf_op | source)
XLA Modules:
  0.0 142.9 jit_solution(4276660406947994586)
XLA Ops:
  0.0 11.3 %all-to-all-start = ((bf16[32,32,1024]{2,1,0:T(8,128)(2,1)}), bf16[32,32,1024]{2,1,0:T(8,128)(2,1)}, u32[]{:S(2)}, u32[]{:S(2)}) async-start(bf16[32,32,1024]{2,1,0:T(8,128)(2,1)} %bitcast.10), calls=%async_computation | async-start | bytes 4194304 | tf_op jit(solution)/shard_map/all_to_all | solution.py:406
  12.0 0.0 copy-done
  12.0 0.0 copy-done.1
  12.0 0.0 copy-done.2
  12.0 0.0 copy-done.3
  12.0 0.2 rebuilt_half.1
  12.2 2.9 %collective-permute-start.1 = (bf16[128,768]{1,0:T(8,128)(2,1)S(1)}, bf16[128,768]{1,0:T(8,128)(2,1)S(1)}, u32[]{:S(2)}, u32[]{:S(2)}) collective-permute-start(bf16[128,768]{1,0:T(8,128)(2,1)S(1)} %get-tuple-element.19), channel_id=1, source_target_pairs={{0,132},{1,133},{2,134},{3,135},{4,128},{5,129},{6,130},{7,131},{8... | collective-permute-start | bytes 589832 | tf_op jit(solution)/shard_map/ppermute | solution.py:46
  15.1 0.1 collective-permute-start
  15.2 4.9 %collective-permute-done.1 = bf16[128,768]{1,0:T(8,128)(2,1)S(1)} collective-permute-done((bf16[128,768]{1,0:T(8,128)(2,1)S(1)}, bf16[128,768]{1,0:T(8,128)(2,1)S(1)}, u32[]{:S(2)}, u32[]{:S(2)}) %collective-permute-start.1) | collective-permute-done | bytes 196640 | tf_op jit(solution)/shard_map/ppermute | solution.py:46
  20.2 2.6 %collective-permute-start.4 = (bf16[2,128,768]{2,1,0:T(8,128)(2,1)S(1)}, bf16[2,128,768]{2,1,0:T(8,128)(2,1)S(1)}, u32[]{:S(2)}, u32[]{:S(2)}) collective-permute-start(bf16[2,128,768]{2,1,0:T(8,128)(2,1)S(1)} %pad_maximum_fusion.1.refs_0_), channel_id=1, source_target_pairs={{0,3},{1,0},{2,1},{3,2},{4,7},{5,4},{6,5},{7,6},{8,11},{9,8},{10,9... | collective-permute-start | bytes 1179656 | tf_op jit(solution)/shard_map/ppermute | solution.py:46
  22.7 0.5 collective-permute-start.3
  23.3 0.6 collective-permute-start.2
  23.9 3.3 %collective-permute-done = bf16[128,1280]{1,0:T(8,128)(2,1)S(1)} collective-permute-done((bf16[128,1280]{1,0:T(8,128)(2,1)S(1)}, bf16[128,1280]{1,0:T(8,128)(2,1)S(1)}, u32[]{:S(2)}, u32[]{:S(2)}) %collective-permute-start) | collective-permute-done | bytes 327712 | tf_op jit(solution)/shard_map/ppermute | solution.py:46
  27.2 0.1 pad_maximum_fusion.refs_0_
  27.2 0.0 copy-start.4
  27.2 3.3 %collective-permute-done.4.refs_3_ = bf16[2,128,768]{2,1,0:T(8,128)(2,1)S(1)} collective-permute-done((bf16[2,128,768]{2,1,0:T(8,128)(2,1)S(1)}, bf16[2,128,768]{2,1,0:T(8,128)(2,1)S(1)}, u32[]{:S(2)}, u32[]{:S(2)}) %collective-permute-start.4) | collective-permute-done | bytes 393248 | tf_op jit(solution)/shard_map/ppermute | solution.py:46
  30.5 2.8 %collective-permute-done.3.refs_2_ = bf16[2,128,768]{2,1,0:T(8,128)(2,1)S(1)} collective-permute-done((bf16[2,128,768]{2,1,0:T(8,128)(2,1)S(1)}, bf16[2,128,768]{2,1,0:T(8,128)(2,1)S(1)}, u32[]{:S(2)}, u32[]{:S(2)}) %collective-permute-start.3) | collective-permute-done | bytes 393248 | tf_op jit(solution)/shard_map/ppermute | solution.py:46
  33.4 10.5 %collective-permute-done.2.refs_1_ = bf16[2,128,768]{2,1,0:T(8,128)(2,1)S(1)} collective-permute-done((bf16[2,128,768]{2,1,0:T(8,128)(2,1)S(1)}, bf16[2,128,768]{2,1,0:T(8,128)(2,1)S(1)}, u32[]{:S(2)}, u32[]{:S(2)}) %collective-permute-start.2) | collective-permute-done | bytes 393248 | tf_op jit(solution)/shard_map/ppermute | solution.py:46
  43.8 0.4 collective-permute-start.8
  44.2 0.1 collective-permute-start.9
  44.3 0.4 collective-permute-start.10
  44.7 0.1 collective-permute-start.11
  44.9 0.7 collective-permute-done.8.refs_4_
  45.6 0.6 collective-permute-done.9.refs_5_
  46.1 1.1 collective-permute-done.10.refs_6_
  47.3 0.8 copy-done.18
  48.0 0.0 collective-permute-done.11.refs_7_
  48.0 12.9 %all-to-all-done.x_hbm = bf16[32,32,1024]{2,1,0:T(8,128)(2,1)} async-done(((bf16[32,32,1024]{2,1,0:T(8,128)(2,1)}), bf16[32,32,1024]{2,1,0:T(8,128)(2,1)}, u32[]{:S(2)}, u32[]{:S(2)}) %all-to-all-start) | async-done | bytes 2097184 | tf_op jit(solution)/shard_map/all_to_all | solution.py:406
  60.9 10.7 %col_heads.1 = bf16[32,32,512]{2,1,0:T(8,128)(2,1)} custom-call(bf16[32,32,1024]{2,1,0:T(8,128)(2,1)} %all-to-all-done.x_hbm, bf16[2,128,768]{2,1,0:T(8,128)(2,1)} %copy-done.5, bf16[2,128,768]{2,1,0:T(8,128)(2,1)} %copy-done.15, bf16[2,128,768]{2,1,0:T(8,128)(2,1)} %copy-done.14, bf16[2,128,768]{2,1,0:T(8,128)(2,1)} %copy-done.13, ...), custom_call_target="tpu_custom_call" | custom-call | flops 4000000000 | bytes 6291456 | tf_op jit(solution)/shard_map/col_heads/pallas_call | solution.py:353
  71.6 5.4 %all-to-all-start.1 = ((bf16[32,32,512]{2,1,0:T(8,128)(2,1)}), bf16[32,32,512]{2,1,0:T(8,128)(2,1)}, u32[]{:S(2)}, u32[]{:S(2)}) async-start(bf16[32,32,512]{2,1,0:T(8,128)(2,1)} %col_heads.1), calls=%async_computation.1 | async-start | bytes 2097152 | tf_op jit(solution)/shard_map/all_to_all | solution.py:406
  77.1 2.6 %collective-permute-start.7 = (bf16[2,128,1280]{2,1,0:T(8,128)(2,1)S(1)}, bf16[2,128,1280]{2,1,0:T(8,128)(2,1)S(1)}, u32[]{:S(2)}, u32[]{:S(2)}) collective-permute-start(bf16[2,128,1280]{2,1,0:T(8,128)(2,1)S(1)} %pad_maximum_fusion.refs_0_), channel_id=1, source_target_pairs={{0,3},{1,0},{2,1},{3,2},{4,7},{5,4},{6,5},{7,6},{8,11},{9,8},{10,9... | collective-permute-start | bytes 1966088 | tf_op jit(solution)/shard_map/ppermute | solution.py:46
  79.6 0.5 collective-permute-start.6
  80.2 0.6 collective-permute-start.5
  80.8 26.6 %collective-permute-done.7.refs_3_ = bf16[2,128,1280]{2,1,0:T(8,128)(2,1)S(1)} collective-permute-done((bf16[2,128,1280]{2,1,0:T(8,128)(2,1)S(1)}, bf16[2,128,1280]{2,1,0:T(8,128)(2,1)S(1)}, u32[]{:S(2)}, u32[]{:S(2)}) %collective-permute-start.7) | collective-permute-done | bytes 655392 | tf_op jit(solution)/shard_map/ppermute | solution.py:46
  107.4 0.0 collective-permute-done.6.refs_2_
  107.4 4.5 %collective-permute-done.5.refs_1_ = bf16[2,128,1280]{2,1,0:T(8,128)(2,1)S(1)} collective-permute-done((bf16[2,128,1280]{2,1,0:T(8,128)(2,1)S(1)}, bf16[2,128,1280]{2,1,0:T(8,128)(2,1)S(1)}, u32[]{:S(2)}, u32[]{:S(2)}) %collective-permute-start.5) | collective-permute-done | bytes 655392 | tf_op jit(solution)/shard_map/ppermute | solution.py:46
  111.8 0.5 collective-permute-start.12
  112.3 0.1 collective-permute-start.13
  112.4 0.4 collective-permute-start.14
  112.9 0.1 collective-permute-start.15
  112.9 1.1 collective-permute-done.12.refs_4_
  114.1 0.9 collective-permute-done.13.refs_5_
  115.0 0.9 collective-permute-done.14.refs_6_
  115.9 0.9 collective-permute-done.15.refs_7_
  116.9 0.8 copy-done.12
  117.7 19.9 %row_heads.1 = (f32[1024,1024]{1,0:T(8,128)}, bf16[2,512,512]{2,1,0:T(8,128)(2,1)}) custom-call(bf16[1024,1024]{1,0:T(8,128)(2,1)} %bitcast.11, bf16[2,128,1280]{2,1,0:T(8,128)(2,1)} %copy-done.4, bf16[2,128,1280]{2,1,0:T(8,128)(2,1)} %copy-done.8, bf16[2,128,1280]{2,1,0:T(8,128)(2,1)} %copy-done.7, bf16[2,128,1280]{2,1,0:T(8,128)(2,1)} %copy-done.6, ...), custom_call_target="tpu_custom_call" | custom-call | flops 7000000000 | bytes 12582912 | tf_op jit(solution)/shard_map/row_heads/pallas_call | solution.py:324
  137.6 0.0 all-to-all-done.1
  137.7 5.1 %project_out.1 = bf16[1024,1024]{1,0:T(8,128)(2,1)} custom-call(f32[1024,1024]{1,0:T(8,128)} %get-tuple-element.29.part_hbm, bf16[1024,512]{1,0:T(8,128)(2,1)} %bitcast.6.col_hbm, bf16[2,512,512]{2,1,0:T(8,128)(2,1)} %get-tuple-element.30.w_hbm), custom_call_target="tpu_custom_call" | custom-call | flops 1000000000 | bytes 8388608 | tf_op jit(solution)/shard_map/project_out/pallas_call | solution.py:379
  (32 shorter events, 0.1 us)
Async XLA Ops:
  0.0 12.0 %copy-start = (bf16[128,3072]{1,0:T(8,128)(2,1)S(1)}, bf16[128,3072]{1,0:T(8,128)(2,1)}, u32[]{:S(2)}) copy-start(bf16[128,3072]{1,0:T(8,128)(2,1)} %qb_ref.1) | copy-start | bytes 2359300
  0.0 12.0 %copy-start.1 = (bf16[128,3072]{1,0:T(8,128)(2,1)S(1)}, bf16[128,3072]{1,0:T(8,128)(2,1)}, u32[]{:S(2)}) copy-start(bf16[128,3072]{1,0:T(8,128)(2,1)} %qd_ref.1) | copy-start | bytes 2359300
  0.0 12.0 %copy-start.2 = (bf16[128,1024]{1,0:T(8,128)(2,1)S(1)}, bf16[128,1024]{1,0:T(8,128)(2,1)}, u32[]{:S(2)}) copy-start(bf16[128,1024]{1,0:T(8,128)(2,1)} %ob_ref.1) | copy-start | bytes 786436
  0.0 12.0 %copy-start.3 = (bf16[128,1024]{1,0:T(8,128)(2,1)S(1)}, bf16[128,1024]{1,0:T(8,128)(2,1)}, u32[]{:S(2)}) copy-start(bf16[128,1024]{1,0:T(8,128)(2,1)} %od_ref.1) | copy-start | bytes 786436
  0.0 60.9 %all-to-all-start = ((bf16[32,32,1024]{2,1,0:T(8,128)(2,1)}), bf16[32,32,1024]{2,1,0:T(8,128)(2,1)}, u32[]{:S(2)}, u32[]{:S(2)}) async-start(bf16[32,32,1024]{2,1,0:T(8,128)(2,1)} %bitcast.10), calls=%async_computation | async-start | bytes 4194304 | tf_op jit(solution)/shard_map/all_to_all | solution.py:406
  12.2 7.9 %collective-permute-start.1 = (bf16[128,768]{1,0:T(8,128)(2,1)S(1)}, bf16[128,768]{1,0:T(8,128)(2,1)S(1)}, u32[]{:S(2)}, u32[]{:S(2)}) collective-permute-start(bf16[128,768]{1,0:T(8,128)(2,1)S(1)} %get-tuple-element.19), channel_id=1, source_target_pairs={{0,132},{1,133},{2,134},{3,135},{4,128},{5,129},{6,130},{7,131},{8... | collective-permute-start | bytes 589832 | tf_op jit(solution)/shard_map/ppermute | solution.py:46
  15.1 12.0 %collective-permute-start = (bf16[128,1280]{1,0:T(8,128)(2,1)S(1)}, bf16[128,1280]{1,0:T(8,128)(2,1)S(1)}, u32[]{:S(2)}, u32[]{:S(2)}) collective-permute-start(bf16[128,1280]{1,0:T(8,128)(2,1)S(1)} %get-tuple-element.18), channel_id=1, source_target_pairs={{0,132},{1,133},{2,134},{3,135},{4,128},{5,129},{6,130},{7,131},{8... | collective-permute-start | bytes 983048 | tf_op jit(solution)/shard_map/ppermute | solution.py:46
  20.2 23.6 %copy-start.5 = (bf16[2,128,768]{2,1,0:T(8,128)(2,1)}, bf16[2,128,768]{2,1,0:T(8,128)(2,1)S(1)}, u32[]{:S(2)}) copy-start(bf16[2,128,768]{2,1,0:T(8,128)(2,1)S(1)} %pad_maximum_fusion.1.refs_0_) | copy-start | bytes 1179652
  20.2 10.3 %collective-permute-start.4 = (bf16[2,128,768]{2,1,0:T(8,128)(2,1)S(1)}, bf16[2,128,768]{2,1,0:T(8,128)(2,1)S(1)}, u32[]{:S(2)}, u32[]{:S(2)}) collective-permute-start(bf16[2,128,768]{2,1,0:T(8,128)(2,1)S(1)} %pad_maximum_fusion.1.refs_0_), channel_id=1, source_target_pairs={{0,3},{1,0},{2,1},{3,2},{4,7},{5,4},{6,5},{7,6},{8,11},{9,8},{10,9... | collective-permute-start | bytes 1179656 | tf_op jit(solution)/shard_map/ppermute | solution.py:46
  22.7 10.6 %collective-permute-start.3 = (bf16[2,128,768]{2,1,0:T(8,128)(2,1)S(1)}, bf16[2,128,768]{2,1,0:T(8,128)(2,1)S(1)}, u32[]{:S(2)}, u32[]{:S(2)}) collective-permute-start(bf16[2,128,768]{2,1,0:T(8,128)(2,1)S(1)} %pad_maximum_fusion.1.refs_0_), channel_id=1, source_target_pairs={{0,2},{1,3},{2,0},{3,1},{4,6},{5,7},{6,4},{7,5},{8,10},{9,11},{10,... | collective-permute-start | bytes 1179656 | tf_op jit(solution)/shard_map/ppermute | solution.py:46
  23.3 20.6 %collective-permute-start.2 = (bf16[2,128,768]{2,1,0:T(8,128)(2,1)S(1)}, bf16[2,128,768]{2,1,0:T(8,128)(2,1)S(1)}, u32[]{:S(2)}, u32[]{:S(2)}) collective-permute-start(bf16[2,128,768]{2,1,0:T(8,128)(2,1)S(1)} %pad_maximum_fusion.1.refs_0_), channel_id=1, source_target_pairs={{0,1},{1,2},{2,3},{3,0},{4,5},{5,6},{6,7},{7,4},{8,9},{9,10},{10,1... | collective-permute-start | bytes 1179656 | tf_op jit(solution)/shard_map/ppermute | solution.py:46
  27.2 84.6 %copy-start.4 = (bf16[2,128,1280]{2,1,0:T(8,128)(2,1)}, bf16[2,128,1280]{2,1,0:T(8,128)(2,1)S(1)}, u32[]{:S(2)}) copy-start(bf16[2,128,1280]{2,1,0:T(8,128)(2,1)S(1)} %pad_maximum_fusion.refs_0_) | copy-start | bytes 1966084
  30.5 15.0 %copy-start.13 = (bf16[2,128,768]{2,1,0:T(8,128)(2,1)}, bf16[2,128,768]{2,1,0:T(8,128)(2,1)S(1)}, u32[]{:S(2)}) copy-start(bf16[2,128,768]{2,1,0:T(8,128)(2,1)S(1)} %collective-permute-done.4.refs_3_) | copy-start | bytes 1179652
  33.4 12.8 %copy-start.14 = (bf16[2,128,768]{2,1,0:T(8,128)(2,1)}, bf16[2,128,768]{2,1,0:T(8,128)(2,1)S(1)}, u32[]{:S(2)}) copy-start(bf16[2,128,768]{2,1,0:T(8,128)(2,1)S(1)} %collective-permute-done.3.refs_2_) | copy-start | bytes 1179652
  43.8 3.4 %copy-start.15 = (bf16[2,128,768]{2,1,0:T(8,128)(2,1)}, bf16[2,128,768]{2,1,0:T(8,128)(2,1)S(1)}, u32[]{:S(2)}) copy-start(bf16[2,128,768]{2,1,0:T(8,128)(2,1)S(1)} %collective-permute-done.2.refs_1_) | copy-start | bytes 1179652
  43.8 1.7 %collective-permute-start.8 = (bf16[2,128,768]{2,1,0:T(8,128)(2,1)S(1)}, bf16[2,128,768]{2,1,0:T(8,128)(2,1)S(1)}, u32[]{:S(2)}, u32[]{:S(2)}) collective-permute-start(bf16[2,128,768]{2,1,0:T(8,128)(2,1)S(1)} %pad_maximum_fusion.1.refs_0_), channel_id=1, source_target_pairs={{0,8},{1,9},{2,10},{3,11},{4,12},{5,13},{6,14},{7,15},{8,0},{9,1},... | collective-permute-start | bytes 1179656 | tf_op jit(solution)/shard_map/ppermute | solution.py:46
  44.2 1.9 %collective-permute-start.9 = (bf16[2,128,768]{2,1,0:T(8,128)(2,1)S(1)}, bf16[2,128,768]{2,1,0:T(8,128)(2,1)S(1)}, u32[]{:S(2)}, u32[]{:S(2)}) collective-permute-start(bf16[2,128,768]{2,1,0:T(8,128)(2,1)S(1)} %collective-permute-done.2.refs_1_), channel_id=1, source_target_pairs={{0,8},{1,9},{2,10},{3,11},{4,12},{5,13},{6,14},{7,15},{8,0},{9,1},... | collective-permute-start | bytes 1179656 | tf_op jit(solution)/shard_map/ppermute | solution.py:46
  44.3 2.9 %collective-permute-start.10 = (bf16[2,128,768]{2,1,0:T(8,128)(2,1)S(1)}, bf16[2,128,768]{2,1,0:T(8,128)(2,1)S(1)}, u32[]{:S(2)}, u32[]{:S(2)}) collective-permute-start(bf16[2,128,768]{2,1,0:T(8,128)(2,1)S(1)} %collective-permute-done.3.refs_2_), channel_id=1, source_target_pairs={{0,8},{1,9},{2,10},{3,11},{4,12},{5,13},{6,14},{7,15},{8,0},{9,1},... | collective-permute-start | bytes 1179656 | tf_op jit(solution)/shard_map/ppermute | solution.py:46
  44.7 3.3 %collective-permute-start.11 = (bf16[2,128,768]{2,1,0:T(8,128)(2,1)S(1)}, bf16[2,128,768]{2,1,0:T(8,128)(2,1)}, u32[]{:S(2)}, u32[]{:S(2)}) collective-permute-start(bf16[2,128,768]{2,1,0:T(8,128)(2,1)S(1)} %collective-permute-done.4.refs_3_), channel_id=1, source_target_pairs={{0,8},{1,9},{2,10},{3,11},{4,12},{5,13},{6,14},{7,15},{8,0},{9,1},... | collective-permute-start | bytes 1179656 | tf_op jit(solution)/shard_map/ppermute | solution.py:46
  45.6 1.7 %copy-start.16 = (bf16[2,128,768]{2,1,0:T(8,128)(2,1)}, bf16[2,128,768]{2,1,0:T(8,128)(2,1)S(1)}, u32[]{:S(2)}) copy-start(bf16[2,128,768]{2,1,0:T(8,128)(2,1)S(1)} %collective-permute-done.8.refs_4_) | copy-start | bytes 1179652
  46.1 1.1 copy-start.17
  47.3 0.8 copy-start.18
  71.6 66.0 %all-to-all-start.1 = ((bf16[32,32,512]{2,1,0:T(8,128)(2,1)}), bf16[32,32,512]{2,1,0:T(8,128)(2,1)}, u32[]{:S(2)}, u32[]{:S(2)}) async-start(bf16[32,32,512]{2,1,0:T(8,128)(2,1)} %col_heads.1), calls=%async_computation.1 | async-start | bytes 2097152 | tf_op jit(solution)/shard_map/all_to_all | solution.py:406
  77.1 30.3 %collective-permute-start.7 = (bf16[2,128,1280]{2,1,0:T(8,128)(2,1)S(1)}, bf16[2,128,1280]{2,1,0:T(8,128)(2,1)S(1)}, u32[]{:S(2)}, u32[]{:S(2)}) collective-permute-start(bf16[2,128,1280]{2,1,0:T(8,128)(2,1)S(1)} %pad_maximum_fusion.refs_0_), channel_id=1, source_target_pairs={{0,3},{1,0},{2,1},{3,2},{4,7},{5,4},{6,5},{7,6},{8,11},{9,8},{10,9... | collective-permute-start | bytes 1966088 | tf_op jit(solution)/shard_map/ppermute | solution.py:46
  79.6 27.7 %collective-permute-start.6 = (bf16[2,128,1280]{2,1,0:T(8,128)(2,1)S(1)}, bf16[2,128,1280]{2,1,0:T(8,128)(2,1)S(1)}, u32[]{:S(2)}, u32[]{:S(2)}) collective-permute-start(bf16[2,128,1280]{2,1,0:T(8,128)(2,1)S(1)} %pad_maximum_fusion.refs_0_), channel_id=1, source_target_pairs={{0,2},{1,3},{2,0},{3,1},{4,6},{5,7},{6,4},{7,5},{8,10},{9,11},{10,... | collective-permute-start | bytes 1966088 | tf_op jit(solution)/shard_map/ppermute | solution.py:46
  80.2 31.7 %collective-permute-start.5 = (bf16[2,128,1280]{2,1,0:T(8,128)(2,1)S(1)}, bf16[2,128,1280]{2,1,0:T(8,128)(2,1)S(1)}, u32[]{:S(2)}, u32[]{:S(2)}) collective-permute-start(bf16[2,128,1280]{2,1,0:T(8,128)(2,1)S(1)} %pad_maximum_fusion.refs_0_), channel_id=1, source_target_pairs={{0,1},{1,2},{2,3},{3,0},{4,5},{5,6},{6,7},{7,4},{8,9},{9,10},{10,1... | collective-permute-start | bytes 1966088 | tf_op jit(solution)/shard_map/ppermute | solution.py:46
  107.4 6.7 %copy-start.6 = (bf16[2,128,1280]{2,1,0:T(8,128)(2,1)}, bf16[2,128,1280]{2,1,0:T(8,128)(2,1)S(1)}, u32[]{:S(2)}) copy-start(bf16[2,128,1280]{2,1,0:T(8,128)(2,1)S(1)} %collective-permute-done.7.refs_3_) | copy-start | bytes 1966084
  107.4 9.5 %copy-start.7 = (bf16[2,128,1280]{2,1,0:T(8,128)(2,1)}, bf16[2,128,1280]{2,1,0:T(8,128)(2,1)S(1)}, u32[]{:S(2)}) copy-start(bf16[2,128,1280]{2,1,0:T(8,128)(2,1)S(1)} %collective-permute-done.6.refs_2_) | copy-start | bytes 1966084
  111.8 5.0 %copy-start.8 = (bf16[2,128,1280]{2,1,0:T(8,128)(2,1)}, bf16[2,128,1280]{2,1,0:T(8,128)(2,1)S(1)}, u32[]{:S(2)}) copy-start(bf16[2,128,1280]{2,1,0:T(8,128)(2,1)S(1)} %collective-permute-done.5.refs_1_) | copy-start | bytes 1966084
  111.8 2.2 %collective-permute-start.12 = (bf16[2,128,1280]{2,1,0:T(8,128)(2,1)S(1)}, bf16[2,128,1280]{2,1,0:T(8,128)(2,1)S(1)}, u32[]{:S(2)}, u32[]{:S(2)}) collective-permute-start(bf16[2,128,1280]{2,1,0:T(8,128)(2,1)S(1)} %pad_maximum_fusion.refs_0_), channel_id=1, source_target_pairs={{0,8},{1,9},{2,10},{3,11},{4,12},{5,13},{6,14},{7,15},{8,0},{9,1},... | collective-permute-start | bytes 1966088 | tf_op jit(solution)/shard_map/ppermute | solution.py:46
  112.3 2.7 %collective-permute-start.13 = (bf16[2,128,1280]{2,1,0:T(8,128)(2,1)S(1)}, bf16[2,128,1280]{2,1,0:T(8,128)(2,1)S(1)}, u32[]{:S(2)}, u32[]{:S(2)}) collective-permute-start(bf16[2,128,1280]{2,1,0:T(8,128)(2,1)S(1)} %collective-permute-done.5.refs_1_), channel_id=1, source_target_pairs={{0,8},{1,9},{2,10},{3,11},{4,12},{5,13},{6,14},{7,15},{8,0},{9,1},... | collective-permute-start | bytes 1966088 | tf_op jit(solution)/shard_map/ppermute | solution.py:46
  112.4 3.5 %collective-permute-start.14 = (bf16[2,128,1280]{2,1,0:T(8,128)(2,1)S(1)}, bf16[2,128,1280]{2,1,0:T(8,128)(2,1)S(1)}, u32[]{:S(2)}, u32[]{:S(2)}) collective-permute-start(bf16[2,128,1280]{2,1,0:T(8,128)(2,1)S(1)} %collective-permute-done.6.refs_2_), channel_id=1, source_target_pairs={{0,8},{1,9},{2,10},{3,11},{4,12},{5,13},{6,14},{7,15},{8,0},{9,1},... | collective-permute-start | bytes 1966088 | tf_op jit(solution)/shard_map/ppermute | solution.py:46
  112.9 4.0 %collective-permute-start.15 = (bf16[2,128,1280]{2,1,0:T(8,128)(2,1)S(1)}, bf16[2,128,1280]{2,1,0:T(8,128)(2,1)S(1)}, u32[]{:S(2)}, u32[]{:S(2)}) collective-permute-start(bf16[2,128,1280]{2,1,0:T(8,128)(2,1)S(1)} %collective-permute-done.7.refs_3_), channel_id=1, source_target_pairs={{0,8},{1,9},{2,10},{3,11},{4,12},{5,13},{6,14},{7,15},{8,0},{9,1},... | collective-permute-start | bytes 1966088 | tf_op jit(solution)/shard_map/ppermute | solution.py:46
  114.1 2.8 %copy-start.9 = (bf16[2,128,1280]{2,1,0:T(8,128)(2,1)}, bf16[2,128,1280]{2,1,0:T(8,128)(2,1)S(1)}, u32[]{:S(2)}) copy-start(bf16[2,128,1280]{2,1,0:T(8,128)(2,1)S(1)} %collective-permute-done.12.refs_4_) | copy-start | bytes 1966084
  115.0 1.9 %copy-start.10 = (bf16[2,128,1280]{2,1,0:T(8,128)(2,1)}, bf16[2,128,1280]{2,1,0:T(8,128)(2,1)S(1)}, u32[]{:S(2)}) copy-start(bf16[2,128,1280]{2,1,0:T(8,128)(2,1)S(1)} %collective-permute-done.13.refs_5_) | copy-start | bytes 1966084
  115.9 1.0 copy-start.11
  116.9 0.8 copy-start.12

commit v4 on v3

--- a/solution.py
+++ b/solution.py
@@ -51,36 +51,43 @@
     return (rows * lax.rsqrt(mean_square + 1e-06)).astype(BF16)
 
 
-def fetch_weights(slabs, first, width, dest, sems):
+def fetch_weights(pieces, first, width, dest, sems):
     core = lax.axis_index("seq") % 2
     mine = lax.axis_index("fsdp")
     copies = []
-    for n, slab in enumerate(slabs):
-        half = core if n < 4 else 1 - core
-        for k in range(2):
-            y_hi = mine // 4 if k == 0 else 1 - mine // 4
-            feature = pl.multiple_of((y_hi * 4 + (mine % 4 - n % 4 + 4) % 4) * 128, 128)
-            copy = pltpu.make_async_copy(
-                slab.at[k, :, pl.ds(first, width)],
-                dest.at[half, pl.ds(feature, 128), :],
-                sems.at[n * 2 + k],
-            )
-            copy.start()
-            copies.append(copy)
+    for n, (ref, start, other_core, other_y, dx) in enumerate(pieces):
+        half = 1 - core if other_core else core
+        y_hi = 1 - mine // 4 if other_y else mine // 4
+        feature = pl.multiple_of((y_hi * 4 + (mine % 4 - dx + 4) % 4) * 128, 128)
+        copy = pltpu.make_async_copy(
+            ref.at[:, pl.ds(start + first, width)],
+            dest.at[half, pl.ds(feature, 128), :],
+            sems.at[n],
+        )
+        copy.start()
+        copies.append(copy)
     return copies
 
 
-def prep_kernel(alpha_ref, qb_ref, qd_ref, ob_ref, od_ref, cols_ref, rest_ref):
+def pieces_of(refs, start):
+    return [
+        (ref, 0 if n >= 8 else start, n % 8 >= 4, n >= 8, n % 4) for n, ref in enumerate(refs)
+    ]
+
+
+def prep_kernel(alpha_ref, qb_ref, qd_ref, ob_ref, od_ref, o_ref):
     core = lax.axis_index("seq") % 2
     step_alpha = (alpha_ref[0].astype(F32) + NALPHA) / (2.0 * NALPHA)
-    for kind, to_ref in ((1, cols_ref), (0, rest_ref)):
+    at = 0
+    for kind in (1, 0):
         for which in range(3):
             lanes = pl.ds(pl.multiple_of(which * D + kind * HALF + core * 256, 256), 256)
             rebuilt = qb_ref[:, lanes].astype(F32) + step_alpha * qd_ref[:, lanes].astype(F32)
-            to_ref[:, which * 256 : (which + 1) * 256] = rebuilt.astype(BF16)
+            o_ref[:, at : at + 256] = rebuilt.astype(BF16)
+            at += 256
     lanes = pl.ds(pl.multiple_of(core * 512, 512), 512)
     rebuilt = ob_ref[:, lanes].astype(F32) + step_alpha * od_ref[:, lanes].astype(F32)
-    rest_ref[:, 768:] = rebuilt.astype(BF16)
+    o_ref[:, at:] = rebuilt.astype(BF16)
 
 
 def soft_average(queries, keys, values_ones, mask):
@@ -138,10 +145,10 @@
 
 
 def row_kernel(x_ref, *refs):
-    slabs = refs[:8]
-    part_hbm, wc_hbm, w, wo, qkv, attended, mask_ref, part, sems, sems_o, sems_part = refs[8:]
-    copies = fetch_weights(slabs, 0, 768, w, sems)
-    copies_out = fetch_weights(slabs, 768, 512, wo, sems_o)
+    pieces = pieces_of(refs[:16], COLS)
+    part_hbm, wc_hbm, w, wo, qkv, attended, mask_ref, part, sems, sems_o, sems_part = refs[16:]
+    copies = fetch_weights(pieces, 0, 768, w, sems)
+    copies_out = fetch_weights(pieces, 768, 512, wo, sems_o)
     block = 256
     row = lax.broadcasted_iota(jnp.int32, (block, block), 0)
     col = lax.broadcasted_iota(jnp.int32, (block, block), 1)
@@ -210,7 +217,7 @@
 
 
 def col_kernel(x_hbm, *refs):
-    o_hbm, x, w, out, mask_ref, sort_ref, back_ref, normed_ref, sems, sems_x, sems_o = refs[8:]
+    o_hbm, x, w, out, mask_ref, sort_ref, back_ref, normed_ref, sems, sems_x, sems_o = refs[16:]
     steps = x.shape[1] // WIDE
     arrive, leave = [], []
     for i in range(steps):
@@ -218,7 +225,7 @@
         arrive.append(pltpu.make_async_copy(x_hbm.at[:, at, :], x.at[:, at, :], sems_x.at[i]))
         leave.append(pltpu.make_async_copy(out.at[:, at, :], o_hbm.at[:, at, :], sems_o.at[i]))
         arrive[i].start()
-    weights = fetch_weights(refs[:8], 0, 768, w, sems)
+    weights = fetch_weights(pieces_of(refs[:16], 0), 0, 768, w, sems)
     at = lax.broadcasted_iota(jnp.int32, (128, 128), 0)
     to = lax.broadcasted_iota(jnp.int32, (128, 128), 1)
     meets = jnp.logical_and(at // 32 == to // 32, to <= at)
@@ -310,11 +317,9 @@
 def rebuilt_half(alpha_index, *parts):
     return pl.pallas_call(
         prep_kernel,
-        out_shape=[
-            jax.ShapeDtypeStruct((parts[0].shape[0], width), BF16) for width in (COLS, REST)
-        ],
+        out_shape=jax.ShapeDtypeStruct((parts[0].shape[0], COLS + REST), BF16),
         in_specs=[pl.BlockSpec(memory_space=pltpu.SMEM)] + [WHOLE] * 4,
-        out_specs=[WHOLE] * 2,
+        out_specs=WHOLE,
         compiler_params=limit(16),
         name="rebuilt_half",
     )(alpha_index, *parts)
@@ -327,7 +332,7 @@
             jax.ShapeDtypeStruct((STRIDE, D), F32),
             jax.ShapeDtypeStruct((2, HALF, 512), BF16),
         ),
-        in_specs=[WHOLE] + [ANY] * 8,
+        in_specs=[WHOLE] + [ANY] * 16,
         out_specs=(FAR, FAR),
         scratch_shapes=[
             pltpu.VMEM((2, D, 768), BF16),
@@ -353,7 +358,7 @@
     return pl.pallas_call(
         col_kernel,
         out_shape=jax.ShapeDtypeStruct((rows, cols, HALF), BF16),
-        in_specs=[FAR] + [ANY] * 8,
+        in_specs=[FAR] + [ANY] * 16,
         out_specs=FAR,
         scratch_shapes=[
             pltpu.VMEM((rows, cols, D), BF16),
@@ -408,12 +413,12 @@
     )
 
 
-def with_far_y(own):
-    return jnp.stack([own, send(own, hop(1, 0))])
-
-
-def along_x(both):
-    return [both] + [send(both, hop(0, dx)) for dx in range(1, 4)]
+def along_x(piece):
+    return [piece] + [send(piece, hop(0, dx)) for dx in range(1, 4)]
+
+
+def across_y(pieces):
+    return [send(piece, hop(1, 0)) for piece in pieces]
 
 
 def both_cores(pieces):
@@ -423,14 +428,16 @@
 def shards(tokens, qkv_base, qkv_dir, out_base, out_dir, alpha_index):
     sequence = tokens[0]
     columns = exchange(sequence.reshape(32, 32, D))
-    own_cols, own_rest = rebuilt_half(alpha_index, qkv_base, qkv_dir, out_base, out_dir)
-    col_pieces = along_x(with_far_y(own_cols))
-    rest_both, col_pieces = lax.optimization_barrier((with_far_y(own_rest), col_pieces))
-    rest_pieces = along_x(rest_both)
-    attended = col_heads(columns, both_cores(col_pieces))
+    own = rebuilt_half(alpha_index, qkv_base, qkv_dir, out_base, out_dir)
+    (far_cols,) = across_y([own[:, :COLS]])
+    near = along_x(own)
+    far_cols = both_cores(along_x(far_cols))
+    far_rest = across_y([piece[:, COLS:] for piece in near])
+    near = both_cores(near)
+    attended = col_heads(columns, near + far_cols)
+    far_rest, attended = lax.optimization_barrier((far_rest, attended))
     col_out = exchange(attended)
-    rest_pieces, attended = lax.optimization_barrier((rest_pieces, attended))
-    row_part, weights = row_heads(sequence, both_cores(rest_pieces))
+    row_part, weights = row_heads(sequence, near + both_cores(far_rest))
     return project_out(row_part, col_out.reshape(STRIDE, HALF), weights)[None]
 
 

time: 143 us -> 135 us (0.944)
  waiting for transfers between devices: 75 us -> 49.4 us
  starting transfers between devices: 29.3 us -> 45.5 us
  local copies, waits for them, and re-layouts: 1.65 us -> 3.91 us
    ppermute x16 -> x23, waiting for transfers between devices: 62.2 us -> 45.8 us  [send(): return lax.ppermute(value, BOTH, where)]
    ppermute x16 -> x23, starting transfers between devices: 12.5 us -> 26.4 us  [send(): return lax.ppermute(value, BOTH, where)]
    all_to_all x2, waiting for transfers between devices: 12.9 us -> 3.61 us  [exchange(): lax.all_to_all(blocks, 'seq', split_axis=0, concat_axis=0, tiled=True, ax...]
    all_to_all x2, starting transfers between devices: 16.8 us -> 19.1 us  [exchange(): lax.all_to_all(blocks, 'seq', split_axis=0, concat_axis=0, tiled=True, ax...]
    slice x0 -> x5, local copies, waits for them, and re-layouts: none -> 2.33 us  [the longest x4 2.31 us: shards(): far_rest = across_y([piece[:, COLS:] for piece in near])]
  transfers between devices with their start and end apart: 18 -> 25, of which waited for: 15 -> 12; matrix products, arithmetic and copies ran while one was open for 0% -> 2% of each run, Pallas kernels for 14% -> 22%
where the time goes in v4:
time: 135 us
  waiting for transfers between devices  49.4 us (37%)
  starting transfers between devices  45.5 us (34%)
  Pallas kernels  35.3 us (26%)
  local copies, waits for them, and re-layouts  3.91 us (3%)
    ppermute x23, waiting for transfers between devices, send(): return lax.ppermute(value, BOTH, where)  45.8 us
    ppermute x23, starting transfers between devices, send(): return lax.ppermute(value, BOTH, where)  26.4 us
    pallas_call x1, Pallas kernels, row_heads(): pl.pallas_call(row_kernel, out_shape=(jax.ShapeDtypeStruct((STRIDE, D), F...  19.9 us
    all_to_all x2, starting transfers between devices, exchange(): lax.all_to_all(blocks, 'seq', split_axis=0, concat_axis=0, tiled=True, ax...  19.1 us
    pallas_call x1, Pallas kernels, col_heads(): pl.pallas_call(col_kernel, out_shape=jax.ShapeDtypeStruct((rows, cols, HA...  10.1 us
    pallas_call x1, Pallas kernels, project_out(): pl.pallas_call(out_kernel, out_shape=jax.ShapeDtypeStruct((STRIDE, D), BF...  5.09 us
    all_to_all x2, waiting for transfers between devices, exchange(): lax.all_to_all(blocks, 'seq', split_axis=0, concat_axis=0, tiled=True, ax...  3.61 us
  transfers between devices with their start and end apart: 25, of which 12 were waited for; matrix products, arithmetic and copies ran while one was open for 2% of the time, Pallas kernels for 22%

profile of v4, /device:TPU:1, one launch (start us, length us, event | category | flops | bytes accessed | tf_op | source)
XLA Modules:
  0.0 135.2 jit_solution(16514135085468966193)
XLA Ops:
  0.0 11.3 %all-to-all-start = ((bf16[32,32,1024]{2,1,0:T(8,128)(2,1)}), bf16[32,32,1024]{2,1,0:T(8,128)(2,1)}, u32[]{:S(2)}, u32[]{:S(2)}) async-start(bf16[32,32,1024]{2,1,0:T(8,128)(2,1)} %bitcast.4), calls=%async_computation | async-start | bytes 4194304 | tf_op jit(solution)/shard_map/all_to_all | solution.py:411
  12.0 0.2 rebuilt_half.1.refs_0_
  12.3 2.9 %collective-permute-start.11 = (bf16[128,768]{1,0:T(8,128)(2,1)S(1)}, bf16[128,768]{1,0:T(8,128)(2,1)S(1)}, u32[]{:S(2)}, u32[]{:S(2)}) collective-permute-start(bf16[128,768]{1,0:T(8,128)(2,1)S(1)} %slice.24), channel_id=1, source_target_pairs={{0,132},{1,133},{2,134},{3,135},{4,128},{5,129},{6,130},{7,131},{8... | collective-permute-start | bytes 589832 | tf_op jit(solution)/shard_map/ppermute | solution.py:46
  15.2 2.5 %collective-permute-start.2 = (bf16[128,2048]{1,0:T(8,128)(2,1)S(1)}, bf16[128,2048]{1,0:T(8,128)(2,1)S(1)}, u32[]{:S(2)}, u32[]{:S(2)}) collective-permute-start(bf16[128,2048]{1,0:T(8,128)(2,1)S(1)} %rebuilt_half.1.refs_0_), channel_id=1, source_target_pairs={{0,3},{1,0},{2,1},{3,2},{4,7},{5,4},{6,5},{7,6},{8,11},{9,8},{10,9... | collective-permute-start | bytes 1572872 | tf_op jit(solution)/shard_map/ppermute | solution.py:46
  17.7 0.5 collective-permute-start.1
  18.2 0.6 collective-permute-start
  18.8 1.4 %collective-permute-done.11.refs_8_ = bf16[128,768]{1,0:T(8,128)(2,1)S(1)} collective-permute-done((bf16[128,768]{1,0:T(8,128)(2,1)S(1)}, bf16[128,768]{1,0:T(8,128)(2,1)S(1)}, u32[]{:S(2)}, u32[]{:S(2)}) %collective-permute-start.11) | collective-permute-done | bytes 196640 | tf_op jit(solution)/shard_map/ppermute | solution.py:46
  20.2 0.9 collective-permute-start.15
  21.0 2.5 %collective-permute-start.14 = (bf16[128,768]{1,0:T(8,128)(2,1)S(1)}, bf16[128,768]{1,0:T(8,128)(2,1)S(1)}, u32[]{:S(2)}, u32[]{:S(2)}) collective-permute-start(bf16[128,768]{1,0:T(8,128)(2,1)S(1)} %collective-permute-done.11.refs_8_), channel_id=1, source_target_pairs={{0,3},{1,0},{2,1},{3,2},{4,7},{5,4},{6,5},{7,6},{8,11},{9,8},{10,9... | collective-permute-start | bytes 589832 | tf_op jit(solution)/shard_map/ppermute | solution.py:46
  23.5 1.3 collective-permute-start.13
  24.9 19.6 %collective-permute-done.14.refs_11_ = bf16[128,768]{1,0:T(8,128)(2,1)S(1)} collective-permute-done((bf16[128,768]{1,0:T(8,128)(2,1)S(1)}, bf16[128,768]{1,0:T(8,128)(2,1)S(1)}, u32[]{:S(2)}, u32[]{:S(2)}) %collective-permute-start.14) | collective-permute-done | bytes 196640 | tf_op jit(solution)/shard_map/ppermute | solution.py:46
  44.5 5.0 %collective-permute-start.3 = (bf16[128,2048]{1,0:T(8,128)(2,1)S(1)}, bf16[128,2048]{1,0:T(8,128)(2,1)S(1)}, u32[]{:S(2)}, u32[]{:S(2)}) collective-permute-start(bf16[128,2048]{1,0:T(8,128)(2,1)S(1)} %rebuilt_half.1.refs_0_), channel_id=1, source_target_pairs={{0,8},{1,9},{2,10},{3,11},{4,12},{5,13},{6,14},{7,15},{8,0},{9,1},... | collective-permute-start | bytes 1572872 | tf_op jit(solution)/shard_map/ppermute | solution.py:46
  49.5 0.0 collective-permute-done.13.refs_10_
  49.5 0.5 collective-permute-start.12
  50.0 0.0 collective-permute-done.2.refs_3_
  50.0 1.7 %collective-permute-start.6 = (bf16[128,2048]{1,0:T(8,128)(2,1)S(1)}, bf16[128,2048]{1,0:T(8,128)(2,1)S(1)}, u32[]{:S(2)}, u32[]{:S(2)}) collective-permute-start(bf16[128,2048]{1,0:T(8,128)(2,1)S(1)} %collective-permute-done.2.refs_3_), channel_id=1, source_target_pairs={{0,8},{1,9},{2,10},{3,11},{4,12},{5,13},{6,14},{7,15},{8,0},{9,1},... | collective-permute-start | bytes 1572872 | tf_op jit(solution)/shard_map/ppermute | solution.py:46
  51.7 0.1 collective-permute-start.5
  51.8 0.4 collective-permute-start.4
  52.2 6.0 %collective-permute-done.12.refs_9_ = bf16[128,768]{1,0:T(8,128)(2,1)S(1)} collective-permute-done((bf16[128,768]{1,0:T(8,128)(2,1)S(1)}, bf16[128,768]{1,0:T(8,128)(2,1)S(1)}, u32[]{:S(2)}, u32[]{:S(2)}) %collective-permute-start.12) | collective-permute-done | bytes 196640 | tf_op jit(solution)/shard_map/ppermute | solution.py:46
  58.2 0.6 collective-permute-start.18
  58.7 0.8 copy-done.8
  59.5 0.1 collective-permute-start.17
  59.6 0.2 collective-permute-done.18.refs_15_
  59.8 0.7 copy-done.18
  60.5 0.4 collective-permute-start.16
  60.9 0.8 slice.20
  61.7 0.8 slice.23
  62.4 0.8 slice.22
  63.2 0.2 collective-permute-start.7
  63.4 2.6 %collective-permute-start.10 = (bf16[128,1280]{1,0:T(8,128)(2,1)}, bf16[128,1280]{1,0:T(8,128)(2,1)}, u32[]{:S(2)}, u32[]{:S(2)}) collective-permute-start(bf16[128,1280]{1,0:T(8,128)(2,1)} %slice.23), channel_id=1, source_target_pairs={{0,132},{1,133},{2,134},{3,135},{4,128},{5,129},{6,130},{7,131},{8... | collective-permute-start | bytes 983048 | tf_op jit(solution)/shard_map/ppermute | solution.py:46
  66.0 0.1 collective-permute-start.9
  66.1 2.6 %collective-permute-start.8 = (bf16[128,1280]{1,0:T(8,128)(2,1)S(1)}, bf16[128,1280]{1,0:T(8,128)(2,1)}, u32[]{:S(2)}, u32[]{:S(2)}) collective-permute-start(bf16[128,1280]{1,0:T(8,128)(2,1)S(1)} %slice.21), channel_id=1, source_target_pairs={{0,132},{1,133},{2,134},{3,135},{4,128},{5,129},{6,130},{7,131},{8... | collective-permute-start | bytes 983048 | tf_op jit(solution)/shard_map/ppermute | solution.py:46
  68.8 10.1 %col_heads.1 = bf16[32,32,512]{2,1,0:T(8,128)(2,1)} custom-call(bf16[32,32,1024]{2,1,0:T(8,128)(2,1)} %all-to-all-done.x_hbm, bf16[128,2048]{1,0:T(8,128)(2,1)} %copy-done, bf16[128,2048]{1,0:T(8,128)(2,1)} %copy-done.7, bf16[128,2048]{1,0:T(8,128)(2,1)} %copy-done.6, bf16[128,2048]{1,0:T(8,128)(2,1)} %copy-done.5, bf16[128,2048]{1,0:T(8,128)(2,1)} %copy-done.8, ...), custom_call_target="tpu_custom_call" | custom-call | flops 4000000000 | bytes 6291456 | tf_op jit(solution)/shard_map/col_heads/pallas_call | solution.py:358
  78.9 2.1 %collective-permute-done.10.refs_11_ = bf16[128,1280]{1,0:T(8,128)(2,1)} collective-permute-done((bf16[128,1280]{1,0:T(8,128)(2,1)}, bf16[128,1280]{1,0:T(8,128)(2,1)}, u32[]{:S(2)}, u32[]{:S(2)}) %collective-permute-start.10) | collective-permute-done | bytes 327712 | tf_op jit(solution)/shard_map/ppermute | solution.py:46
  81.0 7.0 %collective-permute-done.9.refs_10_ = bf16[128,1280]{1,0:T(8,128)(2,1)} collective-permute-done((bf16[128,1280]{1,0:T(8,128)(2,1)}, bf16[128,1280]{1,0:T(8,128)(2,1)}, u32[]{:S(2)}, u32[]{:S(2)}) %collective-permute-start.9) | collective-permute-done | bytes 327712 | tf_op jit(solution)/shard_map/ppermute | solution.py:46
  88.1 7.0 %collective-permute-done.8.refs_9_ = bf16[128,1280]{1,0:T(8,128)(2,1)} collective-permute-done((bf16[128,1280]{1,0:T(8,128)(2,1)S(1)}, bf16[128,1280]{1,0:T(8,128)(2,1)}, u32[]{:S(2)}, u32[]{:S(2)}) %collective-permute-start.8) | collective-permute-done | bytes 327712 | tf_op jit(solution)/shard_map/ppermute | solution.py:46
  95.1 7.8 %all-to-all-start.1 = ((bf16[32,32,512]{2,1,0:T(8,128)(2,1)}), bf16[32,32,512]{2,1,0:T(8,128)(2,1)}, u32[]{:S(2)}, u32[]{:S(2)}) async-start(bf16[32,32,512]{2,1,0:T(8,128)(2,1)} %col_heads.1), calls=%async_computation.1 | async-start | bytes 2097152 | tf_op jit(solution)/shard_map/all_to_all | solution.py:411
  102.9 0.4 collective-permute-start.19
  103.3 0.2 collective-permute-start.20
  103.5 0.3 collective-permute-start.21
  103.8 0.2 collective-permute-start.22
  104.0 0.8 collective-permute-done.19.refs_12_
  104.8 0.5 collective-permute-done.20.refs_13_
  105.3 0.6 collective-permute-done.21.refs_14_
  105.9 0.5 collective-permute-done.22.refs_15_
  106.4 19.9 %row_heads.1 = (f32[1024,1024]{1,0:T(8,128)}, bf16[2,512,512]{2,1,0:T(8,128)(2,1)}) custom-call(bf16[1024,1024]{1,0:T(8,128)(2,1)} %bitcast.5, bf16[128,2048]{1,0:T(8,128)(2,1)} %copy-done, bf16[128,2048]{1,0:T(8,128)(2,1)} %copy-done.7, bf16[128,2048]{1,0:T(8,128)(2,1)} %copy-done.6, bf16[128,2048]{1,0:T(8,128)(2,1)} %copy-done.5, ...), custom_call_target="tpu_custom_call" | custom-call | flops 7000000000 | bytes 12582912 | tf_op jit(solution)/shard_map/row_heads/pallas_call | solution.py:329
  126.3 3.6 %all-to-all-done.1 = bf16[32,32,512]{2,1,0:T(8,128)(2,1)} async-done(((bf16[32,32,512]{2,1,0:T(8,128)(2,1)}), bf16[32,32,512]{2,1,0:T(8,128)(2,1)}, u32[]{:S(2)}, u32[]{:S(2)}) %all-to-all-start.1) | async-done | bytes 1048608 | tf_op jit(solution)/shard_map/all_to_all | solution.py:411
  129.9 5.1 %project_out.1 = bf16[1024,1024]{1,0:T(8,128)(2,1)} custom-call(f32[1024,1024]{1,0:T(8,128)} %get-tuple-element.16.part_hbm, bf16[1024,512]{1,0:T(8,128)(2,1)} %bitcast.2.col_hbm, bf16[2,512,512]{2,1,0:T(8,128)(2,1)} %get-tuple-element.18.w_hbm), custom_call_target="tpu_custom_call" | custom-call | flops 1000000000 | bytes 8388608 | tf_op jit(solution)/shard_map/project_out/pallas_call | solution.py:384
  (53 shorter events, 0.1 us)
Async XLA Ops:
  0.0 12.0 %copy-start.1 = (bf16[128,3072]{1,0:T(8,128)(2,1)S(1)}, bf16[128,3072]{1,0:T(8,128)(2,1)}, u32[]{:S(2)}) copy-start(bf16[128,3072]{1,0:T(8,128)(2,1)} %qb_ref.1) | copy-start | bytes 2359300
  0.0 12.0 %copy-start.2 = (bf16[128,3072]{1,0:T(8,128)(2,1)S(1)}, bf16[128,3072]{1,0:T(8,128)(2,1)}, u32[]{:S(2)}) copy-start(bf16[128,3072]{1,0:T(8,128)(2,1)} %qd_ref.1) | copy-start | bytes 2359300
  0.0 12.0 %copy-start.3 = (bf16[128,1024]{1,0:T(8,128)(2,1)S(1)}, bf16[128,1024]{1,0:T(8,128)(2,1)}, u32[]{:S(2)}) copy-start(bf16[128,1024]{1,0:T(8,128)(2,1)} %ob_ref.1) | copy-start | bytes 786436
  0.0 12.0 %copy-start.4 = (bf16[128,1024]{1,0:T(8,128)(2,1)S(1)}, bf16[128,1024]{1,0:T(8,128)(2,1)}, u32[]{:S(2)}) copy-start(bf16[128,1024]{1,0:T(8,128)(2,1)} %od_ref.1) | copy-start | bytes 786436
  0.0 68.7 %all-to-all-start = ((bf16[32,32,1024]{2,1,0:T(8,128)(2,1)}), bf16[32,32,1024]{2,1,0:T(8,128)(2,1)}, u32[]{:S(2)}, u32[]{:S(2)}) async-start(bf16[32,32,1024]{2,1,0:T(8,128)(2,1)} %bitcast.4), calls=%async_computation | async-start | bytes 4194304 | tf_op jit(solution)/shard_map/all_to_all | solution.py:411
  12.2 56.5 %copy-start = (bf16[128,2048]{1,0:T(8,128)(2,1)}, bf16[128,2048]{1,0:T(8,128)(2,1)S(1)}, u32[]{:S(2)}) copy-start(bf16[128,2048]{1,0:T(8,128)(2,1)S(1)} %rebuilt_half.1.refs_0_) | copy-start | bytes 1572868
  12.3 7.9 %collective-permute-start.11 = (bf16[128,768]{1,0:T(8,128)(2,1)S(1)}, bf16[128,768]{1,0:T(8,128)(2,1)S(1)}, u32[]{:S(2)}, u32[]{:S(2)}) collective-permute-start(bf16[128,768]{1,0:T(8,128)(2,1)S(1)} %slice.24), channel_id=1, source_target_pairs={{0,132},{1,133},{2,134},{3,135},{4,128},{5,129},{6,130},{7,131},{8... | collective-permute-start | bytes 589832 | tf_op jit(solution)/shard_map/ppermute | solution.py:46
  15.2 34.8 %collective-permute-start.2 = (bf16[128,2048]{1,0:T(8,128)(2,1)S(1)}, bf16[128,2048]{1,0:T(8,128)(2,1)S(1)}, u32[]{:S(2)}, u32[]{:S(2)}) collective-permute-start(bf16[128,2048]{1,0:T(8,128)(2,1)S(1)} %rebuilt_half.1.refs_0_), channel_id=1, source_target_pairs={{0,3},{1,0},{2,1},{3,2},{4,7},{5,4},{6,5},{7,6},{8,11},{9,8},{10,9... | collective-permute-start | bytes 1572872 | tf_op jit(solution)/shard_map/ppermute | solution.py:46
  17.7 34.0 %collective-permute-start.1 = (bf16[128,2048]{1,0:T(8,128)(2,1)S(1)}, bf16[128,2048]{1,0:T(8,128)(2,1)S(1)}, u32[]{:S(2)}, u32[]{:S(2)}) collective-permute-start(bf16[128,2048]{1,0:T(8,128)(2,1)S(1)} %rebuilt_half.1.refs_0_), channel_id=1, source_target_pairs={{0,2},{1,3},{2,0},{3,1},{4,6},{5,7},{6,4},{7,5},{8,10},{9,11},{10,... | collective-permute-start | bytes 1572872 | tf_op jit(solution)/shard_map/ppermute | solution.py:46
  18.2 33.6 %collective-permute-start = (bf16[128,2048]{1,0:T(8,128)(2,1)S(1)}, bf16[128,2048]{1,0:T(8,128)(2,1)S(1)}, u32[]{:S(2)}, u32[]{:S(2)}) collective-permute-start(bf16[128,2048]{1,0:T(8,128)(2,1)S(1)} %rebuilt_half.1.refs_0_), channel_id=1, source_target_pairs={{0,1},{1,2},{2,3},{3,0},{4,5},{5,6},{6,7},{7,4},{8,9},{9,10},{10,1... | collective-permute-start | bytes 1572872 | tf_op jit(solution)/shard_map/ppermute | solution.py:46
  20.2 39.4 %copy-start.13 = (bf16[128,768]{1,0:T(8,128)(2,1)}, bf16[128,768]{1,0:T(8,128)(2,1)S(1)}, u32[]{:S(2)}) copy-start(bf16[128,768]{1,0:T(8,128)(2,1)S(1)} %collective-permute-done.11.refs_8_) | copy-start | bytes 589828
  20.2 3.3 %collective-permute-start.15 = (bf16[128,768]{1,0:T(8,128)(2,1)S(1)}, bf16[128,768]{1,0:T(8,128)(2,1)S(1)}, u32[]{:S(2)}, u32[]{:S(2)}) collective-permute-start(bf16[128,768]{1,0:T(8,128)(2,1)S(1)} %collective-permute-done.11.refs_8_), channel_id=1, source_target_pairs={{0,8},{1,9},{2,10},{3,11},{4,12},{5,13},{6,14},{7,15},{8,0},{9,1},... | collective-permute-start | bytes 589832 | tf_op jit(solution)/shard_map/ppermute | solution.py:46
  21.0 23.4 %collective-permute-start.14 = (bf16[128,768]{1,0:T(8,128)(2,1)S(1)}, bf16[128,768]{1,0:T(8,128)(2,1)S(1)}, u32[]{:S(2)}, u32[]{:S(2)}) collective-permute-start(bf16[128,768]{1,0:T(8,128)(2,1)S(1)} %collective-permute-done.11.refs_8_), channel_id=1, source_target_pairs={{0,3},{1,0},{2,1},{3,2},{4,7},{5,4},{6,5},{7,6},{8,11},{9,8},{10,9... | collective-permute-start | bytes 589832 | tf_op jit(solution)/shard_map/ppermute | solution.py:46
  23.5 36.3 %copy-start.14 = (bf16[128,768]{1,0:T(8,128)(2,1)}, bf16[128,768]{1,0:T(8,128)(2,1)S(1)}, u32[]{:S(2)}) copy-start(bf16[128,768]{1,0:T(8,128)(2,1)S(1)} %collective-permute-done.15.refs_12_) | copy-start | bytes 589828
  23.5 26.0 %collective-permute-start.13 = (bf16[128,768]{1,0:T(8,128)(2,1)S(1)}, bf16[128,768]{1,0:T(8,128)(2,1)S(1)}, u32[]{:S(2)}, u32[]{:S(2)}) collective-permute-start(bf16[128,768]{1,0:T(8,128)(2,1)S(1)} %collective-permute-done.11.refs_8_), channel_id=1, source_target_pairs={{0,2},{1,3},{2,0},{3,1},{4,6},{5,7},{6,4},{7,5},{8,10},{9,11},{10,... | collective-permute-start | bytes 589832 | tf_op jit(solution)/shard_map/ppermute | solution.py:46
  44.5 15.3 %copy-start.15 = (bf16[128,768]{1,0:T(8,128)(2,1)}, bf16[128,768]{1,0:T(8,128)(2,1)S(1)}, u32[]{:S(2)}) copy-start(bf16[128,768]{1,0:T(8,128)(2,1)S(1)} %collective-permute-done.14.refs_11_) | copy-start | bytes 589828
  44.5 14.2 %collective-permute-start.3 = (bf16[128,2048]{1,0:T(8,128)(2,1)S(1)}, bf16[128,2048]{1,0:T(8,128)(2,1)S(1)}, u32[]{:S(2)}, u32[]{:S(2)}) collective-permute-start(bf16[128,2048]{1,0:T(8,128)(2,1)S(1)} %rebuilt_half.1.refs_0_), channel_id=1, source_target_pairs={{0,8},{1,9},{2,10},{3,11},{4,12},{5,13},{6,14},{7,15},{8,0},{9,1},... | collective-permute-start | bytes 1572872 | tf_op jit(solution)/shard_map/ppermute | solution.py:46
  49.5 19.2 %copy-start.16 = (bf16[128,768]{1,0:T(8,128)(2,1)}, bf16[128,768]{1,0:T(8,128)(2,1)S(1)}, u32[]{:S(2)}) copy-start(bf16[128,768]{1,0:T(8,128)(2,1)S(1)} %collective-permute-done.13.refs_10_) | copy-start | bytes 589828
  49.5 8.7 %collective-permute-start.12 = (bf16[128,768]{1,0:T(8,128)(2,1)S(1)}, bf16[128,768]{1,0:T(8,128)(2,1)S(1)}, u32[]{:S(2)}, u32[]{:S(2)}) collective-permute-start(bf16[128,768]{1,0:T(8,128)(2,1)S(1)} %collective-permute-done.11.refs_8_), channel_id=1, source_target_pairs={{0,1},{1,2},{2,3},{3,0},{4,5},{5,6},{6,7},{7,4},{8,9},{9,10},{10,1... | collective-permute-start | bytes 589832 | tf_op jit(solution)/shard_map/ppermute | solution.py:46
  50.0 18.7 %copy-start.5 = (bf16[128,2048]{1,0:T(8,128)(2,1)}, bf16[128,2048]{1,0:T(8,128)(2,1)S(1)}, u32[]{:S(2)}) copy-start(bf16[128,2048]{1,0:T(8,128)(2,1)S(1)} %collective-permute-done.2.refs_3_) | copy-start | bytes 1572868
  50.0 16.0 %collective-permute-start.6 = (bf16[128,2048]{1,0:T(8,128)(2,1)S(1)}, bf16[128,2048]{1,0:T(8,128)(2,1)S(1)}, u32[]{:S(2)}, u32[]{:S(2)}) collective-permute-start(bf16[128,2048]{1,0:T(8,128)(2,1)S(1)} %collective-permute-done.2.refs_3_), channel_id=1, source_target_pairs={{0,8},{1,9},{2,10},{3,11},{4,12},{5,13},{6,14},{7,15},{8,0},{9,1},... | collective-permute-start | bytes 1572872 | tf_op jit(solution)/shard_map/ppermute | solution.py:46
  51.7 17.0 %copy-start.6 = (bf16[128,2048]{1,0:T(8,128)(2,1)}, bf16[128,2048]{1,0:T(8,128)(2,1)S(1)}, u32[]{:S(2)}) copy-start(bf16[128,2048]{1,0:T(8,128)(2,1)S(1)} %collective-permute-done.1.refs_2_) | copy-start | bytes 1572868
  51.7 14.5 %collective-permute-start.5 = (bf16[128,2048]{1,0:T(8,128)(2,1)S(1)}, bf16[128,2048]{1,0:T(8,128)(2,1)S(1)}, u32[]{:S(2)}, u32[]{:S(2)}) collective-permute-start(bf16[128,2048]{1,0:T(8,128)(2,1)S(1)} %collective-permute-done.1.refs_2_), channel_id=1, source_target_pairs={{0,8},{1,9},{2,10},{3,11},{4,12},{5,13},{6,14},{7,15},{8,0},{9,1},... | collective-permute-start | bytes 1572872 | tf_op jit(solution)/shard_map/ppermute | solution.py:46
  51.8 16.9 %copy-start.7 = (bf16[128,2048]{1,0:T(8,128)(2,1)}, bf16[128,2048]{1,0:T(8,128)(2,1)S(1)}, u32[]{:S(2)}) copy-start(bf16[128,2048]{1,0:T(8,128)(2,1)S(1)} %collective-permute-done.refs_1_) | copy-start | bytes 1572868
  51.8 17.0 %collective-permute-start.4 = (bf16[128,2048]{1,0:T(8,128)(2,1)S(1)}, bf16[128,2048]{1,0:T(8,128)(2,1)}, u32[]{:S(2)}, u32[]{:S(2)}) collective-permute-start(bf16[128,2048]{1,0:T(8,128)(2,1)S(1)} %collective-permute-done.refs_1_), channel_id=1, source_target_pairs={{0,8},{1,9},{2,10},{3,11},{4,12},{5,13},{6,14},{7,15},{8,0},{9,1},... | collective-permute-start | bytes 1572872 | tf_op jit(solution)/shard_map/ppermute | solution.py:46
  58.2 10.5 %copy-start.17 = (bf16[128,768]{1,0:T(8,128)(2,1)}, bf16[128,768]{1,0:T(8,128)(2,1)S(1)}, u32[]{:S(2)}) copy-start(bf16[128,768]{1,0:T(8,128)(2,1)S(1)} %collective-permute-done.12.refs_9_) | copy-start | bytes 589828
  58.2 1.6 %collective-permute-start.18 = (bf16[128,768]{1,0:T(8,128)(2,1)S(1)}, bf16[128,768]{1,0:T(8,128)(2,1)S(1)}, u32[]{:S(2)}, u32[]{:S(2)}) collective-permute-start(bf16[128,768]{1,0:T(8,128)(2,1)S(1)} %collective-permute-done.14.refs_11_), channel_id=1, source_target_pairs={{0,8},{1,9},{2,10},{3,11},{4,12},{5,13},{6,14},{7,15},{8,0},{9,1},... | collective-permute-start | bytes 589832 | tf_op jit(solution)/shard_map/ppermute | solution.py:46
  58.7 0.8 copy-start.8
  59.5 3.7 %collective-permute-start.17 = (bf16[128,768]{1,0:T(8,128)(2,1)S(1)}, bf16[128,768]{1,0:T(8,128)(2,1)S(1)}, u32[]{:S(2)}, u32[]{:S(2)}) collective-permute-start(bf16[128,768]{1,0:T(8,128)(2,1)S(1)} %collective-permute-done.13.refs_10_), channel_id=1, source_target_pairs={{0,8},{1,9},{2,10},{3,11},{4,12},{5,13},{6,14},{7,15},{8,0},{9,1},... | collective-permute-start | bytes 589832 | tf_op jit(solution)/shard_map/ppermute | solution.py:46
  59.8 0.7 copy-start.18
  60.5 2.9 %collective-permute-start.16 = (bf16[128,768]{1,0:T(8,128)(2,1)S(1)}, bf16[128,768]{1,0:T(8,128)(2,1)S(1)}, u32[]{:S(2)}, u32[]{:S(2)}) collective-permute-start(bf16[128,768]{1,0:T(8,128)(2,1)S(1)} %collective-permute-done.12.refs_9_), channel_id=1, source_target_pairs={{0,8},{1,9},{2,10},{3,11},{4,12},{5,13},{6,14},{7,15},{8,0},{9,1},... | collective-permute-start | bytes 589832 | tf_op jit(solution)/shard_map/ppermute | solution.py:46
  63.2 5.5 %copy-start.19 = (bf16[128,768]{1,0:T(8,128)(2,1)}, bf16[128,768]{1,0:T(8,128)(2,1)S(1)}, u32[]{:S(2)}) copy-start(bf16[128,768]{1,0:T(8,128)(2,1)S(1)} %collective-permute-done.17.refs_14_) | copy-start | bytes 589828
  63.2 15.7 %collective-permute-start.7 = (bf16[128,1280]{1,0:T(8,128)(2,1)}, bf16[128,1280]{1,0:T(8,128)(2,1)}, u32[]{:S(2)}, u32[]{:S(2)}) collective-permute-start(bf16[128,1280]{1,0:T(8,128)(2,1)} %slice.20), channel_id=1, source_target_pairs={{0,132},{1,133},{2,134},{3,135},{4,128},{5,129},{6,130},{7,131},{8... | collective-permute-start | bytes 983048 | tf_op jit(solution)/shard_map/ppermute | solution.py:46
  63.4 5.3 %copy-start.20 = (bf16[128,768]{1,0:T(8,128)(2,1)}, bf16[128,768]{1,0:T(8,128)(2,1)S(1)}, u32[]{:S(2)}) copy-start(bf16[128,768]{1,0:T(8,128)(2,1)S(1)} %collective-permute-done.16.refs_13_) | copy-start | bytes 589828
  63.4 17.6 %collective-permute-start.10 = (bf16[128,1280]{1,0:T(8,128)(2,1)}, bf16[128,1280]{1,0:T(8,128)(2,1)}, u32[]{:S(2)}, u32[]{:S(2)}) collective-permute-start(bf16[128,1280]{1,0:T(8,128)(2,1)} %slice.23), channel_id=1, source_target_pairs={{0,132},{1,133},{2,134},{3,135},{4,128},{5,129},{6,130},{7,131},{8... | collective-permute-start | bytes 983048 | tf_op jit(solution)/shard_map/ppermute | solution.py:46
  66.0 2.7 %copy-start.9 = (bf16[128,2048]{1,0:T(8,128)(2,1)}, bf16[128,2048]{1,0:T(8,128)(2,1)S(1)}, u32[]{:S(2)}) copy-start(bf16[128,2048]{1,0:T(8,128)(2,1)S(1)} %collective-permute-done.6.refs_7_) | copy-start | bytes 1572868
  66.0 22.1 %collective-permute-start.9 = (bf16[128,1280]{1,0:T(8,128)(2,1)}, bf16[128,1280]{1,0:T(8,128)(2,1)}, u32[]{:S(2)}, u32[]{:S(2)}) collective-permute-start(bf16[128,1280]{1,0:T(8,128)(2,1)} %slice.22), channel_id=1, source_target_pairs={{0,132},{1,133},{2,134},{3,135},{4,128},{5,129},{6,130},{7,131},{8... | collective-permute-start | bytes 983048 | tf_op jit(solution)/shard_map/ppermute | solution.py:46
  66.1 2.6 %copy-start.10 = (bf16[128,2048]{1,0:T(8,128)(2,1)}, bf16[128,2048]{1,0:T(8,128)(2,1)S(1)}, u32[]{:S(2)}) copy-start(bf16[128,2048]{1,0:T(8,128)(2,1)S(1)} %collective-permute-done.5.refs_6_) | copy-start | bytes 1572868
  66.1 29.0 %collective-permute-start.8 = (bf16[128,1280]{1,0:T(8,128)(2,1)S(1)}, bf16[128,1280]{1,0:T(8,128)(2,1)}, u32[]{:S(2)}, u32[]{:S(2)}) collective-permute-start(bf16[128,1280]{1,0:T(8,128)(2,1)S(1)} %slice.21), channel_id=1, source_target_pairs={{0,132},{1,133},{2,134},{3,135},{4,128},{5,129},{6,130},{7,131},{8... | collective-permute-start | bytes 983048 | tf_op jit(solution)/shard_map/ppermute | solution.py:46
  95.1 34.8 %all-to-all-start.1 = ((bf16[32,32,512]{2,1,0:T(8,128)(2,1)}), bf16[32,32,512]{2,1,0:T(8,128)(2,1)}, u32[]{:S(2)}, u32[]{:S(2)}) async-start(bf16[32,32,512]{2,1,0:T(8,128)(2,1)} %col_heads.1), calls=%async_computation.1 | async-start | bytes 2097152 | tf_op jit(solution)/shard_map/all_to_all | solution.py:411
  102.9 1.9 %collective-permute-start.19 = (bf16[128,1280]{1,0:T(8,128)(2,1)}, bf16[128,1280]{1,0:T(8,128)(2,1)S(1)}, u32[]{:S(2)}, u32[]{:S(2)}) collective-permute-start(bf16[128,1280]{1,0:T(8,128)(2,1)} %collective-permute-done.7.refs_8_), channel_id=1, source_target_pairs={{0,8},{1,9},{2,10},{3,11},{4,12},{5,13},{6,14},{7,15},{8,0},{9,1},... | collective-permute-start | bytes 983048 | tf_op jit(solution)/shard_map/ppermute | solution.py:46
  103.3 2.0 %collective-permute-start.20 = (bf16[128,1280]{1,0:T(8,128)(2,1)}, bf16[128,1280]{1,0:T(8,128)(2,1)S(1)}, u32[]{:S(2)}, u32[]{:S(2)}) collective-permute-start(bf16[128,1280]{1,0:T(8,128)(2,1)} %collective-permute-done.8.refs_9_), channel_id=1, source_target_pairs={{0,8},{1,9},{2,10},{3,11},{4,12},{5,13},{6,14},{7,15},{8,0},{9,1},... | collective-permute-start | bytes 983048 | tf_op jit(solution)/shard_map/ppermute | solution.py:46
  103.5 2.4 %collective-permute-start.21 = (bf16[128,1280]{1,0:T(8,128)(2,1)}, bf16[128,1280]{1,0:T(8,128)(2,1)}, u32[]{:S(2)}, u32[]{:S(2)}) collective-permute-start(bf16[128,1280]{1,0:T(8,128)(2,1)} %collective-permute-done.9.refs_10_), channel_id=1, source_target_pairs={{0,8},{1,9},{2,10},{3,11},{4,12},{5,13},{6,14},{7,15},{8,0},{9,1},... | collective-permute-start | bytes 983048 | tf_op jit(solution)/shard_map/ppermute | solution.py:46
  103.8 2.6 %collective-permute-start.22 = (bf16[128,1280]{1,0:T(8,128)(2,1)}, bf16[128,1280]{1,0:T(8,128)(2,1)}, u32[]{:S(2)}, u32[]{:S(2)}) collective-permute-start(bf16[128,1280]{1,0:T(8,128)(2,1)} %collective-permute-done.10.refs_11_), channel_id=1, source_target_pairs={{0,8},{1,9},{2,10},{3,11},{4,12},{5,13},{6,14},{7,15},{8,0},{9,1},... | collective-permute-start | bytes 983048 | tf_op jit(solution)/shard_map/ppermute | solution.py:46
  104.8 1.5 %copy-start.11 = (bf16[128,1280]{1,0:T(8,128)(2,1)}, bf16[128,1280]{1,0:T(8,128)(2,1)S(1)}, u32[]{:S(2)}) copy-start(bf16[128,1280]{1,0:T(8,128)(2,1)S(1)} %collective-permute-done.19.refs_12_) | copy-start | bytes 983044
  105.3 1.1 copy-start.12

commit v5 on v3

--- a/solution.py
+++ b/solution.py
@@ -14,7 +14,7 @@
 HEAD_DIM = D // HEADS
 HALF = D // 2
 PAIR = 2 * HEAD_DIM
-COLS, REST = 768, 1280
+QKV, OUT = 768, 512
 F32, BF16 = jnp.float32, jnp.bfloat16
 LOG2_SCALE = math.log2(math.e) / math.sqrt(HEAD_DIM)
 BOTH = ("seq", "fsdp")
@@ -51,7 +51,7 @@
     return (rows * lax.rsqrt(mean_square + 1e-06)).astype(BF16)
 
 
-def fetch_weights(slabs, first, width, dest, sems):
+def fetch_weights(slabs, dest, sems):
     core = lax.axis_index("seq") % 2
     mine = lax.axis_index("fsdp")
     copies = []
@@ -61,7 +61,7 @@
             y_hi = mine // 4 if k == 0 else 1 - mine // 4
             feature = pl.multiple_of((y_hi * 4 + (mine % 4 - n % 4 + 4) % 4) * 128, 128)
             copy = pltpu.make_async_copy(
-                slab.at[k, :, pl.ds(first, width)],
+                slab.at[k],
                 dest.at[half, pl.ds(feature, 128), :],
                 sems.at[n * 2 + k],
             )
@@ -139,9 +139,8 @@
 
 def row_kernel(x_ref, *refs):
     slabs = refs[:8]
-    part_hbm, wc_hbm, w, wo, qkv, attended, mask_ref, part, sems, sems_o, sems_part = refs[8:]
-    copies = fetch_weights(slabs, 0, 768, w, sems)
-    copies_out = fetch_weights(slabs, 768, 512, wo, sems_o)
+    o_hbm, w, qkv, attended, mask_ref, sems, sems_o = refs[8:]
+    copies = fetch_weights(slabs, w, sems)
     block = 256
     row = lax.broadcasted_iota(jnp.int32, (block, block), 0)
     col = lax.broadcasted_iota(jnp.int32, (block, block), 1)
@@ -171,21 +170,9 @@
                 qkv[2, p, :upto, :],
                 mask_ref[...],
             )
-    for copy in copies_out:
-        copy.wait()
-
-    copies = [pltpu.make_async_copy(wo.at[:, pl.ds(HALF, HALF), :], wc_hbm, sems.at[0])]
-    copies[0].start()
-    for i in range(STRIDE // block):
-        at = slice(i * block, (i + 1) * block)
-        for half in range(2):
-            part[at, half * 512 : (half + 1) * 512] = jnp.dot(
-                attended[at, :], wo[half, :HALF, :], preferred_element_type=F32
-            )
-        copies.append(pltpu.make_async_copy(part.at[at, :], part_hbm.at[at, :], sems_part.at[i]))
-        copies[-1].start()
-    for copy in copies:
-        copy.wait()
+    copy = pltpu.make_async_copy(attended, o_hbm, sems_o.at[0])
+    copy.start()
+    copy.wait()
 
 
 def sequence_row(place):
@@ -218,7 +205,7 @@
         arrive.append(pltpu.make_async_copy(x_hbm.at[:, at, :], x.at[:, at, :], sems_x.at[i]))
         leave.append(pltpu.make_async_copy(out.at[:, at, :], o_hbm.at[:, at, :], sems_o.at[i]))
         arrive[i].start()
-    weights = fetch_weights(refs[:8], 0, 768, w, sems)
+    weights = fetch_weights(refs[:8], w, sems)
     at = lax.broadcasted_iota(jnp.int32, (128, 128), 0)
     to = lax.broadcasted_iota(jnp.int32, (128, 128), 1)
     meets = jnp.logical_and(at // 32 == to // 32, to <= at)
@@ -269,29 +256,28 @@
         copy.wait()
 
 
-def out_kernel(part_hbm, col_hbm, w_hbm, o_hbm, part, col, w, out, sem_w, sems_p, sems_c, sems_o):
+def out_kernel(row_hbm, col_hbm, *refs):
+    o_hbm, row, col, w, out, sems, sems_r, sems_c, sems_o = refs[8:]
     block = 256
-    weights = pltpu.make_async_copy(w_hbm, w, sem_w.at[0])
-    weights.start()
-    parts, cols, outs = [], [], []
+    weights = fetch_weights(refs[:8], w, sems)
+    rows, cols, outs = [], [], []
     for i in range(STRIDE // block):
         at = pl.ds(i * block, block)
-        parts.append(pltpu.make_async_copy(part_hbm.at[at, :], part.at[at, :], sems_p.at[i]))
+        rows.append(pltpu.make_async_copy(row_hbm.at[at, :], row.at[at, :], sems_r.at[i]))
         cols.append(pltpu.make_async_copy(col_hbm.at[at, :], col.at[at, :], sems_c.at[i]))
         outs.append(pltpu.make_async_copy(out.at[at, :], o_hbm.at[at, :], sems_o.at[i]))
+        rows[i].start()
         cols[i].start()
-        parts[i].start()
-    weights.wait()
+    for copy in weights:
+        copy.wait()
     for i in range(STRIDE // block):
         at = slice(i * block, (i + 1) * block)
+        rows[i].wait()
         cols[i].wait()
-        parts[i].wait()
         for half in range(2):
-            lanes = slice(half * 512, (half + 1) * 512)
-            total = part[at, lanes] + jnp.dot(
-                col[at, :], w[half], preferred_element_type=F32
-            )
-            out[at, lanes] = total.astype(BF16)
+            total = jnp.dot(row[at, :], w[half, :HALF, :], preferred_element_type=F32)
+            total += jnp.dot(col[at, :], w[half, HALF:, :], preferred_element_type=F32)
+            out[at, half * 512 : (half + 1) * 512] = total.astype(BF16)
         outs[i].start()
     for copy in outs:
         copy.wait()
@@ -311,7 +297,7 @@
     return pl.pallas_call(
         prep_kernel,
         out_shape=[
-            jax.ShapeDtypeStruct((parts[0].shape[0], width), BF16) for width in (COLS, REST)
+            jax.ShapeDtypeStruct((parts[0].shape[0], width), BF16) for width in (QKV, QKV + OUT)
         ],
         in_specs=[pl.BlockSpec(memory_space=pltpu.SMEM)] + [WHOLE] * 4,
         out_specs=[WHOLE] * 2,
@@ -323,26 +309,20 @@
 def row_heads(sequence, slabs):
     return pl.pallas_call(
         row_kernel,
-        out_shape=(
-            jax.ShapeDtypeStruct((STRIDE, D), F32),
-            jax.ShapeDtypeStruct((2, HALF, 512), BF16),
-        ),
+        out_shape=jax.ShapeDtypeStruct((STRIDE, HALF), BF16),
         in_specs=[WHOLE] + [ANY] * 8,
-        out_specs=(FAR, FAR),
+        out_specs=FAR,
         scratch_shapes=[
-            pltpu.VMEM((2, D, 768), BF16),
-            pltpu.VMEM((2, D, 512), BF16),
+            pltpu.VMEM((2, D, QKV), BF16),
             pltpu.VMEM((3, 4, STRIDE, PAIR), BF16),
             pltpu.VMEM((STRIDE, HALF), BF16),
             pltpu.VMEM((256, 256), F32),
-            pltpu.VMEM((STRIDE, D), F32),
             DMA((16,)),
-            DMA((16,)),
-            DMA((4,)),
+            DMA((1,)),
         ],
         compiler_params=limit(63),
         cost_estimate=pl.CostEstimate(
-            flops=7_000_000_000, bytes_accessed=12 << 20, transcendentals=5_000_000
+            flops=6_000_000_000, bytes_accessed=6 << 20, transcendentals=5_000_000
         ),
         name="row_heads",
     )(sequence, *slabs)
@@ -357,7 +337,7 @@
         out_specs=FAR,
         scratch_shapes=[
             pltpu.VMEM((rows, cols, D), BF16),
-            pltpu.VMEM((2, D, 768), BF16),
+            pltpu.VMEM((2, D, QKV), BF16),
             pltpu.VMEM((rows, cols, HALF), BF16),
             pltpu.VMEM((128, 128), F32),
             pltpu.VMEM((STEP, STEP), BF16),
@@ -375,28 +355,28 @@
     )(columns, *slabs)
 
 
-def project_out(row_part, col_out, weights):
+def project_out(row_out, col_out, slabs):
     return pl.pallas_call(
         out_kernel,
         out_shape=jax.ShapeDtypeStruct((STRIDE, D), BF16),
-        in_specs=[FAR] * 3,
+        in_specs=[FAR] * 2 + [ANY] * 8,
         out_specs=FAR,
         scratch_shapes=[
-            pltpu.VMEM((STRIDE, D), F32),
             pltpu.VMEM((STRIDE, HALF), BF16),
-            pltpu.VMEM((2, HALF, 512), BF16),
+            pltpu.VMEM((STRIDE, HALF), BF16),
+            pltpu.VMEM((2, D, OUT), BF16),
             pltpu.VMEM((STRIDE, D), BF16),
-            DMA((1,)),
+            DMA((16,)),
             DMA((4,)),
             DMA((4,)),
             DMA((4,)),
         ],
         compiler_params=limit(63),
         cost_estimate=pl.CostEstimate(
-            flops=1_000_000_000, bytes_accessed=8 << 20, transcendentals=0
+            flops=2_000_000_000, bytes_accessed=6 << 20, transcendentals=0
         ),
         name="project_out",
-    )(row_part, col_out, weights)
+    )(row_out, col_out, *slabs)
 
 
 ORDER = [sequence_row(place) for place in range(32)]
@@ -425,13 +405,15 @@
     columns = exchange(sequence.reshape(32, 32, D))
     own_cols, own_rest = rebuilt_half(alpha_index, qkv_base, qkv_dir, out_base, out_dir)
     col_pieces = along_x(with_far_y(own_cols))
-    rest_both, col_pieces = lax.optimization_barrier((with_far_y(own_rest), col_pieces))
-    rest_pieces = along_x(rest_both)
+    rest, col_pieces = lax.optimization_barrier((with_far_y(own_rest), col_pieces))
+    row_pieces = along_x(rest[:, :, :QKV])
     attended = col_heads(columns, both_cores(col_pieces))
+    row_pieces, rest, attended = lax.optimization_barrier((row_pieces, rest, attended))
     col_out = exchange(attended)
-    rest_pieces, attended = lax.optimization_barrier((rest_pieces, attended))
-    row_part, weights = row_heads(sequence, both_cores(rest_pieces))
-    return project_out(row_part, col_out.reshape(STRIDE, HALF), weights)[None]
+    out_pieces = along_x(rest[:, :, QKV:])
+    row_out = row_heads(sequence, both_cores(row_pieces))
+    out_pieces, row_out = lax.optimization_barrier((out_pieces, row_out))
+    return project_out(row_out, col_out.reshape(STRIDE, HALF), both_cores(out_pieces))[None]
 
 
 def solution(mesh):

time: 143 us -> 113 us (0.79)
  waiting for transfers between devices: 75 us -> 34.2 us
  starting transfers between devices: 29.3 us -> 39.1 us
  local copies, waits for them, and re-layouts: 1.65 us -> 3.13 us
    ppermute x16 -> x23, waiting for transfers between devices: 62.2 us -> 22 us  [send(): return lax.ppermute(value, BOTH, where)]
    ppermute x16 -> x23, starting transfers between devices: 12.5 us -> 22.6 us  [send(): return lax.ppermute(value, BOTH, where)]
    pallas_call x1, Pallas kernels: 19.9 us -> 17.8 us  [row_heads(): pl.pallas_call(row_kernel, out_shape=jax.ShapeDtypeStruct((STRIDE, HALF),...]
  transfers between devices with their start and end apart: 18 -> 25, of which waited for: 15 -> 9; matrix products, arithmetic and copies ran while one was open for 0% -> 1% of each run, Pallas kernels for 14% -> 26%
where the time goes in v5:
time: 113 us; the launch traced here: 112 us
  starting transfers between devices  39.1 us (35%)
  Pallas kernels  34.7 us (31%)
  waiting for transfers between devices  34.2 us (30%)
  local copies, waits for them, and re-layouts  3.13 us (3%)
    ppermute x23, starting transfers between devices, send(): return lax.ppermute(value, BOTH, where)  22.6 us
    ppermute x23, waiting for transfers between devices, send(): return lax.ppermute(value, BOTH, where)  22 us
    pallas_call x1, Pallas kernels, row_heads(): pl.pallas_call(row_kernel, out_shape=jax.ShapeDtypeStruct((STRIDE, HALF),...  17.8 us
    all_to_all x2, starting transfers between devices, exchange(): lax.all_to_all(blocks, 'seq', split_axis=0, concat_axis=0, tiled=True, ax...  16.5 us
    all_to_all x2, waiting for transfers between devices, exchange(): lax.all_to_all(blocks, 'seq', split_axis=0, concat_axis=0, tiled=True, ax...  12.2 us
    pallas_call x1, Pallas kernels, col_heads(): pl.pallas_call(col_kernel, out_shape=jax.ShapeDtypeStruct((rows, cols, HA...  10.7 us
    pallas_call x1, Pallas kernels, project_out(): pl.pallas_call(out_kernel, out_shape=jax.ShapeDtypeStruct((STRIDE, D), BF...  5.99 us
    unnamed x38, local copies, waits for them, and re-layouts  2.31 us
  transfers between devices with their start and end apart: 25, of which 9 were waited for; matrix products, arithmetic and copies ran while one was open for 1% of the time, Pallas kernels for 26%

profile of v5, /device:TPU:1, one launch (start us, length us, event | category | flops | bytes accessed | tf_op | source)
XLA Modules:
  0.0 112.2 jit_solution(650110592749213826)
XLA Ops:
  0.0 11.3 %all-to-all-start = ((bf16[32,32,1024]{2,1,0:T(8,128)(2,1)}), bf16[32,32,1024]{2,1,0:T(8,128)(2,1)}, u32[]{:S(2)}, u32[]{:S(2)}) async-start(bf16[32,32,1024]{2,1,0:T(8,128)(2,1)} %bitcast.10), calls=%async_computation | async-start | bytes 4194304 | tf_op jit(solution)/shard_map/all_to_all | solution.py:386
  12.0 0.2 rebuilt_half.1
  12.2 2.9 %collective-permute-start.1 = (bf16[128,768]{1,0:T(8,128)(2,1)S(1)}, bf16[128,768]{1,0:T(8,128)(2,1)S(1)}, u32[]{:S(2)}, u32[]{:S(2)}) collective-permute-start(bf16[128,768]{1,0:T(8,128)(2,1)S(1)} %get-tuple-element.24), channel_id=1, source_target_pairs={{0,132},{1,133},{2,134},{3,135},{4,128},{5,129},{6,130},{7,131},{8... | collective-permute-start | bytes 589832 | tf_op jit(solution)/shard_map/ppermute | solution.py:46
  15.1 0.1 collective-permute-start
  15.2 4.9 %collective-permute-done.1 = bf16[128,768]{1,0:T(8,128)(2,1)S(1)} collective-permute-done((bf16[128,768]{1,0:T(8,128)(2,1)S(1)}, bf16[128,768]{1,0:T(8,128)(2,1)S(1)}, u32[]{:S(2)}, u32[]{:S(2)}) %collective-permute-start.1) | collective-permute-done | bytes 196640 | tf_op jit(solution)/shard_map/ppermute | solution.py:46
  20.2 1.3 %collective-permute-start.2 = (bf16[2,128,768]{2,1,0:T(8,128)(2,1)S(1)}, bf16[2,128,768]{2,1,0:T(8,128)(2,1)S(1)}, u32[]{:S(2)}, u32[]{:S(2)}) collective-permute-start(bf16[2,128,768]{2,1,0:T(8,128)(2,1)S(1)} %pad_maximum_fusion.1.refs_0_), channel_id=1, source_target_pairs={{0,1},{1,2},{2,3},{3,0},{4,5},{5,6},{6,7},{7,4},{8,9},{9,10},{10,1... | collective-permute-start | bytes 1179656 | tf_op jit(solution)/shard_map/ppermute | solution.py:46
  21.5 2.5 %collective-permute-start.3 = (bf16[2,128,768]{2,1,0:T(8,128)(2,1)S(1)}, bf16[2,128,768]{2,1,0:T(8,128)(2,1)S(1)}, u32[]{:S(2)}, u32[]{:S(2)}) collective-permute-start(bf16[2,128,768]{2,1,0:T(8,128)(2,1)S(1)} %pad_maximum_fusion.1.refs_0_), channel_id=1, source_target_pairs={{0,2},{1,3},{2,0},{3,1},{4,6},{5,7},{6,4},{7,5},{8,10},{9,11},{10,... | collective-permute-start | bytes 1179656 | tf_op jit(solution)/shard_map/ppermute | solution.py:46
  23.9 1.2 %collective-permute-start.4 = (bf16[2,128,768]{2,1,0:T(8,128)(2,1)S(1)}, bf16[2,128,768]{2,1,0:T(8,128)(2,1)S(1)}, u32[]{:S(2)}, u32[]{:S(2)}) collective-permute-start(bf16[2,128,768]{2,1,0:T(8,128)(2,1)S(1)} %pad_maximum_fusion.1.refs_0_), channel_id=1, source_target_pairs={{0,3},{1,0},{2,1},{3,2},{4,7},{5,4},{6,5},{7,6},{8,11},{9,8},{10,9... | collective-permute-start | bytes 1179656 | tf_op jit(solution)/shard_map/ppermute | solution.py:46
  25.1 2.1 %collective-permute-done = bf16[128,1280]{1,0:T(8,128)(2,1)S(1)} collective-permute-done((bf16[128,1280]{1,0:T(8,128)(2,1)S(1)}, bf16[128,1280]{1,0:T(8,128)(2,1)S(1)}, u32[]{:S(2)}, u32[]{:S(2)}) %collective-permute-start) | collective-permute-done | bytes 327712 | tf_op jit(solution)/shard_map/ppermute | solution.py:46
  27.2 0.1 pad_maximum_fusion
  27.2 3.6 %collective-permute-done.2.refs_1_ = bf16[2,128,768]{2,1,0:T(8,128)(2,1)S(1)} collective-permute-done((bf16[2,128,768]{2,1,0:T(8,128)(2,1)S(1)}, bf16[2,128,768]{2,1,0:T(8,128)(2,1)S(1)}, u32[]{:S(2)}, u32[]{:S(2)}) %collective-permute-start.2) | collective-permute-done | bytes 393248 | tf_op jit(solution)/shard_map/ppermute | solution.py:46
  30.8 9.4 %collective-permute-done.3.refs_2_ = bf16[2,128,768]{2,1,0:T(8,128)(2,1)S(1)} collective-permute-done((bf16[2,128,768]{2,1,0:T(8,128)(2,1)S(1)}, bf16[2,128,768]{2,1,0:T(8,128)(2,1)S(1)}, u32[]{:S(2)}, u32[]{:S(2)}) %collective-permute-start.3) | collective-permute-done | bytes 393248 | tf_op jit(solution)/shard_map/ppermute | solution.py:46
  40.2 0.3 collective-permute-done.4.refs_3_
  40.5 2.0 %collective-permute-start.10 = (bf16[2,128,768]{2,1,0:T(8,128)(2,1)S(1)}, bf16[2,128,768]{2,1,0:T(8,128)(2,1)S(1)}, u32[]{:S(2)}, u32[]{:S(2)}) collective-permute-start(bf16[2,128,768]{2,1,0:T(8,128)(2,1)S(1)} %collective-permute-done.3.refs_2_), channel_id=1, source_target_pairs={{0,8},{1,9},{2,10},{3,11},{4,12},{5,13},{6,14},{7,15},{8,0},{9,1},... | collective-permute-start | bytes 1179656 | tf_op jit(solution)/shard_map/ppermute | solution.py:46
  42.5 0.1 collective-permute-start.11
  42.6 0.4 collective-permute-start.8
  43.0 0.1 collective-permute-start.9
  43.1 0.8 slice.6.refs_0_
  43.9 0.9 collective-permute-start.5
  44.8 0.0 collective-permute-done.10.refs_6_
  44.8 2.2 %collective-permute-start.6 = (bf16[2,128,768]{2,1,0:T(8,128)(2,1)}, bf16[2,128,768]{2,1,0:T(8,128)(2,1)}, u32[]{:S(2)}, u32[]{:S(2)}) collective-permute-start(bf16[2,128,768]{2,1,0:T(8,128)(2,1)} %slice.6.refs_0_), channel_id=1, source_target_pairs={{0,2},{1,3},{2,0},{3,1},{4,6},{5,7},{6,4},{7,5},{8,10},{9,11},{10,... | collective-permute-start | bytes 1179656 | tf_op jit(solution)/shard_map/ppermute | solution.py:46
  47.0 0.0 collective-permute-done.11.refs_7_
  47.0 1.2 %collective-permute-start.7 = (bf16[2,128,768]{2,1,0:T(8,128)(2,1)}, bf16[2,128,768]{2,1,0:T(8,128)(2,1)}, u32[]{:S(2)}, u32[]{:S(2)}) collective-permute-start(bf16[2,128,768]{2,1,0:T(8,128)(2,1)} %slice.6.refs_0_), channel_id=1, source_target_pairs={{0,3},{1,0},{2,1},{3,2},{4,7},{5,4},{6,5},{7,6},{8,11},{9,8},{10,9... | collective-permute-start | bytes 1179656 | tf_op jit(solution)/shard_map/ppermute | solution.py:46
  48.3 0.7 copy-done.12
  49.0 12.2 %all-to-all-done.x_hbm = bf16[32,32,1024]{2,1,0:T(8,128)(2,1)} async-done(((bf16[32,32,1024]{2,1,0:T(8,128)(2,1)}), bf16[32,32,1024]{2,1,0:T(8,128)(2,1)}, u32[]{:S(2)}, u32[]{:S(2)}) %all-to-all-start) | async-done | bytes 2097184 | tf_op jit(solution)/shard_map/all_to_all | solution.py:386
  61.2 10.7 %col_heads.1 = bf16[32,32,512]{2,1,0:T(8,128)(2,1)} custom-call(bf16[32,32,1024]{2,1,0:T(8,128)(2,1)} %all-to-all-done.x_hbm, bf16[2,128,768]{2,1,0:T(8,128)(2,1)} %copy-done.4, bf16[2,128,768]{2,1,0:T(8,128)(2,1)} %copy-done.6, bf16[2,128,768]{2,1,0:T(8,128)(2,1)} %copy-done.7, bf16[2,128,768]{2,1,0:T(8,128)(2,1)} %copy-done.8, ...), custom_call_target="tpu_custom_call" | custom-call | flops 4000000000 | bytes 6291456 | tf_op jit(solution)/shard_map/col_heads/pallas_call | solution.py:333
  71.9 0.0 collective-permute-done.5.refs_1_
  71.9 0.0 collective-permute-done.6.refs_2_
  72.0 5.1 %all-to-all-start.1 = ((bf16[32,32,512]{2,1,0:T(8,128)(2,1)}), bf16[32,32,512]{2,1,0:T(8,128)(2,1)}, u32[]{:S(2)}, u32[]{:S(2)}) async-start(bf16[32,32,512]{2,1,0:T(8,128)(2,1)} %col_heads.1), calls=%async_computation.1 | async-start | bytes 2097152 | tf_op jit(solution)/shard_map/all_to_all | solution.py:386
  77.1 0.4 collective-permute-start.15
  77.5 0.2 collective-permute-start.16
  77.7 0.3 collective-permute-start.17
  78.0 0.2 collective-permute-start.18
  78.3 1.3 %collective-permute-start.12 = (bf16[2,128,512]{2,1,0:T(8,128)(2,1)S(1)}, bf16[2,128,512]{2,1,0:T(8,128)(2,1)S(1)}, u32[]{:S(2)}, u32[]{:S(2)}) collective-permute-start(bf16[2,128,512]{2,1,0:T(8,128)(2,1)S(1)} %slice.7.refs_0_), channel_id=1, source_target_pairs={{0,1},{1,2},{2,3},{3,0},{4,5},{5,6},{6,7},{7,4},{8,9},{9,10},{10,1... | collective-permute-start | bytes 786440 | tf_op jit(solution)/shard_map/ppermute | solution.py:46
  79.6 2.4 %collective-permute-start.13 = (bf16[2,128,512]{2,1,0:T(8,128)(2,1)S(1)}, bf16[2,128,512]{2,1,0:T(8,128)(2,1)S(1)}, u32[]{:S(2)}, u32[]{:S(2)}) collective-permute-start(bf16[2,128,512]{2,1,0:T(8,128)(2,1)S(1)} %slice.7.refs_0_), channel_id=1, source_target_pairs={{0,2},{1,3},{2,0},{3,1},{4,6},{5,7},{6,4},{7,5},{8,10},{9,11},{10,... | collective-permute-start | bytes 786440 | tf_op jit(solution)/shard_map/ppermute | solution.py:46
  82.0 0.0 collective-permute-done.16.refs_5_
  82.0 0.8 copy-done.13
  82.8 1.2 %collective-permute-start.14 = (bf16[2,128,512]{2,1,0:T(8,128)(2,1)S(1)}, bf16[2,128,512]{2,1,0:T(8,128)(2,1)}, u32[]{:S(2)}, u32[]{:S(2)}) collective-permute-start(bf16[2,128,512]{2,1,0:T(8,128)(2,1)S(1)} %slice.7.refs_0_), channel_id=1, source_target_pairs={{0,3},{1,0},{2,1},{3,2},{4,7},{5,4},{6,5},{7,6},{8,11},{9,8},{10,9... | collective-permute-start | bytes 786440 | tf_op jit(solution)/shard_map/ppermute | solution.py:46
  83.9 17.8 %row_heads.1.row_hbm = bf16[1024,512]{1,0:T(8,128)(2,1)} custom-call(bf16[1024,1024]{1,0:T(8,128)(2,1)} %bitcast.11, bf16[2,128,768]{2,1,0:T(8,128)(2,1)} %slice.6.refs_0_, bf16[2,128,768]{2,1,0:T(8,128)(2,1)} %collective-permute-done.5.refs_1_, bf16[2,128,768]{2,1,0:T(8,128)(2,1)} %collective-permute-done.6.refs_2_, ...), custom_call_target="tpu_custom_call" | custom-call | flops 6000000000 | bytes 6291456 | tf_op jit(solution)/shard_map/row_heads/pallas_call | solution.py:310
  101.8 1.2 %collective-permute-start.19 = (bf16[2,128,512]{2,1,0:T(8,128)(2,1)S(1)}, bf16[2,128,512]{2,1,0:T(8,128)(2,1)S(1)}, u32[]{:S(2)}, u32[]{:S(2)}) collective-permute-start(bf16[2,128,512]{2,1,0:T(8,128)(2,1)S(1)} %slice.7.refs_0_), channel_id=1, source_target_pairs={{0,8},{1,9},{2,10},{3,11},{4,12},{5,13},{6,14},{7,15},{8,0},{9,1},... | collective-permute-start | bytes 786440 | tf_op jit(solution)/shard_map/ppermute | solution.py:46
  103.0 0.1 collective-permute-start.20
  103.1 0.4 collective-permute-start.21
  103.5 0.1 collective-permute-start.22
  103.6 0.6 collective-permute-done.19.refs_4_
  104.2 0.4 collective-permute-done.20.refs_5_
  104.6 0.7 collective-permute-done.21.refs_6_
  105.3 0.7 copy-done.18
  106.1 6.0 %project_out.1 = bf16[1024,1024]{1,0:T(8,128)(2,1)} custom-call(bf16[1024,512]{1,0:T(8,128)(2,1)} %row_heads.1.row_hbm, bf16[1024,512]{1,0:T(8,128)(2,1)} %bitcast.6.col_hbm, bf16[2,128,512]{2,1,0:T(8,128)(2,1)} %copy-done.5, bf16[2,128,512]{2,1,0:T(8,128)(2,1)} %copy-done.14, bf16[2,128,512]{2,1,0:T(8,128)(2,1)} %copy-done.15, ...), custom_call_target="tpu_custom_call" | custom-call | flops 2000000000 | bytes 6291456 | tf_op jit(solution)/shard_map/project_out/pallas_call | solution.py:359
  (48 shorter events, 0.2 us)
Async XLA Ops:
  0.0 12.0 %copy-start = (bf16[128,3072]{1,0:T(8,128)(2,1)S(1)}, bf16[128,3072]{1,0:T(8,128)(2,1)}, u32[]{:S(2)}) copy-start(bf16[128,3072]{1,0:T(8,128)(2,1)} %qb_ref.1) | copy-start | bytes 2359300
  0.0 12.0 %copy-start.1 = (bf16[128,3072]{1,0:T(8,128)(2,1)S(1)}, bf16[128,3072]{1,0:T(8,128)(2,1)}, u32[]{:S(2)}) copy-start(bf16[128,3072]{1,0:T(8,128)(2,1)} %qd_ref.1) | copy-start | bytes 2359300
  0.0 12.0 %copy-start.2 = (bf16[128,1024]{1,0:T(8,128)(2,1)S(1)}, bf16[128,1024]{1,0:T(8,128)(2,1)}, u32[]{:S(2)}) copy-start(bf16[128,1024]{1,0:T(8,128)(2,1)} %ob_ref.1) | copy-start | bytes 786436
  0.0 12.0 %copy-start.3 = (bf16[128,1024]{1,0:T(8,128)(2,1)S(1)}, bf16[128,1024]{1,0:T(8,128)(2,1)}, u32[]{:S(2)}) copy-start(bf16[128,1024]{1,0:T(8,128)(2,1)} %od_ref.1) | copy-start | bytes 786436
  0.0 61.2 %all-to-all-start = ((bf16[32,32,1024]{2,1,0:T(8,128)(2,1)}), bf16[32,32,1024]{2,1,0:T(8,128)(2,1)}, u32[]{:S(2)}, u32[]{:S(2)}) async-start(bf16[32,32,1024]{2,1,0:T(8,128)(2,1)} %bitcast.10), calls=%async_computation | async-start | bytes 4194304 | tf_op jit(solution)/shard_map/all_to_all | solution.py:386
  12.2 7.9 %collective-permute-start.1 = (bf16[128,768]{1,0:T(8,128)(2,1)S(1)}, bf16[128,768]{1,0:T(8,128)(2,1)S(1)}, u32[]{:S(2)}, u32[]{:S(2)}) collective-permute-start(bf16[128,768]{1,0:T(8,128)(2,1)S(1)} %get-tuple-element.24), channel_id=1, source_target_pairs={{0,132},{1,133},{2,134},{3,135},{4,128},{5,129},{6,130},{7,131},{8... | collective-permute-start | bytes 589832 | tf_op jit(solution)/shard_map/ppermute | solution.py:46
  15.1 12.0 %collective-permute-start = (bf16[128,1280]{1,0:T(8,128)(2,1)S(1)}, bf16[128,1280]{1,0:T(8,128)(2,1)S(1)}, u32[]{:S(2)}, u32[]{:S(2)}) collective-permute-start(bf16[128,1280]{1,0:T(8,128)(2,1)S(1)} %get-tuple-element.23), channel_id=1, source_target_pairs={{0,132},{1,133},{2,134},{3,135},{4,128},{5,129},{6,130},{7,131},{8... | collective-permute-start | bytes 983048 | tf_op jit(solution)/shard_map/ppermute | solution.py:46
  20.2 22.4 %copy-start.4 = (bf16[2,128,768]{2,1,0:T(8,128)(2,1)}, bf16[2,128,768]{2,1,0:T(8,128)(2,1)S(1)}, u32[]{:S(2)}) copy-start(bf16[2,128,768]{2,1,0:T(8,128)(2,1)S(1)} %pad_maximum_fusion.1.refs_0_) | copy-start | bytes 1179652
  20.2 10.6 %collective-permute-start.2 = (bf16[2,128,768]{2,1,0:T(8,128)(2,1)S(1)}, bf16[2,128,768]{2,1,0:T(8,128)(2,1)S(1)}, u32[]{:S(2)}, u32[]{:S(2)}) collective-permute-start(bf16[2,128,768]{2,1,0:T(8,128)(2,1)S(1)} %pad_maximum_fusion.1.refs_0_), channel_id=1, source_target_pairs={{0,1},{1,2},{2,3},{3,0},{4,5},{5,6},{6,7},{7,4},{8,9},{9,10},{10,1... | collective-permute-start | bytes 1179656 | tf_op jit(solution)/shard_map/ppermute | solution.py:46
  21.5 18.7 %collective-permute-start.3 = (bf16[2,128,768]{2,1,0:T(8,128)(2,1)S(1)}, bf16[2,128,768]{2,1,0:T(8,128)(2,1)S(1)}, u32[]{:S(2)}, u32[]{:S(2)}) collective-permute-start(bf16[2,128,768]{2,1,0:T(8,128)(2,1)S(1)} %pad_maximum_fusion.1.refs_0_), channel_id=1, source_target_pairs={{0,2},{1,3},{2,0},{3,1},{4,6},{5,7},{6,4},{7,5},{8,10},{9,11},{10,... | collective-permute-start | bytes 1179656 | tf_op jit(solution)/shard_map/ppermute | solution.py:46
  23.9 16.6 %collective-permute-start.4 = (bf16[2,128,768]{2,1,0:T(8,128)(2,1)S(1)}, bf16[2,128,768]{2,1,0:T(8,128)(2,1)S(1)}, u32[]{:S(2)}, u32[]{:S(2)}) collective-permute-start(bf16[2,128,768]{2,1,0:T(8,128)(2,1)S(1)} %pad_maximum_fusion.1.refs_0_), channel_id=1, source_target_pairs={{0,3},{1,0},{2,1},{3,2},{4,7},{5,4},{6,5},{7,6},{8,11},{9,8},{10,9... | collective-permute-start | bytes 1179656 | tf_op jit(solution)/shard_map/ppermute | solution.py:46
  30.8 17.4 %copy-start.6 = (bf16[2,128,768]{2,1,0:T(8,128)(2,1)}, bf16[2,128,768]{2,1,0:T(8,128)(2,1)S(1)}, u32[]{:S(2)}) copy-start(bf16[2,128,768]{2,1,0:T(8,128)(2,1)S(1)} %collective-permute-done.2.refs_1_) | copy-start | bytes 1179652
  40.2 8.0 %copy-start.7 = (bf16[2,128,768]{2,1,0:T(8,128)(2,1)}, bf16[2,128,768]{2,1,0:T(8,128)(2,1)S(1)}, u32[]{:S(2)}) copy-start(bf16[2,128,768]{2,1,0:T(8,128)(2,1)S(1)} %collective-permute-done.3.refs_2_) | copy-start | bytes 1179652
  40.5 7.7 %copy-start.8 = (bf16[2,128,768]{2,1,0:T(8,128)(2,1)}, bf16[2,128,768]{2,1,0:T(8,128)(2,1)S(1)}, u32[]{:S(2)}) copy-start(bf16[2,128,768]{2,1,0:T(8,128)(2,1)S(1)} %collective-permute-done.4.refs_3_) | copy-start | bytes 1179652
  40.5 4.3 %collective-permute-start.10 = (bf16[2,128,768]{2,1,0:T(8,128)(2,1)S(1)}, bf16[2,128,768]{2,1,0:T(8,128)(2,1)S(1)}, u32[]{:S(2)}, u32[]{:S(2)}) collective-permute-start(bf16[2,128,768]{2,1,0:T(8,128)(2,1)S(1)} %collective-permute-done.3.refs_2_), channel_id=1, source_target_pairs={{0,8},{1,9},{2,10},{3,11},{4,12},{5,13},{6,14},{7,15},{8,0},{9,1},... | collective-permute-start | bytes 1179656 | tf_op jit(solution)/shard_map/ppermute | solution.py:46
  42.5 4.5 %collective-permute-start.11 = (bf16[2,128,768]{2,1,0:T(8,128)(2,1)S(1)}, bf16[2,128,768]{2,1,0:T(8,128)(2,1)S(1)}, u32[]{:S(2)}, u32[]{:S(2)}) collective-permute-start(bf16[2,128,768]{2,1,0:T(8,128)(2,1)S(1)} %collective-permute-done.4.refs_3_), channel_id=1, source_target_pairs={{0,8},{1,9},{2,10},{3,11},{4,12},{5,13},{6,14},{7,15},{8,0},{9,1},... | collective-permute-start | bytes 1179656 | tf_op jit(solution)/shard_map/ppermute | solution.py:46
  42.6 5.6 %collective-permute-start.8 = (bf16[2,128,768]{2,1,0:T(8,128)(2,1)S(1)}, bf16[2,128,768]{2,1,0:T(8,128)(2,1)S(1)}, u32[]{:S(2)}, u32[]{:S(2)}) collective-permute-start(bf16[2,128,768]{2,1,0:T(8,128)(2,1)S(1)} %pad_maximum_fusion.1.refs_0_), channel_id=1, source_target_pairs={{0,8},{1,9},{2,10},{3,11},{4,12},{5,13},{6,14},{7,15},{8,0},{9,1},... | collective-permute-start | bytes 1179656 | tf_op jit(solution)/shard_map/ppermute | solution.py:46
  43.0 6.0 %collective-permute-start.9 = (bf16[2,128,768]{2,1,0:T(8,128)(2,1)S(1)}, bf16[2,128,768]{2,1,0:T(8,128)(2,1)}, u32[]{:S(2)}, u32[]{:S(2)}) collective-permute-start(bf16[2,128,768]{2,1,0:T(8,128)(2,1)S(1)} %collective-permute-done.2.refs_1_), channel_id=1, source_target_pairs={{0,8},{1,9},{2,10},{3,11},{4,12},{5,13},{6,14},{7,15},{8,0},{9,1},... | collective-permute-start | bytes 1179656 | tf_op jit(solution)/shard_map/ppermute | solution.py:46
  43.9 28.0 %collective-permute-start.5 = (bf16[2,128,768]{2,1,0:T(8,128)(2,1)}, bf16[2,128,768]{2,1,0:T(8,128)(2,1)}, u32[]{:S(2)}, u32[]{:S(2)}) collective-permute-start(bf16[2,128,768]{2,1,0:T(8,128)(2,1)} %slice.6.refs_0_), channel_id=1, source_target_pairs={{0,1},{1,2},{2,3},{3,0},{4,5},{5,6},{6,7},{7,4},{8,9},{9,10},{10,1... | collective-permute-start | bytes 1179656 | tf_op jit(solution)/shard_map/ppermute | solution.py:46
  44.8 3.4 %copy-start.9 = (bf16[2,128,768]{2,1,0:T(8,128)(2,1)}, bf16[2,128,768]{2,1,0:T(8,128)(2,1)S(1)}, u32[]{:S(2)}) copy-start(bf16[2,128,768]{2,1,0:T(8,128)(2,1)S(1)} %collective-permute-done.10.refs_6_) | copy-start | bytes 1179652
  44.8 27.1 %collective-permute-start.6 = (bf16[2,128,768]{2,1,0:T(8,128)(2,1)}, bf16[2,128,768]{2,1,0:T(8,128)(2,1)}, u32[]{:S(2)}, u32[]{:S(2)}) collective-permute-start(bf16[2,128,768]{2,1,0:T(8,128)(2,1)} %slice.6.refs_0_), channel_id=1, source_target_pairs={{0,2},{1,3},{2,0},{3,1},{4,6},{5,7},{6,4},{7,5},{8,10},{9,11},{10,... | collective-permute-start | bytes 1179656 | tf_op jit(solution)/shard_map/ppermute | solution.py:46
  47.0 1.2 %copy-start.10 = (bf16[2,128,768]{2,1,0:T(8,128)(2,1)}, bf16[2,128,768]{2,1,0:T(8,128)(2,1)S(1)}, u32[]{:S(2)}) copy-start(bf16[2,128,768]{2,1,0:T(8,128)(2,1)S(1)} %collective-permute-done.11.refs_7_) | copy-start | bytes 1179652
  47.0 24.9 %collective-permute-start.7 = (bf16[2,128,768]{2,1,0:T(8,128)(2,1)}, bf16[2,128,768]{2,1,0:T(8,128)(2,1)}, u32[]{:S(2)}, u32[]{:S(2)}) collective-permute-start(bf16[2,128,768]{2,1,0:T(8,128)(2,1)} %slice.6.refs_0_), channel_id=1, source_target_pairs={{0,3},{1,0},{2,1},{3,2},{4,7},{5,4},{6,5},{7,6},{8,11},{9,8},{10,9... | collective-permute-start | bytes 1179656 | tf_op jit(solution)/shard_map/ppermute | solution.py:46
  48.2 0.8 copy-start.12
  72.0 34.1 %all-to-all-start.1 = ((bf16[32,32,512]{2,1,0:T(8,128)(2,1)}), bf16[32,32,512]{2,1,0:T(8,128)(2,1)}, u32[]{:S(2)}, u32[]{:S(2)}) async-start(bf16[32,32,512]{2,1,0:T(8,128)(2,1)} %col_heads.1), calls=%async_computation.1 | async-start | bytes 2097152 | tf_op jit(solution)/shard_map/all_to_all | solution.py:386
  77.1 2.4 %collective-permute-start.15 = (bf16[2,128,768]{2,1,0:T(8,128)(2,1)}, bf16[2,128,768]{2,1,0:T(8,128)(2,1)S(1)}, u32[]{:S(2)}, u32[]{:S(2)}) collective-permute-start(bf16[2,128,768]{2,1,0:T(8,128)(2,1)} %slice.6.refs_0_), channel_id=1, source_target_pairs={{0,8},{1,9},{2,10},{3,11},{4,12},{5,13},{6,14},{7,15},{8,0},{9,1},... | collective-permute-start | bytes 1179656 | tf_op jit(solution)/shard_map/ppermute | solution.py:46
  77.5 4.5 %collective-permute-start.16 = (bf16[2,128,768]{2,1,0:T(8,128)(2,1)}, bf16[2,128,768]{2,1,0:T(8,128)(2,1)S(1)}, u32[]{:S(2)}, u32[]{:S(2)}) collective-permute-start(bf16[2,128,768]{2,1,0:T(8,128)(2,1)} %collective-permute-done.5.refs_1_), channel_id=1, source_target_pairs={{0,8},{1,9},{2,10},{3,11},{4,12},{5,13},{6,14},{7,15},{8,0},{9,1},... | collective-permute-start | bytes 1179656 | tf_op jit(solution)/shard_map/ppermute | solution.py:46
  77.7 6.2 %collective-permute-start.17 = (bf16[2,128,768]{2,1,0:T(8,128)(2,1)}, bf16[2,128,768]{2,1,0:T(8,128)(2,1)}, u32[]{:S(2)}, u32[]{:S(2)}) collective-permute-start(bf16[2,128,768]{2,1,0:T(8,128)(2,1)} %collective-permute-done.6.refs_2_), channel_id=1, source_target_pairs={{0,8},{1,9},{2,10},{3,11},{4,12},{5,13},{6,14},{7,15},{8,0},{9,1},... | collective-permute-start | bytes 1179656 | tf_op jit(solution)/shard_map/ppermute | solution.py:46
  78.0 5.9 %collective-permute-start.18 = (bf16[2,128,768]{2,1,0:T(8,128)(2,1)}, bf16[2,128,768]{2,1,0:T(8,128)(2,1)}, u32[]{:S(2)}, u32[]{:S(2)}) collective-permute-start(bf16[2,128,768]{2,1,0:T(8,128)(2,1)} %collective-permute-done.7.refs_3_), channel_id=1, source_target_pairs={{0,8},{1,9},{2,10},{3,11},{4,12},{5,13},{6,14},{7,15},{8,0},{9,1},... | collective-permute-start | bytes 1179656 | tf_op jit(solution)/shard_map/ppermute | solution.py:46
  78.2 23.5 %copy-start.5 = (bf16[2,128,512]{2,1,0:T(8,128)(2,1)}, bf16[2,128,512]{2,1,0:T(8,128)(2,1)S(1)}, u32[]{:S(2)}) copy-start(bf16[2,128,512]{2,1,0:T(8,128)(2,1)S(1)} %slice.7.refs_0_) | copy-start | bytes 786436
  78.3 23.5 %collective-permute-start.12 = (bf16[2,128,512]{2,1,0:T(8,128)(2,1)S(1)}, bf16[2,128,512]{2,1,0:T(8,128)(2,1)S(1)}, u32[]{:S(2)}, u32[]{:S(2)}) collective-permute-start(bf16[2,128,512]{2,1,0:T(8,128)(2,1)S(1)} %slice.7.refs_0_), channel_id=1, source_target_pairs={{0,1},{1,2},{2,3},{3,0},{4,5},{5,6},{6,7},{7,4},{8,9},{9,10},{10,1... | collective-permute-start | bytes 786440 | tf_op jit(solution)/shard_map/ppermute | solution.py:46
  79.6 2.4 %copy-start.11 = (bf16[2,128,768]{2,1,0:T(8,128)(2,1)}, bf16[2,128,768]{2,1,0:T(8,128)(2,1)S(1)}, u32[]{:S(2)}) copy-start(bf16[2,128,768]{2,1,0:T(8,128)(2,1)S(1)} %collective-permute-done.15.refs_4_) | copy-start | bytes 1179652
  79.6 22.2 %collective-permute-start.13 = (bf16[2,128,512]{2,1,0:T(8,128)(2,1)S(1)}, bf16[2,128,512]{2,1,0:T(8,128)(2,1)S(1)}, u32[]{:S(2)}, u32[]{:S(2)}) collective-permute-start(bf16[2,128,512]{2,1,0:T(8,128)(2,1)S(1)} %slice.7.refs_0_), channel_id=1, source_target_pairs={{0,2},{1,3},{2,0},{3,1},{4,6},{5,7},{6,4},{7,5},{8,10},{9,11},{10,... | collective-permute-start | bytes 786440 | tf_op jit(solution)/shard_map/ppermute | solution.py:46
  82.0 0.8 copy-start.13
  82.8 19.0 %collective-permute-start.14 = (bf16[2,128,512]{2,1,0:T(8,128)(2,1)S(1)}, bf16[2,128,512]{2,1,0:T(8,128)(2,1)}, u32[]{:S(2)}, u32[]{:S(2)}) collective-permute-start(bf16[2,128,512]{2,1,0:T(8,128)(2,1)S(1)} %slice.7.refs_0_), channel_id=1, source_target_pairs={{0,3},{1,0},{2,1},{3,2},{4,7},{5,4},{6,5},{7,6},{8,11},{9,8},{10,9... | collective-permute-start | bytes 786440 | tf_op jit(solution)/shard_map/ppermute | solution.py:46
  101.7 4.3 %copy-start.14 = (bf16[2,128,512]{2,1,0:T(8,128)(2,1)}, bf16[2,128,512]{2,1,0:T(8,128)(2,1)S(1)}, u32[]{:S(2)}) copy-start(bf16[2,128,512]{2,1,0:T(8,128)(2,1)S(1)} %collective-permute-done.12.refs_1_) | copy-start | bytes 786436
  101.8 4.3 %copy-start.15 = (bf16[2,128,512]{2,1,0:T(8,128)(2,1)}, bf16[2,128,512]{2,1,0:T(8,128)(2,1)S(1)}, u32[]{:S(2)}) copy-start(bf16[2,128,512]{2,1,0:T(8,128)(2,1)S(1)} %collective-permute-done.13.refs_2_) | copy-start | bytes 786436
  101.8 2.4 %collective-permute-start.19 = (bf16[2,128,512]{2,1,0:T(8,128)(2,1)S(1)}, bf16[2,128,512]{2,1,0:T(8,128)(2,1)S(1)}, u32[]{:S(2)}, u32[]{:S(2)}) collective-permute-start(bf16[2,128,512]{2,1,0:T(8,128)(2,1)S(1)} %slice.7.refs_0_), channel_id=1, source_target_pairs={{0,8},{1,9},{2,10},{3,11},{4,12},{5,13},{6,14},{7,15},{8,0},{9,1},... | collective-permute-start | bytes 786440 | tf_op jit(solution)/shard_map/ppermute | solution.py:46
  103.0 1.5 %collective-permute-start.20 = (bf16[2,128,512]{2,1,0:T(8,128)(2,1)S(1)}, bf16[2,128,512]{2,1,0:T(8,128)(2,1)S(1)}, u32[]{:S(2)}, u32[]{:S(2)}) collective-permute-start(bf16[2,128,512]{2,1,0:T(8,128)(2,1)S(1)} %collective-permute-done.12.refs_1_), channel_id=1, source_target_pairs={{0,8},{1,9},{2,10},{3,11},{4,12},{5,13},{6,14},{7,15},{8,0},{9,1},... | collective-permute-start | bytes 786440 | tf_op jit(solution)/shard_map/ppermute | solution.py:46
  103.1 2.2 %collective-permute-start.21 = (bf16[2,128,512]{2,1,0:T(8,128)(2,1)S(1)}, bf16[2,128,512]{2,1,0:T(8,128)(2,1)S(1)}, u32[]{:S(2)}, u32[]{:S(2)}) collective-permute-start(bf16[2,128,512]{2,1,0:T(8,128)(2,1)S(1)} %collective-permute-done.13.refs_2_), channel_id=1, source_target_pairs={{0,8},{1,9},{2,10},{3,11},{4,12},{5,13},{6,14},{7,15},{8,0},{9,1},... | collective-permute-start | bytes 786440 | tf_op jit(solution)/shard_map/ppermute | solution.py:46
  103.5 2.5 %collective-permute-start.22 = (bf16[2,128,512]{2,1,0:T(8,128)(2,1)}, bf16[2,128,512]{2,1,0:T(8,128)(2,1)}, u32[]{:S(2)}, u32[]{:S(2)}) collective-permute-start(bf16[2,128,512]{2,1,0:T(8,128)(2,1)} %collective-permute-done.14.refs_3_), channel_id=1, source_target_pairs={{0,8},{1,9},{2,10},{3,11},{4,12},{5,13},{6,14},{7,15},{8,0},{9,1},... | collective-permute-start | bytes 786440 | tf_op jit(solution)/shard_map/ppermute | solution.py:46
  104.2 1.1 %copy-start.16 = (bf16[2,128,512]{2,1,0:T(8,128)(2,1)}, bf16[2,128,512]{2,1,0:T(8,128)(2,1)S(1)}, u32[]{:S(2)}) copy-start(bf16[2,128,512]{2,1,0:T(8,128)(2,1)S(1)} %collective-permute-done.19.refs_4_) | copy-start | bytes 786436
  104.6 0.8 copy-start.17
  105.3 0.7 copy-start.18

commit v6 on v5

--- a/solution.py
+++ b/solution.py
@@ -83,28 +83,24 @@
     rest_ref[:, 768:] = rebuilt.astype(BF16)
 
 
-def soft_average(queries, keys, values_ones, mask):
-    scores = lax.dot_general(queries, keys, (((1,), (1,)), ((), ())), preferred_element_type=F32)
-    width = mask.shape[1]
-    last = scores[:, -width:] + mask
-    scores = last if width == scores.shape[1] else jnp.concatenate([scores[:, :-width], last], 1)
-    peak = jnp.max(scores, axis=-1, keepdims=True)
-    weights = jnp.exp2((scores - peak) * LOG2_SCALE).astype(BF16)
-    both = jnp.dot(weights, values_ones, preferred_element_type=F32)
-    return both[:, :PAIR] / both[:, PAIR:]
-
-
 def lanes_of_first(rows):
     return lax.broadcasted_iota(jnp.int32, (rows, PAIR), 1) < HEAD_DIM
 
 
-def pair_attend(q, k, v, mask):
-    first = lanes_of_first(q.shape[0])
-    nothing = jnp.zeros_like(q)
-    values_ones = jnp.concatenate([v, jnp.ones_like(v)], 1)
-    even = soft_average(jnp.where(first, q, nothing), k, values_ones, mask)
-    odd = soft_average(jnp.where(first, nothing, q), k, values_ones, mask)
-    return jnp.where(first, even, odd).astype(BF16)
+def split_values(v, lanes):
+    nothing = jnp.zeros_like(v)
+    return jnp.concatenate(
+        [jnp.where(lanes, v, nothing), jnp.where(lanes, jnp.ones_like(v), nothing)], 1
+    )
+
+
+def causal_weights(q, k, mask):
+    scores = lax.dot_general(q, k, (((1,), (1,)), ((), ())), preferred_element_type=F32)
+    before = scores.shape[1] - mask.shape[1]
+    last = scores[:, before:] + mask
+    scores = jnp.concatenate([scores[:, :before], last], 1) if before else last
+    peak = jnp.max(scores, axis=-1, keepdims=True)
+    return jnp.exp2((scores - peak) * LOG2_SCALE).astype(BF16)
 
 
 def block_scores(q, k):
@@ -125,54 +121,66 @@
 
 def block_average(weights, v):
     first = lanes_of_first(v.shape[0])
-    nothing, one = jnp.zeros_like(v), jnp.ones_like(v)
-    values = jnp.concatenate(
-        [
-            jnp.concatenate([jnp.where(first, v, nothing), jnp.where(first, one, nothing)], 1),
-            jnp.concatenate([jnp.where(first, nothing, v), jnp.where(first, nothing, one)], 1),
-        ],
-        0,
-    )
-    both = jnp.dot(weights, values, preferred_element_type=F32)
+    values = [split_values(v, first), split_values(v, jnp.logical_not(first))]
+    both = jnp.dot(weights, jnp.concatenate(values, 0), preferred_element_type=F32)
     return (both[:, :PAIR] / both[:, PAIR:]).astype(BF16)
 
 
-def row_kernel(x_ref, *refs):
-    slabs = refs[:8]
-    o_hbm, w, qkv, attended, mask_ref, sems, sems_o = refs[8:]
-    copies = fetch_weights(slabs, w, sems)
+def row_kernel(x_hbm, *refs):
+    o_hbm, x, w, normed, qkv, attended, mask_ref, sems, sems_x, sems_o = refs[8:]
     block = 256
+    count = STRIDE // block
+    arrive = []
+    for i in range(count):
+        at = pl.ds(i * block, block)
+        arrive.append(pltpu.make_async_copy(x_hbm.at[at, :], x.at[at, :], sems_x.at[i]))
+        arrive[i].start()
+    copies = fetch_weights(refs[:8], w, sems)
     row = lax.broadcasted_iota(jnp.int32, (block, block), 0)
     col = lax.broadcasted_iota(jnp.int32, (block, block), 1)
     mask_ref[...] = jnp.where(col <= row, 0.0, -jnp.inf)
+    for i in range(count):
+        arrive[i].wait()
+        at = slice(i * block, (i + 1) * block)
+        normed[at, :] = normalized(x[at, :].astype(F32))
     for copy in copies:
         copy.wait()
-
-    def project(i, _):
-        at = pl.ds(pl.multiple_of(i * block, block), block)
-        normed = normalized(x_ref[at, :].astype(F32))
+    for i in range(count):
+        at = slice(i * block, (i + 1) * block)
         for half in range(2):
-            made = jnp.dot(normed, w[half], preferred_element_type=F32).astype(BF16)
+            made = jnp.dot(normed[at, :], w[half], preferred_element_type=F32).astype(BF16)
             for which in range(3):
                 for p in range(2):
                     lane = which * 256 + p * PAIR
                     qkv[which, half * 2 + p, at, :] = made[:, lane : lane + PAIR]
-        return 0
-
-    lax.fori_loop(0, STRIDE // block, project, 0)
-
+    leave = []
     for p in range(4):
-        for i in range(STRIDE // block):
-            upto = (i + 1) * block
-            attended[i * block : upto, p * PAIR : (p + 1) * PAIR] = pair_attend(
-                qkv[0, p, i * block : upto, :],
-                qkv[1, p, :upto, :],
-                qkv[2, p, :upto, :],
-                mask_ref[...],
+        first = lanes_of_first(STRIDE)
+        values = [split_values(qkv[2, p], first), split_values(qkv[2, p], jnp.logical_not(first))]
+        shares = []
+        for i in range(count):
+            q, k = qkv[0, p, i * block : (i + 1) * block, :], qkv[1, p, : (i + 1) * block, :]
+            mine = lanes_of_first(block)
+            nothing = jnp.zeros_like(q)
+            shares.append(
+                [
+                    causal_weights(masked, k, mask_ref[...])
+                    for masked in (jnp.where(mine, q, nothing), jnp.where(mine, nothing, q))
+                ]
             )
-    copy = pltpu.make_async_copy(attended, o_hbm, sems_o.at[0])
-    copy.start()
-    copy.wait()
+        for i in range(count):
+            both = jnp.dot(
+                jnp.concatenate(shares[i], 1),
+                jnp.concatenate([value[: (i + 1) * block] for value in values], 0),
+                preferred_element_type=F32,
+            )
+            attended[p, i * block : (i + 1) * block, :] = (both[:, :PAIR] / both[:, PAIR:]).astype(BF16)
+        leave.append(
+            pltpu.make_async_copy(attended.at[p], o_hbm.at[:, pl.ds(p * PAIR, PAIR)], sems_o.at[p])
+        )
+        leave[p].start()
+    for copy in leave:
+        copy.wait()
 
 
 def sequence_row(place):
@@ -310,15 +318,18 @@
     return pl.pallas_call(
         row_kernel,
         out_shape=jax.ShapeDtypeStruct((STRIDE, HALF), BF16),
-        in_specs=[WHOLE] + [ANY] * 8,
+        in_specs=[FAR] + [ANY] * 8,
         out_specs=FAR,
         scratch_shapes=[
+            pltpu.VMEM((STRIDE, D), BF16),
             pltpu.VMEM((2, D, QKV), BF16),
+            pltpu.VMEM((STRIDE, D), BF16),
             pltpu.VMEM((3, 4, STRIDE, PAIR), BF16),
-            pltpu.VMEM((STRIDE, HALF), BF16),
+            pltpu.VMEM((4, STRIDE, PAIR), BF16),
             pltpu.VMEM((256, 256), F32),
             DMA((16,)),
-            DMA((1,)),
+            DMA((4,)),
+            DMA((4,)),
         ],
         compiler_params=limit(63),
         cost_estimate=pl.CostEstimate(

time: 113 us -> 111 us (0.982)
  Pallas kernels: 34.7 us -> 30.5 us
  waiting for transfers between devices: 34.2 us -> 36.3 us
    pallas_call x1, Pallas kernels: 17.8 us -> 13.7 us  [row_heads(): pl.pallas_call(row_kernel, out_shape=jax.ShapeDtypeStruct((STRIDE, HALF),...]
    all_to_all x2, waiting for transfers between devices: 12.2 us -> 14.3 us  [exchange(): lax.all_to_all(blocks, 'seq', split_axis=0, concat_axis=0, tiled=True, ax...]
  transfers between devices with their start and end apart: 25 -> 25, of which waited for: 9 -> 10; matrix products, arithmetic and copies ran while one was open for 1% -> 1% of each run, Pallas kernels for 26% -> 22%
where the time goes in v6:
time: 111 us; the launch traced here: 110 us
  starting transfers between devices  39.1 us (35%)
  waiting for transfers between devices  36.3 us (33%)
  Pallas kernels  30.5 us (27%)
  local copies, waits for them, and re-layouts  3.13 us (3%)
    ppermute x23, starting transfers between devices, send(): return lax.ppermute(value, BOTH, where)  22.6 us
    ppermute x23, waiting for transfers between devices, send(): return lax.ppermute(value, BOTH, where)  22 us
    all_to_all x2, starting transfers between devices, exchange(): lax.all_to_all(blocks, 'seq', split_axis=0, concat_axis=0, tiled=True, ax...  16.5 us
    all_to_all x2, waiting for transfers between devices, exchange(): lax.all_to_all(blocks, 'seq', split_axis=0, concat_axis=0, tiled=True, ax...  14.3 us
    pallas_call x1, Pallas kernels, row_heads(): pl.pallas_call(row_kernel, out_shape=jax.ShapeDtypeStruct((STRIDE, HALF),...  13.7 us
    pallas_call x1, Pallas kernels, col_heads(): pl.pallas_call(col_kernel, out_shape=jax.ShapeDtypeStruct((rows, cols, HA...  10.7 us
    pallas_call x1, Pallas kernels, project_out(): pl.pallas_call(out_kernel, out_shape=jax.ShapeDtypeStruct((STRIDE, D), BF...  5.95 us
    unnamed x38, local copies, waits for them, and re-layouts  2.31 us
  transfers between devices with their start and end apart: 25, of which 10 were waited for; matrix products, arithmetic and copies ran while one was open for 1% of the time, Pallas kernels for 22%

profile of v6, /device:TPU:1, one launch (start us, length us, event | category | flops | bytes accessed | tf_op | source)
XLA Modules:
  0.0 110.3 jit_solution(4248315993542223126)
XLA Ops:
  0.0 11.3 %all-to-all-start = ((bf16[32,32,1024]{2,1,0:T(8,128)(2,1)}), bf16[32,32,1024]{2,1,0:T(8,128)(2,1)}, u32[]{:S(2)}, u32[]{:S(2)}) async-start(bf16[32,32,1024]{2,1,0:T(8,128)(2,1)} %bitcast.10), calls=%async_computation | async-start | bytes 4194304 | tf_op jit(solution)/shard_map/all_to_all | solution.py:397
  12.0 0.2 rebuilt_half.1
  12.2 2.9 %collective-permute-start.1 = (bf16[128,768]{1,0:T(8,128)(2,1)S(1)}, bf16[128,768]{1,0:T(8,128)(2,1)S(1)}, u32[]{:S(2)}, u32[]{:S(2)}) collective-permute-start(bf16[128,768]{1,0:T(8,128)(2,1)S(1)} %get-tuple-element.24), channel_id=1, source_target_pairs={{0,132},{1,133},{2,134},{3,135},{4,128},{5,129},{6,130},{7,131},{8... | collective-permute-start | bytes 589832 | tf_op jit(solution)/shard_map/ppermute | solution.py:46
  15.1 0.1 collective-permute-start
  15.2 4.9 %collective-permute-done.1 = bf16[128,768]{1,0:T(8,128)(2,1)S(1)} collective-permute-done((bf16[128,768]{1,0:T(8,128)(2,1)S(1)}, bf16[128,768]{1,0:T(8,128)(2,1)S(1)}, u32[]{:S(2)}, u32[]{:S(2)}) %collective-permute-start.1) | collective-permute-done | bytes 196640 | tf_op jit(solution)/shard_map/ppermute | solution.py:46
  20.2 1.3 %collective-permute-start.2 = (bf16[2,128,768]{2,1,0:T(8,128)(2,1)S(1)}, bf16[2,128,768]{2,1,0:T(8,128)(2,1)S(1)}, u32[]{:S(2)}, u32[]{:S(2)}) collective-permute-start(bf16[2,128,768]{2,1,0:T(8,128)(2,1)S(1)} %pad_maximum_fusion.1.refs_0_), channel_id=1, source_target_pairs={{0,1},{1,2},{2,3},{3,0},{4,5},{5,6},{6,7},{7,4},{8,9},{9,10},{10,1... | collective-permute-start | bytes 1179656 | tf_op jit(solution)/shard_map/ppermute | solution.py:46
  21.5 2.5 %collective-permute-start.3 = (bf16[2,128,768]{2,1,0:T(8,128)(2,1)S(1)}, bf16[2,128,768]{2,1,0:T(8,128)(2,1)S(1)}, u32[]{:S(2)}, u32[]{:S(2)}) collective-permute-start(bf16[2,128,768]{2,1,0:T(8,128)(2,1)S(1)} %pad_maximum_fusion.1.refs_0_), channel_id=1, source_target_pairs={{0,2},{1,3},{2,0},{3,1},{4,6},{5,7},{6,4},{7,5},{8,10},{9,11},{10,... | collective-permute-start | bytes 1179656 | tf_op jit(solution)/shard_map/ppermute | solution.py:46
  23.9 1.2 %collective-permute-start.4 = (bf16[2,128,768]{2,1,0:T(8,128)(2,1)S(1)}, bf16[2,128,768]{2,1,0:T(8,128)(2,1)S(1)}, u32[]{:S(2)}, u32[]{:S(2)}) collective-permute-start(bf16[2,128,768]{2,1,0:T(8,128)(2,1)S(1)} %pad_maximum_fusion.1.refs_0_), channel_id=1, source_target_pairs={{0,3},{1,0},{2,1},{3,2},{4,7},{5,4},{6,5},{7,6},{8,11},{9,8},{10,9... | collective-permute-start | bytes 1179656 | tf_op jit(solution)/shard_map/ppermute | solution.py:46
  25.1 2.1 %collective-permute-done = bf16[128,1280]{1,0:T(8,128)(2,1)S(1)} collective-permute-done((bf16[128,1280]{1,0:T(8,128)(2,1)S(1)}, bf16[128,1280]{1,0:T(8,128)(2,1)S(1)}, u32[]{:S(2)}, u32[]{:S(2)}) %collective-permute-start) | collective-permute-done | bytes 327712 | tf_op jit(solution)/shard_map/ppermute | solution.py:46
  27.2 0.1 pad_maximum_fusion
  27.2 3.6 %collective-permute-done.2.refs_1_ = bf16[2,128,768]{2,1,0:T(8,128)(2,1)S(1)} collective-permute-done((bf16[2,128,768]{2,1,0:T(8,128)(2,1)S(1)}, bf16[2,128,768]{2,1,0:T(8,128)(2,1)S(1)}, u32[]{:S(2)}, u32[]{:S(2)}) %collective-permute-start.2) | collective-permute-done | bytes 393248 | tf_op jit(solution)/shard_map/ppermute | solution.py:46
  30.8 9.4 %collective-permute-done.3.refs_2_ = bf16[2,128,768]{2,1,0:T(8,128)(2,1)S(1)} collective-permute-done((bf16[2,128,768]{2,1,0:T(8,128)(2,1)S(1)}, bf16[2,128,768]{2,1,0:T(8,128)(2,1)S(1)}, u32[]{:S(2)}, u32[]{:S(2)}) %collective-permute-start.3) | collective-permute-done | bytes 393248 | tf_op jit(solution)/shard_map/ppermute | solution.py:46
  40.2 0.3 collective-permute-done.4.refs_3_
  40.5 2.0 %collective-permute-start.10 = (bf16[2,128,768]{2,1,0:T(8,128)(2,1)S(1)}, bf16[2,128,768]{2,1,0:T(8,128)(2,1)S(1)}, u32[]{:S(2)}, u32[]{:S(2)}) collective-permute-start(bf16[2,128,768]{2,1,0:T(8,128)(2,1)S(1)} %collective-permute-done.3.refs_2_), channel_id=1, source_target_pairs={{0,8},{1,9},{2,10},{3,11},{4,12},{5,13},{6,14},{7,15},{8,0},{9,1},... | collective-permute-start | bytes 1179656 | tf_op jit(solution)/shard_map/ppermute | solution.py:46
  42.5 0.1 collective-permute-start.11
  42.6 0.4 collective-permute-start.8
  43.0 0.1 collective-permute-start.9
  43.1 0.8 slice.6.refs_0_
  43.9 0.9 collective-permute-start.5
  44.8 2.2 %collective-permute-start.6 = (bf16[2,128,768]{2,1,0:T(8,128)(2,1)}, bf16[2,128,768]{2,1,0:T(8,128)(2,1)}, u32[]{:S(2)}, u32[]{:S(2)}) collective-permute-start(bf16[2,128,768]{2,1,0:T(8,128)(2,1)} %slice.6.refs_0_), channel_id=1, source_target_pairs={{0,2},{1,3},{2,0},{3,1},{4,6},{5,7},{6,4},{7,5},{8,10},{9,11},{10,... | collective-permute-start | bytes 1179656 | tf_op jit(solution)/shard_map/ppermute | solution.py:46
  47.0 0.0 collective-permute-done.11.refs_7_
  47.0 1.2 %collective-permute-start.7 = (bf16[2,128,768]{2,1,0:T(8,128)(2,1)}, bf16[2,128,768]{2,1,0:T(8,128)(2,1)}, u32[]{:S(2)}, u32[]{:S(2)}) collective-permute-start(bf16[2,128,768]{2,1,0:T(8,128)(2,1)} %slice.6.refs_0_), channel_id=1, source_target_pairs={{0,3},{1,0},{2,1},{3,2},{4,7},{5,4},{6,5},{7,6},{8,11},{9,8},{10,9... | collective-permute-start | bytes 1179656 | tf_op jit(solution)/shard_map/ppermute | solution.py:46
  48.2 0.0 collective-permute-done.8.refs_4_
  48.3 0.7 copy-done.12
  49.0 0.0 collective-permute-done.9.refs_5_
  49.0 12.2 %all-to-all-done.x_hbm = bf16[32,32,1024]{2,1,0:T(8,128)(2,1)} async-done(((bf16[32,32,1024]{2,1,0:T(8,128)(2,1)}), bf16[32,32,1024]{2,1,0:T(8,128)(2,1)}, u32[]{:S(2)}, u32[]{:S(2)}) %all-to-all-start) | async-done | bytes 2097184 | tf_op jit(solution)/shard_map/all_to_all | solution.py:397
  61.2 10.7 %col_heads.1 = bf16[32,32,512]{2,1,0:T(8,128)(2,1)} custom-call(bf16[32,32,1024]{2,1,0:T(8,128)(2,1)} %all-to-all-done.x_hbm, bf16[2,128,768]{2,1,0:T(8,128)(2,1)} %copy-done.4, bf16[2,128,768]{2,1,0:T(8,128)(2,1)} %copy-done.6, bf16[2,128,768]{2,1,0:T(8,128)(2,1)} %copy-done.7, bf16[2,128,768]{2,1,0:T(8,128)(2,1)} %copy-done.8, ...), custom_call_target="tpu_custom_call" | custom-call | flops 4000000000 | bytes 6291456 | tf_op jit(solution)/shard_map/col_heads/pallas_call | solution.py:344
  71.9 0.0 collective-permute-done.5.refs_1_
  72.0 5.1 %all-to-all-start.1 = ((bf16[32,32,512]{2,1,0:T(8,128)(2,1)}), bf16[32,32,512]{2,1,0:T(8,128)(2,1)}, u32[]{:S(2)}, u32[]{:S(2)}) async-start(bf16[32,32,512]{2,1,0:T(8,128)(2,1)} %col_heads.1), calls=%async_computation.1 | async-start | bytes 2097152 | tf_op jit(solution)/shard_map/all_to_all | solution.py:397
  77.1 0.4 collective-permute-start.15
  77.5 0.2 collective-permute-start.16
  77.7 0.3 collective-permute-start.17
  78.0 0.2 collective-permute-start.18
  78.2 1.3 %collective-permute-start.12 = (bf16[2,128,512]{2,1,0:T(8,128)(2,1)S(1)}, bf16[2,128,512]{2,1,0:T(8,128)(2,1)S(1)}, u32[]{:S(2)}, u32[]{:S(2)}) collective-permute-start(bf16[2,128,512]{2,1,0:T(8,128)(2,1)S(1)} %slice.7.refs_0_), channel_id=1, source_target_pairs={{0,1},{1,2},{2,3},{3,0},{4,5},{5,6},{6,7},{7,4},{8,9},{9,10},{10,1... | collective-permute-start | bytes 786440 | tf_op jit(solution)/shard_map/ppermute | solution.py:46
  79.6 2.4 %collective-permute-start.13 = (bf16[2,128,512]{2,1,0:T(8,128)(2,1)S(1)}, bf16[2,128,512]{2,1,0:T(8,128)(2,1)S(1)}, u32[]{:S(2)}, u32[]{:S(2)}) collective-permute-start(bf16[2,128,512]{2,1,0:T(8,128)(2,1)S(1)} %slice.7.refs_0_), channel_id=1, source_target_pairs={{0,2},{1,3},{2,0},{3,1},{4,6},{5,7},{6,4},{7,5},{8,10},{9,11},{10,... | collective-permute-start | bytes 786440 | tf_op jit(solution)/shard_map/ppermute | solution.py:46
  82.0 0.8 copy-done.13
  82.8 1.2 %collective-permute-start.14 = (bf16[2,128,512]{2,1,0:T(8,128)(2,1)S(1)}, bf16[2,128,512]{2,1,0:T(8,128)(2,1)}, u32[]{:S(2)}, u32[]{:S(2)}) collective-permute-start(bf16[2,128,512]{2,1,0:T(8,128)(2,1)S(1)} %slice.7.refs_0_), channel_id=1, source_target_pairs={{0,3},{1,0},{2,1},{3,2},{4,7},{5,4},{6,5},{7,6},{8,11},{9,8},{10,9... | collective-permute-start | bytes 786440 | tf_op jit(solution)/shard_map/ppermute | solution.py:46
  83.9 13.7 %row_heads.1.row_hbm = bf16[1024,512]{1,0:T(8,128)(2,1)} custom-call(bf16[1024,1024]{1,0:T(8,128)(2,1)} %bitcast.11, bf16[2,128,768]{2,1,0:T(8,128)(2,1)} %slice.6.refs_0_, bf16[2,128,768]{2,1,0:T(8,128)(2,1)} %collective-permute-done.5.refs_1_, bf16[2,128,768]{2,1,0:T(8,128)(2,1)} %collective-permute-done.6.refs_2_, ...), custom_call_target="tpu_custom_call" | custom-call | flops 6000000000 | bytes 6291456 | tf_op jit(solution)/shard_map/row_heads/pallas_call | solution.py:318
  97.7 1.2 %collective-permute-start.19 = (bf16[2,128,512]{2,1,0:T(8,128)(2,1)S(1)}, bf16[2,128,512]{2,1,0:T(8,128)(2,1)S(1)}, u32[]{:S(2)}, u32[]{:S(2)}) collective-permute-start(bf16[2,128,512]{2,1,0:T(8,128)(2,1)S(1)} %slice.7.refs_0_), channel_id=1, source_target_pairs={{0,8},{1,9},{2,10},{3,11},{4,12},{5,13},{6,14},{7,15},{8,0},{9,1},... | collective-permute-start | bytes 786440 | tf_op jit(solution)/shard_map/ppermute | solution.py:46
  98.9 0.1 collective-permute-start.20
  99.0 0.4 collective-permute-start.21
  99.5 0.1 collective-permute-start.22
  99.6 0.6 collective-permute-done.19.refs_4_
  100.1 0.4 collective-permute-done.20.refs_5_
  100.5 0.7 collective-permute-done.21.refs_6_
  101.2 0.7 copy-done.18
  102.0 2.1 %all-to-all-done.1 = bf16[32,32,512]{2,1,0:T(8,128)(2,1)} async-done(((bf16[32,32,512]{2,1,0:T(8,128)(2,1)}), bf16[32,32,512]{2,1,0:T(8,128)(2,1)}, u32[]{:S(2)}, u32[]{:S(2)}) %all-to-all-start.1) | async-done | bytes 1048608 | tf_op jit(solution)/shard_map/all_to_all | solution.py:397
  104.1 6.0 %project_out.1 = bf16[1024,1024]{1,0:T(8,128)(2,1)} custom-call(bf16[1024,512]{1,0:T(8,128)(2,1)} %row_heads.1.row_hbm, bf16[1024,512]{1,0:T(8,128)(2,1)} %bitcast.6.col_hbm, bf16[2,128,512]{2,1,0:T(8,128)(2,1)} %copy-done.5, bf16[2,128,512]{2,1,0:T(8,128)(2,1)} %copy-done.14, bf16[2,128,512]{2,1,0:T(8,128)(2,1)} %copy-done.15, ...), custom_call_target="tpu_custom_call" | custom-call | flops 2000000000 | bytes 6291456 | tf_op jit(solution)/shard_map/project_out/pallas_call | solution.py:370
  (48 shorter events, 0.2 us)
Async XLA Ops:
  0.0 12.0 %copy-start = (bf16[128,3072]{1,0:T(8,128)(2,1)S(1)}, bf16[128,3072]{1,0:T(8,128)(2,1)}, u32[]{:S(2)}) copy-start(bf16[128,3072]{1,0:T(8,128)(2,1)} %qb_ref.1) | copy-start | bytes 2359300
  0.0 12.0 %copy-start.1 = (bf16[128,3072]{1,0:T(8,128)(2,1)S(1)}, bf16[128,3072]{1,0:T(8,128)(2,1)}, u32[]{:S(2)}) copy-start(bf16[128,3072]{1,0:T(8,128)(2,1)} %qd_ref.1) | copy-start | bytes 2359300
  0.0 12.0 %copy-start.2 = (bf16[128,1024]{1,0:T(8,128)(2,1)S(1)}, bf16[128,1024]{1,0:T(8,128)(2,1)}, u32[]{:S(2)}) copy-start(bf16[128,1024]{1,0:T(8,128)(2,1)} %ob_ref.1) | copy-start | bytes 786436
  0.0 12.0 %copy-start.3 = (bf16[128,1024]{1,0:T(8,128)(2,1)S(1)}, bf16[128,1024]{1,0:T(8,128)(2,1)}, u32[]{:S(2)}) copy-start(bf16[128,1024]{1,0:T(8,128)(2,1)} %od_ref.1) | copy-start | bytes 786436
  0.0 61.2 %all-to-all-start = ((bf16[32,32,1024]{2,1,0:T(8,128)(2,1)}), bf16[32,32,1024]{2,1,0:T(8,128)(2,1)}, u32[]{:S(2)}, u32[]{:S(2)}) async-start(bf16[32,32,1024]{2,1,0:T(8,128)(2,1)} %bitcast.10), calls=%async_computation | async-start | bytes 4194304 | tf_op jit(solution)/shard_map/all_to_all | solution.py:397
  12.2 7.9 %collective-permute-start.1 = (bf16[128,768]{1,0:T(8,128)(2,1)S(1)}, bf16[128,768]{1,0:T(8,128)(2,1)S(1)}, u32[]{:S(2)}, u32[]{:S(2)}) collective-permute-start(bf16[128,768]{1,0:T(8,128)(2,1)S(1)} %get-tuple-element.24), channel_id=1, source_target_pairs={{0,132},{1,133},{2,134},{3,135},{4,128},{5,129},{6,130},{7,131},{8... | collective-permute-start | bytes 589832 | tf_op jit(solution)/shard_map/ppermute | solution.py:46
  15.1 12.0 %collective-permute-start = (bf16[128,1280]{1,0:T(8,128)(2,1)S(1)}, bf16[128,1280]{1,0:T(8,128)(2,1)S(1)}, u32[]{:S(2)}, u32[]{:S(2)}) collective-permute-start(bf16[128,1280]{1,0:T(8,128)(2,1)S(1)} %get-tuple-element.23), channel_id=1, source_target_pairs={{0,132},{1,133},{2,134},{3,135},{4,128},{5,129},{6,130},{7,131},{8... | collective-permute-start | bytes 983048 | tf_op jit(solution)/shard_map/ppermute | solution.py:46
  20.2 22.4 %copy-start.4 = (bf16[2,128,768]{2,1,0:T(8,128)(2,1)}, bf16[2,128,768]{2,1,0:T(8,128)(2,1)S(1)}, u32[]{:S(2)}) copy-start(bf16[2,128,768]{2,1,0:T(8,128)(2,1)S(1)} %pad_maximum_fusion.1.refs_0_) | copy-start | bytes 1179652
  20.2 10.6 %collective-permute-start.2 = (bf16[2,128,768]{2,1,0:T(8,128)(2,1)S(1)}, bf16[2,128,768]{2,1,0:T(8,128)(2,1)S(1)}, u32[]{:S(2)}, u32[]{:S(2)}) collective-permute-start(bf16[2,128,768]{2,1,0:T(8,128)(2,1)S(1)} %pad_maximum_fusion.1.refs_0_), channel_id=1, source_target_pairs={{0,1},{1,2},{2,3},{3,0},{4,5},{5,6},{6,7},{7,4},{8,9},{9,10},{10,1... | collective-permute-start | bytes 1179656 | tf_op jit(solution)/shard_map/ppermute | solution.py:46
  21.5 18.7 %collective-permute-start.3 = (bf16[2,128,768]{2,1,0:T(8,128)(2,1)S(1)}, bf16[2,128,768]{2,1,0:T(8,128)(2,1)S(1)}, u32[]{:S(2)}, u32[]{:S(2)}) collective-permute-start(bf16[2,128,768]{2,1,0:T(8,128)(2,1)S(1)} %pad_maximum_fusion.1.refs_0_), channel_id=1, source_target_pairs={{0,2},{1,3},{2,0},{3,1},{4,6},{5,7},{6,4},{7,5},{8,10},{9,11},{10,... | collective-permute-start | bytes 1179656 | tf_op jit(solution)/shard_map/ppermute | solution.py:46
  23.9 16.6 %collective-permute-start.4 = (bf16[2,128,768]{2,1,0:T(8,128)(2,1)S(1)}, bf16[2,128,768]{2,1,0:T(8,128)(2,1)S(1)}, u32[]{:S(2)}, u32[]{:S(2)}) collective-permute-start(bf16[2,128,768]{2,1,0:T(8,128)(2,1)S(1)} %pad_maximum_fusion.1.refs_0_), channel_id=1, source_target_pairs={{0,3},{1,0},{2,1},{3,2},{4,7},{5,4},{6,5},{7,6},{8,11},{9,8},{10,9... | collective-permute-start | bytes 1179656 | tf_op jit(solution)/shard_map/ppermute | solution.py:46
  30.8 17.4 %copy-start.6 = (bf16[2,128,768]{2,1,0:T(8,128)(2,1)}, bf16[2,128,768]{2,1,0:T(8,128)(2,1)S(1)}, u32[]{:S(2)}) copy-start(bf16[2,128,768]{2,1,0:T(8,128)(2,1)S(1)} %collective-permute-done.2.refs_1_) | copy-start | bytes 1179652
  40.2 8.0 %copy-start.7 = (bf16[2,128,768]{2,1,0:T(8,128)(2,1)}, bf16[2,128,768]{2,1,0:T(8,128)(2,1)S(1)}, u32[]{:S(2)}) copy-start(bf16[2,128,768]{2,1,0:T(8,128)(2,1)S(1)} %collective-permute-done.3.refs_2_) | copy-start | bytes 1179652
  40.5 7.7 %copy-start.8 = (bf16[2,128,768]{2,1,0:T(8,128)(2,1)}, bf16[2,128,768]{2,1,0:T(8,128)(2,1)S(1)}, u32[]{:S(2)}) copy-start(bf16[2,128,768]{2,1,0:T(8,128)(2,1)S(1)} %collective-permute-done.4.refs_3_) | copy-start | bytes 1179652
  40.5 4.3 %collective-permute-start.10 = (bf16[2,128,768]{2,1,0:T(8,128)(2,1)S(1)}, bf16[2,128,768]{2,1,0:T(8,128)(2,1)S(1)}, u32[]{:S(2)}, u32[]{:S(2)}) collective-permute-start(bf16[2,128,768]{2,1,0:T(8,128)(2,1)S(1)} %collective-permute-done.3.refs_2_), channel_id=1, source_target_pairs={{0,8},{1,9},{2,10},{3,11},{4,12},{5,13},{6,14},{7,15},{8,0},{9,1},... | collective-permute-start | bytes 1179656 | tf_op jit(solution)/shard_map/ppermute | solution.py:46
  42.5 4.5 %collective-permute-start.11 = (bf16[2,128,768]{2,1,0:T(8,128)(2,1)S(1)}, bf16[2,128,768]{2,1,0:T(8,128)(2,1)S(1)}, u32[]{:S(2)}, u32[]{:S(2)}) collective-permute-start(bf16[2,128,768]{2,1,0:T(8,128)(2,1)S(1)} %collective-permute-done.4.refs_3_), channel_id=1, source_target_pairs={{0,8},{1,9},{2,10},{3,11},{4,12},{5,13},{6,14},{7,15},{8,0},{9,1},... | collective-permute-start | bytes 1179656 | tf_op jit(solution)/shard_map/ppermute | solution.py:46
  42.6 5.6 %collective-permute-start.8 = (bf16[2,128,768]{2,1,0:T(8,128)(2,1)S(1)}, bf16[2,128,768]{2,1,0:T(8,128)(2,1)S(1)}, u32[]{:S(2)}, u32[]{:S(2)}) collective-permute-start(bf16[2,128,768]{2,1,0:T(8,128)(2,1)S(1)} %pad_maximum_fusion.1.refs_0_), channel_id=1, source_target_pairs={{0,8},{1,9},{2,10},{3,11},{4,12},{5,13},{6,14},{7,15},{8,0},{9,1},... | collective-permute-start | bytes 1179656 | tf_op jit(solution)/shard_map/ppermute | solution.py:46
  43.0 6.0 %collective-permute-start.9 = (bf16[2,128,768]{2,1,0:T(8,128)(2,1)S(1)}, bf16[2,128,768]{2,1,0:T(8,128)(2,1)}, u32[]{:S(2)}, u32[]{:S(2)}) collective-permute-start(bf16[2,128,768]{2,1,0:T(8,128)(2,1)S(1)} %collective-permute-done.2.refs_1_), channel_id=1, source_target_pairs={{0,8},{1,9},{2,10},{3,11},{4,12},{5,13},{6,14},{7,15},{8,0},{9,1},... | collective-permute-start | bytes 1179656 | tf_op jit(solution)/shard_map/ppermute | solution.py:46
  43.9 28.0 %collective-permute-start.5 = (bf16[2,128,768]{2,1,0:T(8,128)(2,1)}, bf16[2,128,768]{2,1,0:T(8,128)(2,1)}, u32[]{:S(2)}, u32[]{:S(2)}) collective-permute-start(bf16[2,128,768]{2,1,0:T(8,128)(2,1)} %slice.6.refs_0_), channel_id=1, source_target_pairs={{0,1},{1,2},{2,3},{3,0},{4,5},{5,6},{6,7},{7,4},{8,9},{9,10},{10,1... | collective-permute-start | bytes 1179656 | tf_op jit(solution)/shard_map/ppermute | solution.py:46
  44.8 3.4 %copy-start.9 = (bf16[2,128,768]{2,1,0:T(8,128)(2,1)}, bf16[2,128,768]{2,1,0:T(8,128)(2,1)S(1)}, u32[]{:S(2)}) copy-start(bf16[2,128,768]{2,1,0:T(8,128)(2,1)S(1)} %collective-permute-done.10.refs_6_) | copy-start | bytes 1179652
  44.8 27.1 %collective-permute-start.6 = (bf16[2,128,768]{2,1,0:T(8,128)(2,1)}, bf16[2,128,768]{2,1,0:T(8,128)(2,1)}, u32[]{:S(2)}, u32[]{:S(2)}) collective-permute-start(bf16[2,128,768]{2,1,0:T(8,128)(2,1)} %slice.6.refs_0_), channel_id=1, source_target_pairs={{0,2},{1,3},{2,0},{3,1},{4,6},{5,7},{6,4},{7,5},{8,10},{9,11},{10,... | collective-permute-start | bytes 1179656 | tf_op jit(solution)/shard_map/ppermute | solution.py:46
  47.0 1.2 %copy-start.10 = (bf16[2,128,768]{2,1,0:T(8,128)(2,1)}, bf16[2,128,768]{2,1,0:T(8,128)(2,1)S(1)}, u32[]{:S(2)}) copy-start(bf16[2,128,768]{2,1,0:T(8,128)(2,1)S(1)} %collective-permute-done.11.refs_7_) | copy-start | bytes 1179652
  47.0 24.9 %collective-permute-start.7 = (bf16[2,128,768]{2,1,0:T(8,128)(2,1)}, bf16[2,128,768]{2,1,0:T(8,128)(2,1)}, u32[]{:S(2)}, u32[]{:S(2)}) collective-permute-start(bf16[2,128,768]{2,1,0:T(8,128)(2,1)} %slice.6.refs_0_), channel_id=1, source_target_pairs={{0,3},{1,0},{2,1},{3,2},{4,7},{5,4},{6,5},{7,6},{8,11},{9,8},{10,9... | collective-permute-start | bytes 1179656 | tf_op jit(solution)/shard_map/ppermute | solution.py:46
  48.2 0.8 copy-start.12
  72.0 32.1 %all-to-all-start.1 = ((bf16[32,32,512]{2,1,0:T(8,128)(2,1)}), bf16[32,32,512]{2,1,0:T(8,128)(2,1)}, u32[]{:S(2)}, u32[]{:S(2)}) async-start(bf16[32,32,512]{2,1,0:T(8,128)(2,1)} %col_heads.1), calls=%async_computation.1 | async-start | bytes 2097152 | tf_op jit(solution)/shard_map/all_to_all | solution.py:397
  77.1 2.4 %collective-permute-start.15 = (bf16[2,128,768]{2,1,0:T(8,128)(2,1)}, bf16[2,128,768]{2,1,0:T(8,128)(2,1)S(1)}, u32[]{:S(2)}, u32[]{:S(2)}) collective-permute-start(bf16[2,128,768]{2,1,0:T(8,128)(2,1)} %slice.6.refs_0_), channel_id=1, source_target_pairs={{0,8},{1,9},{2,10},{3,11},{4,12},{5,13},{6,14},{7,15},{8,0},{9,1},... | collective-permute-start | bytes 1179656 | tf_op jit(solution)/shard_map/ppermute | solution.py:46
  77.5 4.5 %collective-permute-start.16 = (bf16[2,128,768]{2,1,0:T(8,128)(2,1)}, bf16[2,128,768]{2,1,0:T(8,128)(2,1)S(1)}, u32[]{:S(2)}, u32[]{:S(2)}) collective-permute-start(bf16[2,128,768]{2,1,0:T(8,128)(2,1)} %collective-permute-done.5.refs_1_), channel_id=1, source_target_pairs={{0,8},{1,9},{2,10},{3,11},{4,12},{5,13},{6,14},{7,15},{8,0},{9,1},... | collective-permute-start | bytes 1179656 | tf_op jit(solution)/shard_map/ppermute | solution.py:46
  77.7 6.2 %collective-permute-start.17 = (bf16[2,128,768]{2,1,0:T(8,128)(2,1)}, bf16[2,128,768]{2,1,0:T(8,128)(2,1)}, u32[]{:S(2)}, u32[]{:S(2)}) collective-permute-start(bf16[2,128,768]{2,1,0:T(8,128)(2,1)} %collective-permute-done.6.refs_2_), channel_id=1, source_target_pairs={{0,8},{1,9},{2,10},{3,11},{4,12},{5,13},{6,14},{7,15},{8,0},{9,1},... | collective-permute-start | bytes 1179656 | tf_op jit(solution)/shard_map/ppermute | solution.py:46
  78.0 5.9 %collective-permute-start.18 = (bf16[2,128,768]{2,1,0:T(8,128)(2,1)}, bf16[2,128,768]{2,1,0:T(8,128)(2,1)}, u32[]{:S(2)}, u32[]{:S(2)}) collective-permute-start(bf16[2,128,768]{2,1,0:T(8,128)(2,1)} %collective-permute-done.7.refs_3_), channel_id=1, source_target_pairs={{0,8},{1,9},{2,10},{3,11},{4,12},{5,13},{6,14},{7,15},{8,0},{9,1},... | collective-permute-start | bytes 1179656 | tf_op jit(solution)/shard_map/ppermute | solution.py:46
  78.2 19.5 %copy-start.5 = (bf16[2,128,512]{2,1,0:T(8,128)(2,1)}, bf16[2,128,512]{2,1,0:T(8,128)(2,1)S(1)}, u32[]{:S(2)}) copy-start(bf16[2,128,512]{2,1,0:T(8,128)(2,1)S(1)} %slice.7.refs_0_) | copy-start | bytes 786436
  78.2 19.4 %collective-permute-start.12 = (bf16[2,128,512]{2,1,0:T(8,128)(2,1)S(1)}, bf16[2,128,512]{2,1,0:T(8,128)(2,1)S(1)}, u32[]{:S(2)}, u32[]{:S(2)}) collective-permute-start(bf16[2,128,512]{2,1,0:T(8,128)(2,1)S(1)} %slice.7.refs_0_), channel_id=1, source_target_pairs={{0,1},{1,2},{2,3},{3,0},{4,5},{5,6},{6,7},{7,4},{8,9},{9,10},{10,1... | collective-permute-start | bytes 786440 | tf_op jit(solution)/shard_map/ppermute | solution.py:46
  79.6 2.4 %copy-start.11 = (bf16[2,128,768]{2,1,0:T(8,128)(2,1)}, bf16[2,128,768]{2,1,0:T(8,128)(2,1)S(1)}, u32[]{:S(2)}) copy-start(bf16[2,128,768]{2,1,0:T(8,128)(2,1)S(1)} %collective-permute-done.15.refs_4_) | copy-start | bytes 1179652
  79.6 18.1 %collective-permute-start.13 = (bf16[2,128,512]{2,1,0:T(8,128)(2,1)S(1)}, bf16[2,128,512]{2,1,0:T(8,128)(2,1)S(1)}, u32[]{:S(2)}, u32[]{:S(2)}) collective-permute-start(bf16[2,128,512]{2,1,0:T(8,128)(2,1)S(1)} %slice.7.refs_0_), channel_id=1, source_target_pairs={{0,2},{1,3},{2,0},{3,1},{4,6},{5,7},{6,4},{7,5},{8,10},{9,11},{10,... | collective-permute-start | bytes 786440 | tf_op jit(solution)/shard_map/ppermute | solution.py:46
  82.0 0.8 copy-start.13
  82.8 14.9 %collective-permute-start.14 = (bf16[2,128,512]{2,1,0:T(8,128)(2,1)S(1)}, bf16[2,128,512]{2,1,0:T(8,128)(2,1)}, u32[]{:S(2)}, u32[]{:S(2)}) collective-permute-start(bf16[2,128,512]{2,1,0:T(8,128)(2,1)S(1)} %slice.7.refs_0_), channel_id=1, source_target_pairs={{0,3},{1,0},{2,1},{3,2},{4,7},{5,4},{6,5},{7,6},{8,11},{9,8},{10,9... | collective-permute-start | bytes 786440 | tf_op jit(solution)/shard_map/ppermute | solution.py:46
  97.7 6.5 %copy-start.14 = (bf16[2,128,512]{2,1,0:T(8,128)(2,1)}, bf16[2,128,512]{2,1,0:T(8,128)(2,1)S(1)}, u32[]{:S(2)}) copy-start(bf16[2,128,512]{2,1,0:T(8,128)(2,1)S(1)} %collective-permute-done.12.refs_1_) | copy-start | bytes 786436
  97.7 6.4 %copy-start.15 = (bf16[2,128,512]{2,1,0:T(8,128)(2,1)}, bf16[2,128,512]{2,1,0:T(8,128)(2,1)S(1)}, u32[]{:S(2)}) copy-start(bf16[2,128,512]{2,1,0:T(8,128)(2,1)S(1)} %collective-permute-done.13.refs_2_) | copy-start | bytes 786436
  97.7 2.4 %collective-permute-start.19 = (bf16[2,128,512]{2,1,0:T(8,128)(2,1)S(1)}, bf16[2,128,512]{2,1,0:T(8,128)(2,1)S(1)}, u32[]{:S(2)}, u32[]{:S(2)}) collective-permute-start(bf16[2,128,512]{2,1,0:T(8,128)(2,1)S(1)} %slice.7.refs_0_), channel_id=1, source_target_pairs={{0,8},{1,9},{2,10},{3,11},{4,12},{5,13},{6,14},{7,15},{8,0},{9,1},... | collective-permute-start | bytes 786440 | tf_op jit(solution)/shard_map/ppermute | solution.py:46
  98.9 1.5 %collective-permute-start.20 = (bf16[2,128,512]{2,1,0:T(8,128)(2,1)S(1)}, bf16[2,128,512]{2,1,0:T(8,128)(2,1)S(1)}, u32[]{:S(2)}, u32[]{:S(2)}) collective-permute-start(bf16[2,128,512]{2,1,0:T(8,128)(2,1)S(1)} %collective-permute-done.12.refs_1_), channel_id=1, source_target_pairs={{0,8},{1,9},{2,10},{3,11},{4,12},{5,13},{6,14},{7,15},{8,0},{9,1},... | collective-permute-start | bytes 786440 | tf_op jit(solution)/shard_map/ppermute | solution.py:46
  99.0 2.2 %collective-permute-start.21 = (bf16[2,128,512]{2,1,0:T(8,128)(2,1)S(1)}, bf16[2,128,512]{2,1,0:T(8,128)(2,1)S(1)}, u32[]{:S(2)}, u32[]{:S(2)}) collective-permute-start(bf16[2,128,512]{2,1,0:T(8,128)(2,1)S(1)} %collective-permute-done.13.refs_2_), channel_id=1, source_target_pairs={{0,8},{1,9},{2,10},{3,11},{4,12},{5,13},{6,14},{7,15},{8,0},{9,1},... | collective-permute-start | bytes 786440 | tf_op jit(solution)/shard_map/ppermute | solution.py:46
  99.5 2.5 %collective-permute-start.22 = (bf16[2,128,512]{2,1,0:T(8,128)(2,1)}, bf16[2,128,512]{2,1,0:T(8,128)(2,1)}, u32[]{:S(2)}, u32[]{:S(2)}) collective-permute-start(bf16[2,128,512]{2,1,0:T(8,128)(2,1)} %collective-permute-done.14.refs_3_), channel_id=1, source_target_pairs={{0,8},{1,9},{2,10},{3,11},{4,12},{5,13},{6,14},{7,15},{8,0},{9,1},... | collective-permute-start | bytes 786440 | tf_op jit(solution)/shard_map/ppermute | solution.py:46
  100.1 1.1 %copy-start.16 = (bf16[2,128,512]{2,1,0:T(8,128)(2,1)}, bf16[2,128,512]{2,1,0:T(8,128)(2,1)S(1)}, u32[]{:S(2)}) copy-start(bf16[2,128,512]{2,1,0:T(8,128)(2,1)S(1)} %collective-permute-done.19.refs_4_) | copy-start | bytes 786436
  100.5 0.8 copy-start.17
  101.2 0.7 copy-start.18

commit v7 on v6

--- a/solution.py
+++ b/solution.py
@@ -264,28 +264,19 @@
         copy.wait()
 
 
-def out_kernel(row_hbm, col_hbm, *refs):
-    o_hbm, row, col, w, out, sems, sems_r, sems_c, sems_o = refs[8:]
+def out_kernel(row, col, *refs):
+    o_hbm, w, out, sems, sems_o = refs[8:]
     block = 256
-    weights = fetch_weights(refs[:8], w, sems)
-    rows, cols, outs = [], [], []
-    for i in range(STRIDE // block):
-        at = pl.ds(i * block, block)
-        rows.append(pltpu.make_async_copy(row_hbm.at[at, :], row.at[at, :], sems_r.at[i]))
-        cols.append(pltpu.make_async_copy(col_hbm.at[at, :], col.at[at, :], sems_c.at[i]))
-        outs.append(pltpu.make_async_copy(out.at[at, :], o_hbm.at[at, :], sems_o.at[i]))
-        rows[i].start()
-        cols[i].start()
-    for copy in weights:
+    outs = []
+    for copy in fetch_weights(refs[:8], w, sems):
         copy.wait()
     for i in range(STRIDE // block):
         at = slice(i * block, (i + 1) * block)
-        rows[i].wait()
-        cols[i].wait()
         for half in range(2):
             total = jnp.dot(row[at, :], w[half, :HALF, :], preferred_element_type=F32)
             total += jnp.dot(col[at, :], w[half, HALF:, :], preferred_element_type=F32)
             out[at, half * 512 : (half + 1) * 512] = total.astype(BF16)
+        outs.append(pltpu.make_async_copy(out.at[at, :], o_hbm.at[at, :], sems_o.at[i]))
         outs[i].start()
     for copy in outs:
         copy.wait()
@@ -319,7 +310,7 @@
         row_kernel,
         out_shape=jax.ShapeDtypeStruct((STRIDE, HALF), BF16),
         in_specs=[FAR] + [ANY] * 8,
-        out_specs=FAR,
+        out_specs=ANY,
         scratch_shapes=[
             pltpu.VMEM((STRIDE, D), BF16),
             pltpu.VMEM((2, D, QKV), BF16),
@@ -331,7 +322,7 @@
             DMA((4,)),
             DMA((4,)),
         ],
-        compiler_params=limit(63),
+        compiler_params=limit(48),
         cost_estimate=pl.CostEstimate(
             flops=6_000_000_000, bytes_accessed=6 << 20, transcendentals=5_000_000
         ),
@@ -370,19 +361,15 @@
     return pl.pallas_call(
         out_kernel,
         out_shape=jax.ShapeDtypeStruct((STRIDE, D), BF16),
-        in_specs=[FAR] * 2 + [ANY] * 8,
+        in_specs=[WHOLE] * 2 + [ANY] * 8,
         out_specs=FAR,
         scratch_shapes=[
-            pltpu.VMEM((STRIDE, HALF), BF16),
-            pltpu.VMEM((STRIDE, HALF), BF16),
             pltpu.VMEM((2, D, OUT), BF16),
             pltpu.VMEM((STRIDE, D), BF16),
             DMA((16,)),
             DMA((4,)),
-            DMA((4,)),
-            DMA((4,)),
         ],
-        compiler_params=limit(63),
+        compiler_params=limit(24),
         cost_estimate=pl.CostEstimate(
             flops=2_000_000_000, bytes_accessed=6 << 20, transcendentals=0
         ),

time: 111 us -> 112 us (level)
  Pallas kernels: 30.5 us -> 32.4 us
  waiting for transfers between devices: 36.3 us -> 34.4 us
    pallas_call x1, Pallas kernels: 13.7 us -> 15.4 us  [row_heads(): pl.pallas_call(row_kernel, out_shape=jax.ShapeDtypeStruct((STRIDE, HALF),...]
    all_to_all x2, waiting for transfers between devices: 14.3 us -> 12.7 us  [exchange(): lax.all_to_all(blocks, 'seq', split_axis=0, concat_axis=0, tiled=True, ax...]
    unnamed x38 -> x28, local copies, waits for them, and re-layouts: 2.31 us -> 2.97 us
  transfers between devices with their start and end apart: 25 -> 25, of which waited for: 10 -> 11; matrix products, arithmetic and copies ran while one was open for 1% -> 1% of each run, Pallas kernels for 22% -> 24%
where the time goes in v7:
time: 112 us; the launch traced here: 111 us
  starting transfers between devices  39.6 us (35%)
  waiting for transfers between devices  34.4 us (31%)
  Pallas kernels  32.4 us (29%)
  local copies, waits for them, and re-layouts  3.96 us (4%)
    ppermute x23, starting transfers between devices, send(): return lax.ppermute(value, BOTH, where)  23.2 us
    ppermute x23, waiting for transfers between devices, send(): return lax.ppermute(value, BOTH, where)  21.7 us
    all_to_all x2, starting transfers between devices, exchange(): lax.all_to_all(blocks, 'seq', split_axis=0, concat_axis=0, tiled=True, ax...  16.4 us
    pallas_call x1, Pallas kernels, row_heads(): pl.pallas_call(row_kernel, out_shape=jax.ShapeDtypeStruct((STRIDE, HALF),...  15.4 us
    all_to_all x2, waiting for transfers between devices, exchange(): lax.all_to_all(blocks, 'seq', split_axis=0, concat_axis=0, tiled=True, ax...  12.7 us
    pallas_call x1, Pallas kernels, col_heads(): pl.pallas_call(col_kernel, out_shape=jax.ShapeDtypeStruct((rows, cols, HA...  10.8 us
    pallas_call x1, Pallas kernels, project_out(): pl.pallas_call(out_kernel, out_shape=jax.ShapeDtypeStruct((STRIDE, D), BF...  6.03 us
    unnamed x28, local copies, waits for them, and re-layouts  2.97 us
  transfers between devices with their start and end apart: 25, of which 11 were waited for; matrix products, arithmetic and copies ran while one was open for 1% of the time, Pallas kernels for 24%

profile of v7, /device:TPU:1, one launch (start us, length us, event | category | flops | bytes accessed | tf_op | source)
XLA Modules:
  0.0 111.5 jit_solution(8876815425166416060)
XLA Ops:
  0.0 11.3 %all-to-all-start = ((bf16[32,32,1024]{2,1,0:T(8,128)(2,1)}), bf16[32,32,1024]{2,1,0:T(8,128)(2,1)}, u32[]{:S(2)}, u32[]{:S(2)}) async-start(bf16[32,32,1024]{2,1,0:T(8,128)(2,1)} %bitcast.11), calls=%async_computation | async-start | bytes 4194304 | tf_op jit(solution)/shard_map/all_to_all | solution.py:384
  12.0 0.2 rebuilt_half.1
  12.2 2.9 %collective-permute-start.1 = (bf16[128,768]{1,0:T(8,128)(2,1)S(1)}, bf16[128,768]{1,0:T(8,128)(2,1)S(1)}, u32[]{:S(2)}, u32[]{:S(2)}) collective-permute-start(bf16[128,768]{1,0:T(8,128)(2,1)S(1)} %get-tuple-element.24), channel_id=1, source_target_pairs={{0,132},{1,133},{2,134},{3,135},{4,128},{5,129},{6,130},{7,131},{8... | collective-permute-start | bytes 589832 | tf_op jit(solution)/shard_map/ppermute | solution.py:46
  15.1 0.1 collective-permute-start
  15.2 4.9 %collective-permute-done.1 = bf16[128,768]{1,0:T(8,128)(2,1)S(1)} collective-permute-done((bf16[128,768]{1,0:T(8,128)(2,1)S(1)}, bf16[128,768]{1,0:T(8,128)(2,1)S(1)}, u32[]{:S(2)}, u32[]{:S(2)}) %collective-permute-start.1) | collective-permute-done | bytes 196640 | tf_op jit(solution)/shard_map/ppermute | solution.py:46
  20.2 1.3 %collective-permute-start.2 = (bf16[2,128,768]{2,1,0:T(8,128)(2,1)S(1)}, bf16[2,128,768]{2,1,0:T(8,128)(2,1)S(1)}, u32[]{:S(2)}, u32[]{:S(2)}) collective-permute-start(bf16[2,128,768]{2,1,0:T(8,128)(2,1)S(1)} %pad_maximum_fusion.1.refs_0_), channel_id=1, source_target_pairs={{0,1},{1,2},{2,3},{3,0},{4,5},{5,6},{6,7},{7,4},{8,9},{9,10},{10,1... | collective-permute-start | bytes 1179656 | tf_op jit(solution)/shard_map/ppermute | solution.py:46
  21.5 2.5 %collective-permute-start.3 = (bf16[2,128,768]{2,1,0:T(8,128)(2,1)S(1)}, bf16[2,128,768]{2,1,0:T(8,128)(2,1)S(1)}, u32[]{:S(2)}, u32[]{:S(2)}) collective-permute-start(bf16[2,128,768]{2,1,0:T(8,128)(2,1)S(1)} %pad_maximum_fusion.1.refs_0_), channel_id=1, source_target_pairs={{0,2},{1,3},{2,0},{3,1},{4,6},{5,7},{6,4},{7,5},{8,10},{9,11},{10,... | collective-permute-start | bytes 1179656 | tf_op jit(solution)/shard_map/ppermute | solution.py:46
  23.9 1.2 %collective-permute-start.4 = (bf16[2,128,768]{2,1,0:T(8,128)(2,1)S(1)}, bf16[2,128,768]{2,1,0:T(8,128)(2,1)S(1)}, u32[]{:S(2)}, u32[]{:S(2)}) collective-permute-start(bf16[2,128,768]{2,1,0:T(8,128)(2,1)S(1)} %pad_maximum_fusion.1.refs_0_), channel_id=1, source_target_pairs={{0,3},{1,0},{2,1},{3,2},{4,7},{5,4},{6,5},{7,6},{8,11},{9,8},{10,9... | collective-permute-start | bytes 1179656 | tf_op jit(solution)/shard_map/ppermute | solution.py:46
  25.1 2.1 %collective-permute-done = bf16[128,1280]{1,0:T(8,128)(2,1)S(1)} collective-permute-done((bf16[128,1280]{1,0:T(8,128)(2,1)S(1)}, bf16[128,1280]{1,0:T(8,128)(2,1)S(1)}, u32[]{:S(2)}, u32[]{:S(2)}) %collective-permute-start) | collective-permute-done | bytes 327712 | tf_op jit(solution)/shard_map/ppermute | solution.py:46
  27.2 0.1 pad_maximum_fusion
  27.2 0.0 copy-start.6
  27.2 3.5 %collective-permute-done.2.refs_1_ = bf16[2,128,768]{2,1,0:T(8,128)(2,1)S(1)} collective-permute-done((bf16[2,128,768]{2,1,0:T(8,128)(2,1)S(1)}, bf16[2,128,768]{2,1,0:T(8,128)(2,1)S(1)}, u32[]{:S(2)}, u32[]{:S(2)}) %collective-permute-start.2) | collective-permute-done | bytes 393248 | tf_op jit(solution)/shard_map/ppermute | solution.py:46
  30.8 9.4 %collective-permute-done.3.refs_2_ = bf16[2,128,768]{2,1,0:T(8,128)(2,1)S(1)} collective-permute-done((bf16[2,128,768]{2,1,0:T(8,128)(2,1)S(1)}, bf16[2,128,768]{2,1,0:T(8,128)(2,1)S(1)}, u32[]{:S(2)}, u32[]{:S(2)}) %collective-permute-start.3) | collective-permute-done | bytes 393248 | tf_op jit(solution)/shard_map/ppermute | solution.py:46
  40.2 0.3 collective-permute-done.4.refs_3_
  40.5 2.0 %collective-permute-start.10 = (bf16[2,128,768]{2,1,0:T(8,128)(2,1)S(1)}, bf16[2,128,768]{2,1,0:T(8,128)(2,1)S(1)}, u32[]{:S(2)}, u32[]{:S(2)}) collective-permute-start(bf16[2,128,768]{2,1,0:T(8,128)(2,1)S(1)} %collective-permute-done.3.refs_2_), channel_id=1, source_target_pairs={{0,8},{1,9},{2,10},{3,11},{4,12},{5,13},{6,14},{7,15},{8,0},{9,1},... | collective-permute-start | bytes 1179656 | tf_op jit(solution)/shard_map/ppermute | solution.py:46
  42.5 0.1 collective-permute-start.11
  42.6 0.4 collective-permute-start.8
  43.0 0.1 collective-permute-start.9
  43.2 1.0 collective-permute-start.5
  44.1 0.0 collective-permute-done.10.refs_6_
  44.1 2.2 %collective-permute-start.6 = (bf16[2,128,768]{2,1,0:T(8,128)(2,1)S(1)}, bf16[2,128,768]{2,1,0:T(8,128)(2,1)}, u32[]{:S(2)}, u32[]{:S(2)}) collective-permute-start(bf16[2,128,768]{2,1,0:T(8,128)(2,1)S(1)} %slice.6.refs_0_), channel_id=1, source_target_pairs={{0,2},{1,3},{2,0},{3,1},{4,6},{5,7},{6,4},{7,5},{8,10},{9,11},{10,... | collective-permute-start | bytes 1179656 | tf_op jit(solution)/shard_map/ppermute | solution.py:46
  46.4 1.4 %collective-permute-start.7 = (bf16[2,128,768]{2,1,0:T(8,128)(2,1)S(1)}, bf16[2,128,768]{2,1,0:T(8,128)(2,1)}, u32[]{:S(2)}, u32[]{:S(2)}) collective-permute-start(bf16[2,128,768]{2,1,0:T(8,128)(2,1)S(1)} %slice.6.refs_0_), channel_id=1, source_target_pairs={{0,3},{1,0},{2,1},{3,2},{4,7},{5,4},{6,5},{7,6},{8,11},{9,8},{10,9... | collective-permute-start | bytes 1179656 | tf_op jit(solution)/shard_map/ppermute | solution.py:46
  47.8 0.7 copy-done.13
  48.6 12.6 %all-to-all-done.x_hbm = bf16[32,32,1024]{2,1,0:T(8,128)(2,1)} async-done(((bf16[32,32,1024]{2,1,0:T(8,128)(2,1)}), bf16[32,32,1024]{2,1,0:T(8,128)(2,1)}, u32[]{:S(2)}, u32[]{:S(2)}) %all-to-all-start) | async-done | bytes 2097184 | tf_op jit(solution)/shard_map/all_to_all | solution.py:384
  61.2 10.8 %col_heads.1 = bf16[32,32,512]{2,1,0:T(8,128)(2,1)} custom-call(bf16[32,32,1024]{2,1,0:T(8,128)(2,1)} %all-to-all-done.x_hbm, bf16[2,128,768]{2,1,0:T(8,128)(2,1)} %copy-done.7, bf16[2,128,768]{2,1,0:T(8,128)(2,1)} %copy-done.8, bf16[2,128,768]{2,1,0:T(8,128)(2,1)} %copy-done.9, bf16[2,128,768]{2,1,0:T(8,128)(2,1)} %copy-done.10, ...), custom_call_target="tpu_custom_call" | custom-call | flops 4000000000 | bytes 6291456 | tf_op jit(solution)/shard_map/col_heads/pallas_call | solution.py:335
  72.0 5.1 %all-to-all-start.1 = ((bf16[32,32,512]{2,1,0:T(8,128)(2,1)}), bf16[32,32,512]{2,1,0:T(8,128)(2,1)S(1)}, u32[]{:S(2)}, u32[]{:S(2)}) async-start(bf16[32,32,512]{2,1,0:T(8,128)(2,1)} %col_heads.1), calls=%async_computation.1 | async-start | bytes 2097152 | tf_op jit(solution)/shard_map/all_to_all | solution.py:384
  77.1 0.3 collective-permute-start.15
  77.4 0.3 collective-permute-start.16
  77.7 0.2 collective-permute-start.17
  77.9 0.3 collective-permute-start.18
  78.2 1.0 slice.7.refs_0_
  79.2 1.3 %collective-permute-start.12 = (bf16[2,128,512]{2,1,0:T(8,128)(2,1)S(1)}, bf16[2,128,512]{2,1,0:T(8,128)(2,1)S(1)}, u32[]{:S(2)}, u32[]{:S(2)}) collective-permute-start(bf16[2,128,512]{2,1,0:T(8,128)(2,1)S(1)} %slice.7.refs_0_), channel_id=1, source_target_pairs={{0,1},{1,2},{2,3},{3,0},{4,5},{5,6},{6,7},{7,4},{8,9},{9,10},{10,1... | collective-permute-start | bytes 786440 | tf_op jit(solution)/shard_map/ppermute | solution.py:46
  80.5 2.4 %collective-permute-start.13 = (bf16[2,128,512]{2,1,0:T(8,128)(2,1)S(1)}, bf16[2,128,512]{2,1,0:T(8,128)(2,1)S(1)}, u32[]{:S(2)}, u32[]{:S(2)}) collective-permute-start(bf16[2,128,512]{2,1,0:T(8,128)(2,1)S(1)} %slice.7.refs_0_), channel_id=1, source_target_pairs={{0,2},{1,3},{2,0},{3,1},{4,6},{5,7},{6,4},{7,5},{8,10},{9,11},{10,... | collective-permute-start | bytes 786440 | tf_op jit(solution)/shard_map/ppermute | solution.py:46
  82.9 1.2 %collective-permute-start.14 = (bf16[2,128,512]{2,1,0:T(8,128)(2,1)S(1)}, bf16[2,128,512]{2,1,0:T(8,128)(2,1)S(1)}, u32[]{:S(2)}, u32[]{:S(2)}) collective-permute-start(bf16[2,128,512]{2,1,0:T(8,128)(2,1)S(1)} %slice.7.refs_0_), channel_id=1, source_target_pairs={{0,3},{1,0},{2,1},{3,2},{4,7},{5,4},{6,5},{7,6},{8,11},{9,8},{10,9... | collective-permute-start | bytes 786440 | tf_op jit(solution)/shard_map/ppermute | solution.py:46
  84.1 15.4 %row_heads.1.row = bf16[1024,512]{1,0:T(8,128)(2,1)S(1)} custom-call(bf16[1024,1024]{1,0:T(8,128)(2,1)} %bitcast.12, bf16[2,128,768]{2,1,0:T(8,128)(2,1)S(1)} %slice.6.refs_0_, bf16[2,128,768]{2,1,0:T(8,128)(2,1)S(1)} %collective-permute-done.5.refs_1_, bf16[2,128,768]{2,1,0:T(8,128)(2,1)} %collective-permute-done.6.refs_2_, ...), custom_call_target="tpu_custom_call" | custom-call | flops 6000000000 | bytes 6291456 | tf_op jit(solution)/shard_map/row_heads/pallas_call | solution.py:309
  99.5 0.0 copy-start.4
  99.5 1.0 copy-done.4
  100.5 1.2 %collective-permute-start.19 = (bf16[2,128,512]{2,1,0:T(8,128)(2,1)S(1)}, bf16[2,128,512]{2,1,0:T(8,128)(2,1)S(1)}, u32[]{:S(2)}, u32[]{:S(2)}) collective-permute-start(bf16[2,128,512]{2,1,0:T(8,128)(2,1)S(1)} %slice.7.refs_0_), channel_id=1, source_target_pairs={{0,8},{1,9},{2,10},{3,11},{4,12},{5,13},{6,14},{7,15},{8,0},{9,1},... | collective-permute-start | bytes 786440 | tf_op jit(solution)/shard_map/ppermute | solution.py:46
  101.6 0.4 collective-permute-start.20
  102.0 0.1 collective-permute-start.21
  102.1 0.4 collective-permute-start.22
  102.5 0.3 collective-permute-done.19.refs_4_
  102.8 0.4 collective-permute-done.20.refs_5_
  103.2 0.4 collective-permute-done.21.refs_6_
  103.5 0.4 collective-permute-done.22.refs_7_
  103.9 0.1 all-to-all-done.1
  104.0 1.2 %copy-done.5 = bf16[1024,512]{1,0:T(8,128)(2,1)S(1)} copy-done((bf16[1024,512]{1,0:T(8,128)(2,1)S(1)}, bf16[1024,512]{1,0:T(8,128)(2,1)}, u32[]{:S(2)}) %copy-start.5) | copy-done | bytes 1048600
  105.3 6.0 %project_out.1 = bf16[1024,1024]{1,0:T(8,128)(2,1)} custom-call(bf16[1024,512]{1,0:T(8,128)(2,1)S(1)} %copy-done.5, bf16[1024,512]{1,0:T(8,128)(2,1)S(1)} %bitcast.8, bf16[2,128,512]{2,1,0:T(8,128)(2,1)S(1)} %slice.7.refs_0_, bf16[2,128,512]{2,1,0:T(8,128)(2,1)S(1)} %collective-permute-done.12.refs_1_, ...), custom_call_target="tpu_custom_call" | custom-call | flops 2000000000 | bytes 6291456 | tf_op jit(solution)/shard_map/project_out/pallas_call | solution.py:361
  (38 shorter events, 0.1 us)
Async XLA Ops:
  0.0 12.0 %copy-start = (bf16[128,3072]{1,0:T(8,128)(2,1)S(1)}, bf16[128,3072]{1,0:T(8,128)(2,1)}, u32[]{:S(2)}) copy-start(bf16[128,3072]{1,0:T(8,128)(2,1)} %qb_ref.1) | copy-start | bytes 2359300
  0.0 12.0 %copy-start.1 = (bf16[128,3072]{1,0:T(8,128)(2,1)S(1)}, bf16[128,3072]{1,0:T(8,128)(2,1)}, u32[]{:S(2)}) copy-start(bf16[128,3072]{1,0:T(8,128)(2,1)} %qd_ref.1) | copy-start | bytes 2359300
  0.0 12.0 %copy-start.2 = (bf16[128,1024]{1,0:T(8,128)(2,1)S(1)}, bf16[128,1024]{1,0:T(8,128)(2,1)}, u32[]{:S(2)}) copy-start(bf16[128,1024]{1,0:T(8,128)(2,1)} %ob_ref.1) | copy-start | bytes 786436
  0.0 12.0 %copy-start.3 = (bf16[128,1024]{1,0:T(8,128)(2,1)S(1)}, bf16[128,1024]{1,0:T(8,128)(2,1)}, u32[]{:S(2)}) copy-start(bf16[128,1024]{1,0:T(8,128)(2,1)} %od_ref.1) | copy-start | bytes 786436
  0.0 61.2 %all-to-all-start = ((bf16[32,32,1024]{2,1,0:T(8,128)(2,1)}), bf16[32,32,1024]{2,1,0:T(8,128)(2,1)}, u32[]{:S(2)}, u32[]{:S(2)}) async-start(bf16[32,32,1024]{2,1,0:T(8,128)(2,1)} %bitcast.11), calls=%async_computation | async-start | bytes 4194304 | tf_op jit(solution)/shard_map/all_to_all | solution.py:384
  12.2 7.9 %collective-permute-start.1 = (bf16[128,768]{1,0:T(8,128)(2,1)S(1)}, bf16[128,768]{1,0:T(8,128)(2,1)S(1)}, u32[]{:S(2)}, u32[]{:S(2)}) collective-permute-start(bf16[128,768]{1,0:T(8,128)(2,1)S(1)} %get-tuple-element.24), channel_id=1, source_target_pairs={{0,132},{1,133},{2,134},{3,135},{4,128},{5,129},{6,130},{7,131},{8... | collective-permute-start | bytes 589832 | tf_op jit(solution)/shard_map/ppermute | solution.py:46
  15.1 12.0 %collective-permute-start = (bf16[128,1280]{1,0:T(8,128)(2,1)S(1)}, bf16[128,1280]{1,0:T(8,128)(2,1)S(1)}, u32[]{:S(2)}, u32[]{:S(2)}) collective-permute-start(bf16[128,1280]{1,0:T(8,128)(2,1)S(1)} %get-tuple-element.23), channel_id=1, source_target_pairs={{0,132},{1,133},{2,134},{3,135},{4,128},{5,129},{6,130},{7,131},{8... | collective-permute-start | bytes 983048 | tf_op jit(solution)/shard_map/ppermute | solution.py:46
  20.2 26.2 %copy-start.7 = (bf16[2,128,768]{2,1,0:T(8,128)(2,1)}, bf16[2,128,768]{2,1,0:T(8,128)(2,1)S(1)}, u32[]{:S(2)}) copy-start(bf16[2,128,768]{2,1,0:T(8,128)(2,1)S(1)} %pad_maximum_fusion.1.refs_0_) | copy-start | bytes 1179652
  20.2 10.6 %collective-permute-start.2 = (bf16[2,128,768]{2,1,0:T(8,128)(2,1)S(1)}, bf16[2,128,768]{2,1,0:T(8,128)(2,1)S(1)}, u32[]{:S(2)}, u32[]{:S(2)}) collective-permute-start(bf16[2,128,768]{2,1,0:T(8,128)(2,1)S(1)} %pad_maximum_fusion.1.refs_0_), channel_id=1, source_target_pairs={{0,1},{1,2},{2,3},{3,0},{4,5},{5,6},{6,7},{7,4},{8,9},{9,10},{10,1... | collective-permute-start | bytes 1179656 | tf_op jit(solution)/shard_map/ppermute | solution.py:46
  21.5 18.7 %collective-permute-start.3 = (bf16[2,128,768]{2,1,0:T(8,128)(2,1)S(1)}, bf16[2,128,768]{2,1,0:T(8,128)(2,1)S(1)}, u32[]{:S(2)}, u32[]{:S(2)}) collective-permute-start(bf16[2,128,768]{2,1,0:T(8,128)(2,1)S(1)} %pad_maximum_fusion.1.refs_0_), channel_id=1, source_target_pairs={{0,2},{1,3},{2,0},{3,1},{4,6},{5,7},{6,4},{7,5},{8,10},{9,11},{10,... | collective-permute-start | bytes 1179656 | tf_op jit(solution)/shard_map/ppermute | solution.py:46
  23.9 16.6 %collective-permute-start.4 = (bf16[2,128,768]{2,1,0:T(8,128)(2,1)S(1)}, bf16[2,128,768]{2,1,0:T(8,128)(2,1)S(1)}, u32[]{:S(2)}, u32[]{:S(2)}) collective-permute-start(bf16[2,128,768]{2,1,0:T(8,128)(2,1)S(1)} %pad_maximum_fusion.1.refs_0_), channel_id=1, source_target_pairs={{0,3},{1,0},{2,1},{3,2},{4,7},{5,4},{6,5},{7,6},{8,11},{9,8},{10,9... | collective-permute-start | bytes 1179656 | tf_op jit(solution)/shard_map/ppermute | solution.py:46
  27.2 19.1 %copy-start.6 = (bf16[2,128,1280]{2,1,0:T(8,128)(2,1)}, bf16[2,128,1280]{2,1,0:T(8,128)(2,1)S(1)}, u32[]{:S(2)}) copy-start(bf16[2,128,1280]{2,1,0:T(8,128)(2,1)S(1)} %pad_maximum_fusion) | copy-start | bytes 1966084
  30.8 17.0 %copy-start.8 = (bf16[2,128,768]{2,1,0:T(8,128)(2,1)}, bf16[2,128,768]{2,1,0:T(8,128)(2,1)S(1)}, u32[]{:S(2)}) copy-start(bf16[2,128,768]{2,1,0:T(8,128)(2,1)S(1)} %collective-permute-done.2.refs_1_) | copy-start | bytes 1179652
  40.2 7.6 %copy-start.9 = (bf16[2,128,768]{2,1,0:T(8,128)(2,1)}, bf16[2,128,768]{2,1,0:T(8,128)(2,1)S(1)}, u32[]{:S(2)}) copy-start(bf16[2,128,768]{2,1,0:T(8,128)(2,1)S(1)} %collective-permute-done.3.refs_2_) | copy-start | bytes 1179652
  40.5 7.3 %copy-start.10 = (bf16[2,128,768]{2,1,0:T(8,128)(2,1)}, bf16[2,128,768]{2,1,0:T(8,128)(2,1)S(1)}, u32[]{:S(2)}) copy-start(bf16[2,128,768]{2,1,0:T(8,128)(2,1)S(1)} %collective-permute-done.4.refs_3_) | copy-start | bytes 1179652
  40.5 3.6 %collective-permute-start.10 = (bf16[2,128,768]{2,1,0:T(8,128)(2,1)S(1)}, bf16[2,128,768]{2,1,0:T(8,128)(2,1)S(1)}, u32[]{:S(2)}, u32[]{:S(2)}) collective-permute-start(bf16[2,128,768]{2,1,0:T(8,128)(2,1)S(1)} %collective-permute-done.3.refs_2_), channel_id=1, source_target_pairs={{0,8},{1,9},{2,10},{3,11},{4,12},{5,13},{6,14},{7,15},{8,0},{9,1},... | collective-permute-start | bytes 1179656 | tf_op jit(solution)/shard_map/ppermute | solution.py:46
  42.5 3.8 %collective-permute-start.11 = (bf16[2,128,768]{2,1,0:T(8,128)(2,1)S(1)}, bf16[2,128,768]{2,1,0:T(8,128)(2,1)S(1)}, u32[]{:S(2)}, u32[]{:S(2)}) collective-permute-start(bf16[2,128,768]{2,1,0:T(8,128)(2,1)S(1)} %collective-permute-done.4.refs_3_), channel_id=1, source_target_pairs={{0,8},{1,9},{2,10},{3,11},{4,12},{5,13},{6,14},{7,15},{8,0},{9,1},... | collective-permute-start | bytes 1179656 | tf_op jit(solution)/shard_map/ppermute | solution.py:46
  42.6 5.2 %collective-permute-start.8 = (bf16[2,128,768]{2,1,0:T(8,128)(2,1)S(1)}, bf16[2,128,768]{2,1,0:T(8,128)(2,1)S(1)}, u32[]{:S(2)}, u32[]{:S(2)}) collective-permute-start(bf16[2,128,768]{2,1,0:T(8,128)(2,1)S(1)} %pad_maximum_fusion.1.refs_0_), channel_id=1, source_target_pairs={{0,8},{1,9},{2,10},{3,11},{4,12},{5,13},{6,14},{7,15},{8,0},{9,1},... | collective-permute-start | bytes 1179656 | tf_op jit(solution)/shard_map/ppermute | solution.py:46
  43.0 5.5 %collective-permute-start.9 = (bf16[2,128,768]{2,1,0:T(8,128)(2,1)S(1)}, bf16[2,128,768]{2,1,0:T(8,128)(2,1)}, u32[]{:S(2)}, u32[]{:S(2)}) collective-permute-start(bf16[2,128,768]{2,1,0:T(8,128)(2,1)S(1)} %collective-permute-done.2.refs_1_), channel_id=1, source_target_pairs={{0,8},{1,9},{2,10},{3,11},{4,12},{5,13},{6,14},{7,15},{8,0},{9,1},... | collective-permute-start | bytes 1179656 | tf_op jit(solution)/shard_map/ppermute | solution.py:46
  43.2 28.8 %collective-permute-start.5 = (bf16[2,128,768]{2,1,0:T(8,128)(2,1)S(1)}, bf16[2,128,768]{2,1,0:T(8,128)(2,1)S(1)}, u32[]{:S(2)}, u32[]{:S(2)}) collective-permute-start(bf16[2,128,768]{2,1,0:T(8,128)(2,1)S(1)} %slice.6.refs_0_), channel_id=1, source_target_pairs={{0,1},{1,2},{2,3},{3,0},{4,5},{5,6},{6,7},{7,4},{8,9},{9,10},{10,1... | collective-permute-start | bytes 1179656 | tf_op jit(solution)/shard_map/ppermute | solution.py:46
  44.1 3.7 %copy-start.11 = (bf16[2,128,768]{2,1,0:T(8,128)(2,1)}, bf16[2,128,768]{2,1,0:T(8,128)(2,1)S(1)}, u32[]{:S(2)}) copy-start(bf16[2,128,768]{2,1,0:T(8,128)(2,1)S(1)} %collective-permute-done.10.refs_6_) | copy-start | bytes 1179652
  44.1 27.9 %collective-permute-start.6 = (bf16[2,128,768]{2,1,0:T(8,128)(2,1)S(1)}, bf16[2,128,768]{2,1,0:T(8,128)(2,1)}, u32[]{:S(2)}, u32[]{:S(2)}) collective-permute-start(bf16[2,128,768]{2,1,0:T(8,128)(2,1)S(1)} %slice.6.refs_0_), channel_id=1, source_target_pairs={{0,2},{1,3},{2,0},{3,1},{4,6},{5,7},{6,4},{7,5},{8,10},{9,11},{10,... | collective-permute-start | bytes 1179656 | tf_op jit(solution)/shard_map/ppermute | solution.py:46
  46.4 1.5 %copy-start.12 = (bf16[2,128,768]{2,1,0:T(8,128)(2,1)}, bf16[2,128,768]{2,1,0:T(8,128)(2,1)S(1)}, u32[]{:S(2)}) copy-start(bf16[2,128,768]{2,1,0:T(8,128)(2,1)S(1)} %collective-permute-done.11.refs_7_) | copy-start | bytes 1179652
  46.4 25.6 %collective-permute-start.7 = (bf16[2,128,768]{2,1,0:T(8,128)(2,1)S(1)}, bf16[2,128,768]{2,1,0:T(8,128)(2,1)}, u32[]{:S(2)}, u32[]{:S(2)}) collective-permute-start(bf16[2,128,768]{2,1,0:T(8,128)(2,1)S(1)} %slice.6.refs_0_), channel_id=1, source_target_pairs={{0,3},{1,0},{2,1},{3,2},{4,7},{5,4},{6,5},{7,6},{8,11},{9,8},{10,9... | collective-permute-start | bytes 1179656 | tf_op jit(solution)/shard_map/ppermute | solution.py:46
  47.8 0.7 copy-start.13
  72.0 32.0 %all-to-all-start.1 = ((bf16[32,32,512]{2,1,0:T(8,128)(2,1)}), bf16[32,32,512]{2,1,0:T(8,128)(2,1)S(1)}, u32[]{:S(2)}, u32[]{:S(2)}) async-start(bf16[32,32,512]{2,1,0:T(8,128)(2,1)} %col_heads.1), calls=%async_computation.1 | async-start | bytes 2097152 | tf_op jit(solution)/shard_map/all_to_all | solution.py:384
  77.1 3.4 %collective-permute-start.15 = (bf16[2,128,768]{2,1,0:T(8,128)(2,1)S(1)}, bf16[2,128,768]{2,1,0:T(8,128)(2,1)S(1)}, u32[]{:S(2)}, u32[]{:S(2)}) collective-permute-start(bf16[2,128,768]{2,1,0:T(8,128)(2,1)S(1)} %slice.6.refs_0_), channel_id=1, source_target_pairs={{0,8},{1,9},{2,10},{3,11},{4,12},{5,13},{6,14},{7,15},{8,0},{9,1},... | collective-permute-start | bytes 1179656 | tf_op jit(solution)/shard_map/ppermute | solution.py:46
  77.4 5.5 %collective-permute-start.16 = (bf16[2,128,768]{2,1,0:T(8,128)(2,1)S(1)}, bf16[2,128,768]{2,1,0:T(8,128)(2,1)S(1)}, u32[]{:S(2)}, u32[]{:S(2)}) collective-permute-start(bf16[2,128,768]{2,1,0:T(8,128)(2,1)S(1)} %collective-permute-done.5.refs_1_), channel_id=1, source_target_pairs={{0,8},{1,9},{2,10},{3,11},{4,12},{5,13},{6,14},{7,15},{8,0},{9,1},... | collective-permute-start | bytes 1179656 | tf_op jit(solution)/shard_map/ppermute | solution.py:46
  77.7 6.4 %collective-permute-start.17 = (bf16[2,128,768]{2,1,0:T(8,128)(2,1)}, bf16[2,128,768]{2,1,0:T(8,128)(2,1)S(1)}, u32[]{:S(2)}, u32[]{:S(2)}) collective-permute-start(bf16[2,128,768]{2,1,0:T(8,128)(2,1)} %collective-permute-done.6.refs_2_), channel_id=1, source_target_pairs={{0,8},{1,9},{2,10},{3,11},{4,12},{5,13},{6,14},{7,15},{8,0},{9,1},... | collective-permute-start | bytes 1179656 | tf_op jit(solution)/shard_map/ppermute | solution.py:46
  77.9 6.2 %collective-permute-start.18 = (bf16[2,128,768]{2,1,0:T(8,128)(2,1)}, bf16[2,128,768]{2,1,0:T(8,128)(2,1)S(1)}, u32[]{:S(2)}, u32[]{:S(2)}) collective-permute-start(bf16[2,128,768]{2,1,0:T(8,128)(2,1)} %collective-permute-done.7.refs_3_), channel_id=1, source_target_pairs={{0,8},{1,9},{2,10},{3,11},{4,12},{5,13},{6,14},{7,15},{8,0},{9,1},... | collective-permute-start | bytes 1179656 | tf_op jit(solution)/shard_map/ppermute | solution.py:46
  79.2 21.3 %collective-permute-start.12 = (bf16[2,128,512]{2,1,0:T(8,128)(2,1)S(1)}, bf16[2,128,512]{2,1,0:T(8,128)(2,1)S(1)}, u32[]{:S(2)}, u32[]{:S(2)}) collective-permute-start(bf16[2,128,512]{2,1,0:T(8,128)(2,1)S(1)} %slice.7.refs_0_), channel_id=1, source_target_pairs={{0,1},{1,2},{2,3},{3,0},{4,5},{5,6},{6,7},{7,4},{8,9},{9,10},{10,1... | collective-permute-start | bytes 786440 | tf_op jit(solution)/shard_map/ppermute | solution.py:46
  80.5 20.0 %collective-permute-start.13 = (bf16[2,128,512]{2,1,0:T(8,128)(2,1)S(1)}, bf16[2,128,512]{2,1,0:T(8,128)(2,1)S(1)}, u32[]{:S(2)}, u32[]{:S(2)}) collective-permute-start(bf16[2,128,512]{2,1,0:T(8,128)(2,1)S(1)} %slice.7.refs_0_), channel_id=1, source_target_pairs={{0,2},{1,3},{2,0},{3,1},{4,6},{5,7},{6,4},{7,5},{8,10},{9,11},{10,... | collective-permute-start | bytes 786440 | tf_op jit(solution)/shard_map/ppermute | solution.py:46
  82.9 17.6 %collective-permute-start.14 = (bf16[2,128,512]{2,1,0:T(8,128)(2,1)S(1)}, bf16[2,128,512]{2,1,0:T(8,128)(2,1)S(1)}, u32[]{:S(2)}, u32[]{:S(2)}) collective-permute-start(bf16[2,128,512]{2,1,0:T(8,128)(2,1)S(1)} %slice.7.refs_0_), channel_id=1, source_target_pairs={{0,3},{1,0},{2,1},{3,2},{4,7},{5,4},{6,5},{7,6},{8,11},{9,8},{10,9... | collective-permute-start | bytes 786440 | tf_op jit(solution)/shard_map/ppermute | solution.py:46
  99.5 1.0 copy-start.4
  100.5 2.3 %collective-permute-start.19 = (bf16[2,128,512]{2,1,0:T(8,128)(2,1)S(1)}, bf16[2,128,512]{2,1,0:T(8,128)(2,1)S(1)}, u32[]{:S(2)}, u32[]{:S(2)}) collective-permute-start(bf16[2,128,512]{2,1,0:T(8,128)(2,1)S(1)} %slice.7.refs_0_), channel_id=1, source_target_pairs={{0,8},{1,9},{2,10},{3,11},{4,12},{5,13},{6,14},{7,15},{8,0},{9,1},... | collective-permute-start | bytes 786440 | tf_op jit(solution)/shard_map/ppermute | solution.py:46
  101.6 1.5 %collective-permute-start.20 = (bf16[2,128,512]{2,1,0:T(8,128)(2,1)S(1)}, bf16[2,128,512]{2,1,0:T(8,128)(2,1)S(1)}, u32[]{:S(2)}, u32[]{:S(2)}) collective-permute-start(bf16[2,128,512]{2,1,0:T(8,128)(2,1)S(1)} %collective-permute-done.12.refs_1_), channel_id=1, source_target_pairs={{0,8},{1,9},{2,10},{3,11},{4,12},{5,13},{6,14},{7,15},{8,0},{9,1},... | collective-permute-start | bytes 786440 | tf_op jit(solution)/shard_map/ppermute | solution.py:46
  102.0 1.6 %collective-permute-start.21 = (bf16[2,128,512]{2,1,0:T(8,128)(2,1)S(1)}, bf16[2,128,512]{2,1,0:T(8,128)(2,1)S(1)}, u32[]{:S(2)}, u32[]{:S(2)}) collective-permute-start(bf16[2,128,512]{2,1,0:T(8,128)(2,1)S(1)} %collective-permute-done.13.refs_2_), channel_id=1, source_target_pairs={{0,8},{1,9},{2,10},{3,11},{4,12},{5,13},{6,14},{7,15},{8,0},{9,1},... | collective-permute-start | bytes 786440 | tf_op jit(solution)/shard_map/ppermute | solution.py:46
  102.1 1.8 %collective-permute-start.22 = (bf16[2,128,512]{2,1,0:T(8,128)(2,1)S(1)}, bf16[2,128,512]{2,1,0:T(8,128)(2,1)S(1)}, u32[]{:S(2)}, u32[]{:S(2)}) collective-permute-start(bf16[2,128,512]{2,1,0:T(8,128)(2,1)S(1)} %collective-permute-done.14.refs_3_), channel_id=1, source_target_pairs={{0,8},{1,9},{2,10},{3,11},{4,12},{5,13},{6,14},{7,15},{8,0},{9,1},... | collective-permute-start | bytes 786440 | tf_op jit(solution)/shard_map/ppermute | solution.py:46
  104.0 1.2 %copy-start.5 = (bf16[1024,512]{1,0:T(8,128)(2,1)S(1)}, bf16[1024,512]{1,0:T(8,128)(2,1)}, u32[]{:S(2)}) copy-start(bf16[1024,512]{1,0:T(8,128)(2,1)} %copy-done.4) | copy-start | bytes 3145732

commit v8 on v6

--- a/solution.py
+++ b/solution.py
@@ -188,54 +188,49 @@
     return ((place >> 1) & 1) * 16 + z * 2 + (place & 1)
 
 
-def place_of(row):
-    z = ((row >> 1) & 1) * 4 + ((row >> 2) & 1) * 2 + ((row >> 3) & 1)
-    return z * 4 + (row >> 4) * 2 + (row & 1)
-
-
-WIDE = 16
-STEP = 32 * WIDE
-
-
-def one_hot(ref, lane_of):
-    wanted = lane_of(lax.broadcasted_iota(jnp.int32, (STEP, 128), 0))
-    lane = lax.broadcasted_iota(jnp.int32, (STEP, 128), 1)
-    for at in range(0, STEP, 128):
-        ref[:, at : at + 128] = jnp.where(wanted == lane + at, 1.0, 0.0).astype(BF16)
+CHUNK = 16
+TILE = CHUNK * CHUNK
 
 
 def col_kernel(x_hbm, *refs):
-    o_hbm, x, w, out, mask_ref, sort_ref, back_ref, normed_ref, sems, sems_x, sems_o = refs[8:]
-    steps = x.shape[1] // WIDE
+    o_hbm, x, w, out, mask_ref, turn_ref, normed_ref, sems, sems_x, sems_o = refs[8:]
+    steps = x.shape[1] // CHUNK
     arrive, leave = [], []
     for i in range(steps):
-        at = pl.ds(i * WIDE, WIDE)
+        at = pl.ds(i * CHUNK, CHUNK)
         arrive.append(pltpu.make_async_copy(x_hbm.at[:, at, :], x.at[:, at, :], sems_x.at[i]))
         leave.append(pltpu.make_async_copy(out.at[:, at, :], o_hbm.at[:, at, :], sems_o.at[i]))
         arrive[i].start()
     weights = fetch_weights(refs[:8], w, sems)
     at = lax.broadcasted_iota(jnp.int32, (128, 128), 0)
     to = lax.broadcasted_iota(jnp.int32, (128, 128), 1)
-    meets = jnp.logical_and(at // 32 == to // 32, to <= at)
+    query_row = sequence_row((at >> 6) * CHUNK + (at & 15))
+    key_row = sequence_row((to >> 6) * CHUNK + (to & 15))
+    meets = jnp.logical_and(((at ^ to) & 48) == 0, key_row <= query_row)
     mask_ref[...] = jnp.where(meets, 0.0, -jnp.inf)
-    one_hot(sort_ref, lambda new: place_of(new & 31) * WIDE + (new >> 5))
-    one_hot(back_ref, lambda old: (old & (WIDE - 1)) * 32 + sequence_row(old >> 4))
+    new = lax.broadcasted_iota(jnp.int32, (TILE, TILE), 0)
+    old = lax.broadcasted_iota(jnp.int32, (TILE, TILE), 1)
+    turn_ref[...] = jnp.where(new == (old & 15) * CHUNK + (old >> 4), 1.0, 0.0).astype(BF16)
     for i in range(steps):
         arrive[i].wait()
-        taken = x[:, i * WIDE : (i + 1) * WIDE, :].reshape(STEP, D)
         for half in range(2):
-            rows = slice(half * 256, half * 256 + 256)
-            ordered = jnp.dot(sort_ref[rows, :], taken, preferred_element_type=F32)
-            normed_ref[i * STEP + half * 256 : i * STEP + half * 256 + 256, :] = normalized(ordered)
+            taken = x[half * CHUNK : (half + 1) * CHUNK, i * CHUNK : (i + 1) * CHUNK, :]
+            ordered = jnp.dot(
+                turn_ref[...], taken.reshape(TILE, D), preferred_element_type=F32
+            )
+            normed = normalized(ordered)
+            for block in range(4):
+                start = i * 2 * TILE + block * 128 + half * 64
+                normed_ref[start : start + 64, :] = normed[block * 64 : (block + 1) * 64, :]
     for copy in weights:
         copy.wait()
     for i in range(steps):
         attended = []
-        for group in range(STEP // 256):
-            start = i * STEP + group * 256
+        for group in range(2):
+            start = (i * 2 + group) * TILE
             parts = [
                 jnp.dot(
-                    normed_ref[start : start + 256, :], w[half], preferred_element_type=F32
+                    normed_ref[start : start + TILE, :], w[half], preferred_element_type=F32
                 ).astype(BF16)
                 for half in range(2)
             ]
@@ -252,13 +247,16 @@
             scores = [block_scores(q, k) for q, k, _ in blocks]
             shares = [block_weights(score, mask_ref[...]) for score in scores]
             done = [block_average(share, v) for share, (_, _, v) in zip(shares, blocks)]
-            attended.append(jnp.concatenate(
-                [jnp.concatenate(done[n::2], 1) for n in range(2)], 0
-            ))
-        back = jnp.dot(
-            back_ref[...], jnp.concatenate(attended, 0), preferred_element_type=F32
-        ).astype(BF16)
-        out[:, i * WIDE : (i + 1) * WIDE, :] = back.reshape(32, WIDE, HALF)
+            attended += [jnp.concatenate(done[n::2], 1) for n in range(2)]
+        for half in range(2):
+            back = jnp.dot(
+                turn_ref[...],
+                jnp.concatenate([block[half * 64 : half * 64 + 64] for block in attended], 0),
+                preferred_element_type=F32,
+            ).astype(BF16)
+            out[half * CHUNK : (half + 1) * CHUNK, i * CHUNK : (i + 1) * CHUNK, :] = back.reshape(
+                CHUNK, CHUNK, HALF
+            )
         leave[i].start()
     for copy in leave:
         copy.wait()
@@ -351,12 +349,11 @@
             pltpu.VMEM((2, D, QKV), BF16),
             pltpu.VMEM((rows, cols, HALF), BF16),
             pltpu.VMEM((128, 128), F32),
-            pltpu.VMEM((STEP, STEP), BF16),
-            pltpu.VMEM((STEP, STEP), BF16),
+            pltpu.VMEM((TILE, TILE), BF16),
             pltpu.VMEM((rows * cols, D), BF16),
             DMA((16,)),
-            DMA((cols // WIDE,)),
-            DMA((cols // WIDE,)),
+            DMA((cols // CHUNK,)),
+            DMA((cols // CHUNK,)),
         ],
         compiler_params=limit(63),
         cost_estimate=pl.CostEstimate(

time: 111 us -> 110 us (level)
  no operation moved by 1% of the time
where the time goes in v8:
time: 110 us
  starting transfers between devices  39.1 us (36%)
  waiting for transfers between devices  36.3 us (33%)
  Pallas kernels  29.9 us (27%)
  local copies, waits for them, and re-layouts  3.13 us (3%)
  between operations  1.1 us (1%)
    ppermute x23, starting transfers between devices, send(): return lax.ppermute(value, BOTH, where)  22.6 us
    ppermute x23, waiting for transfers between devices, send(): return lax.ppermute(value, BOTH, where)  22 us
    all_to_all x2, starting transfers between devices, exchange(): lax.all_to_all(blocks, 'seq', split_axis=0, concat_axis=0, tiled=True, ax...  16.5 us
    all_to_all x2, waiting for transfers between devices, exchange(): lax.all_to_all(blocks, 'seq', split_axis=0, concat_axis=0, tiled=True, ax...  14.3 us
    pallas_call x1, Pallas kernels, row_heads(): pl.pallas_call(row_kernel, out_shape=jax.ShapeDtypeStruct((STRIDE, HALF),...  13.7 us
    pallas_call x1, Pallas kernels, col_heads(): pl.pallas_call(col_kernel, out_shape=jax.ShapeDtypeStruct((rows, cols, HA...  10.1 us
    pallas_call x1, Pallas kernels, project_out(): pl.pallas_call(out_kernel, out_shape=jax.ShapeDtypeStruct((STRIDE, D), BF...  5.95 us
    unnamed x38, local copies, waits for them, and re-layouts  2.31 us
  transfers between devices with their start and end apart: 25, of which 10 were waited for; matrix products, arithmetic and copies ran while one was open for 1% of the time, Pallas kernels for 22%

profile of v8, /device:TPU:1, one launch (start us, length us, event | category | flops | bytes accessed | tf_op | source)
XLA Modules:
  0.0 109.6 jit_solution(13894978592143907373)
XLA Ops:
  0.0 11.3 %all-to-all-start = ((bf16[32,32,1024]{2,1,0:T(8,128)(2,1)}), bf16[32,32,1024]{2,1,0:T(8,128)(2,1)}, u32[]{:S(2)}, u32[]{:S(2)}) async-start(bf16[32,32,1024]{2,1,0:T(8,128)(2,1)} %bitcast.10), calls=%async_computation | async-start | bytes 4194304 | tf_op jit(solution)/shard_map/all_to_all | solution.py:394
  12.0 0.2 rebuilt_half.1
  12.2 2.9 %collective-permute-start.1 = (bf16[128,768]{1,0:T(8,128)(2,1)S(1)}, bf16[128,768]{1,0:T(8,128)(2,1)S(1)}, u32[]{:S(2)}, u32[]{:S(2)}) collective-permute-start(bf16[128,768]{1,0:T(8,128)(2,1)S(1)} %get-tuple-element.24), channel_id=1, source_target_pairs={{0,132},{1,133},{2,134},{3,135},{4,128},{5,129},{6,130},{7,131},{8... | collective-permute-start | bytes 589832 | tf_op jit(solution)/shard_map/ppermute | solution.py:46
  15.1 0.1 collective-permute-start
  15.2 4.9 %collective-permute-done.1 = bf16[128,768]{1,0:T(8,128)(2,1)S(1)} collective-permute-done((bf16[128,768]{1,0:T(8,128)(2,1)S(1)}, bf16[128,768]{1,0:T(8,128)(2,1)S(1)}, u32[]{:S(2)}, u32[]{:S(2)}) %collective-permute-start.1) | collective-permute-done | bytes 196640 | tf_op jit(solution)/shard_map/ppermute | solution.py:46
  20.2 1.3 %collective-permute-start.2 = (bf16[2,128,768]{2,1,0:T(8,128)(2,1)S(1)}, bf16[2,128,768]{2,1,0:T(8,128)(2,1)S(1)}, u32[]{:S(2)}, u32[]{:S(2)}) collective-permute-start(bf16[2,128,768]{2,1,0:T(8,128)(2,1)S(1)} %pad_maximum_fusion.1.refs_0_), channel_id=1, source_target_pairs={{0,1},{1,2},{2,3},{3,0},{4,5},{5,6},{6,7},{7,4},{8,9},{9,10},{10,1... | collective-permute-start | bytes 1179656 | tf_op jit(solution)/shard_map/ppermute | solution.py:46
  21.5 2.5 %collective-permute-start.3 = (bf16[2,128,768]{2,1,0:T(8,128)(2,1)S(1)}, bf16[2,128,768]{2,1,0:T(8,128)(2,1)S(1)}, u32[]{:S(2)}, u32[]{:S(2)}) collective-permute-start(bf16[2,128,768]{2,1,0:T(8,128)(2,1)S(1)} %pad_maximum_fusion.1.refs_0_), channel_id=1, source_target_pairs={{0,2},{1,3},{2,0},{3,1},{4,6},{5,7},{6,4},{7,5},{8,10},{9,11},{10,... | collective-permute-start | bytes 1179656 | tf_op jit(solution)/shard_map/ppermute | solution.py:46
  23.9 1.2 %collective-permute-start.4 = (bf16[2,128,768]{2,1,0:T(8,128)(2,1)S(1)}, bf16[2,128,768]{2,1,0:T(8,128)(2,1)S(1)}, u32[]{:S(2)}, u32[]{:S(2)}) collective-permute-start(bf16[2,128,768]{2,1,0:T(8,128)(2,1)S(1)} %pad_maximum_fusion.1.refs_0_), channel_id=1, source_target_pairs={{0,3},{1,0},{2,1},{3,2},{4,7},{5,4},{6,5},{7,6},{8,11},{9,8},{10,9... | collective-permute-start | bytes 1179656 | tf_op jit(solution)/shard_map/ppermute | solution.py:46
  25.1 2.1 %collective-permute-done = bf16[128,1280]{1,0:T(8,128)(2,1)S(1)} collective-permute-done((bf16[128,1280]{1,0:T(8,128)(2,1)S(1)}, bf16[128,1280]{1,0:T(8,128)(2,1)S(1)}, u32[]{:S(2)}, u32[]{:S(2)}) %collective-permute-start) | collective-permute-done | bytes 327712 | tf_op jit(solution)/shard_map/ppermute | solution.py:46
  27.2 0.1 pad_maximum_fusion
  27.2 3.6 %collective-permute-done.2.refs_1_ = bf16[2,128,768]{2,1,0:T(8,128)(2,1)S(1)} collective-permute-done((bf16[2,128,768]{2,1,0:T(8,128)(2,1)S(1)}, bf16[2,128,768]{2,1,0:T(8,128)(2,1)S(1)}, u32[]{:S(2)}, u32[]{:S(2)}) %collective-permute-start.2) | collective-permute-done | bytes 393248 | tf_op jit(solution)/shard_map/ppermute | solution.py:46
  30.8 9.4 %collective-permute-done.3.refs_2_ = bf16[2,128,768]{2,1,0:T(8,128)(2,1)S(1)} collective-permute-done((bf16[2,128,768]{2,1,0:T(8,128)(2,1)S(1)}, bf16[2,128,768]{2,1,0:T(8,128)(2,1)S(1)}, u32[]{:S(2)}, u32[]{:S(2)}) %collective-permute-start.3) | collective-permute-done | bytes 393248 | tf_op jit(solution)/shard_map/ppermute | solution.py:46
  40.2 0.3 collective-permute-done.4.refs_3_
  40.5 2.0 %collective-permute-start.10 = (bf16[2,128,768]{2,1,0:T(8,128)(2,1)S(1)}, bf16[2,128,768]{2,1,0:T(8,128)(2,1)S(1)}, u32[]{:S(2)}, u32[]{:S(2)}) collective-permute-start(bf16[2,128,768]{2,1,0:T(8,128)(2,1)S(1)} %collective-permute-done.3.refs_2_), channel_id=1, source_target_pairs={{0,8},{1,9},{2,10},{3,11},{4,12},{5,13},{6,14},{7,15},{8,0},{9,1},... | collective-permute-start | bytes 1179656 | tf_op jit(solution)/shard_map/ppermute | solution.py:46
  42.5 0.1 collective-permute-start.11
  42.6 0.4 collective-permute-start.8
  43.0 0.1 collective-permute-start.9
  43.1 0.8 slice.6.refs_0_
  43.9 0.9 collective-permute-start.5
  44.8 0.0 collective-permute-done.10.refs_6_
  44.8 2.2 %collective-permute-start.6 = (bf16[2,128,768]{2,1,0:T(8,128)(2,1)}, bf16[2,128,768]{2,1,0:T(8,128)(2,1)}, u32[]{:S(2)}, u32[]{:S(2)}) collective-permute-start(bf16[2,128,768]{2,1,0:T(8,128)(2,1)} %slice.6.refs_0_), channel_id=1, source_target_pairs={{0,2},{1,3},{2,0},{3,1},{4,6},{5,7},{6,4},{7,5},{8,10},{9,11},{10,... | collective-permute-start | bytes 1179656 | tf_op jit(solution)/shard_map/ppermute | solution.py:46
  47.0 0.0 collective-permute-done.11.refs_7_
  47.0 1.2 %collective-permute-start.7 = (bf16[2,128,768]{2,1,0:T(8,128)(2,1)}, bf16[2,128,768]{2,1,0:T(8,128)(2,1)}, u32[]{:S(2)}, u32[]{:S(2)}) collective-permute-start(bf16[2,128,768]{2,1,0:T(8,128)(2,1)} %slice.6.refs_0_), channel_id=1, source_target_pairs={{0,3},{1,0},{2,1},{3,2},{4,7},{5,4},{6,5},{7,6},{8,11},{9,8},{10,9... | collective-permute-start | bytes 1179656 | tf_op jit(solution)/shard_map/ppermute | solution.py:46
  48.3 0.7 copy-done.12
  49.0 12.2 %all-to-all-done.x_hbm = bf16[32,32,1024]{2,1,0:T(8,128)(2,1)} async-done(((bf16[32,32,1024]{2,1,0:T(8,128)(2,1)}), bf16[32,32,1024]{2,1,0:T(8,128)(2,1)}, u32[]{:S(2)}, u32[]{:S(2)}) %all-to-all-start) | async-done | bytes 2097184 | tf_op jit(solution)/shard_map/all_to_all | solution.py:394
  61.2 10.1 %col_heads.1 = bf16[32,32,512]{2,1,0:T(8,128)(2,1)} custom-call(bf16[32,32,1024]{2,1,0:T(8,128)(2,1)} %all-to-all-done.x_hbm, bf16[2,128,768]{2,1,0:T(8,128)(2,1)} %copy-done.4, bf16[2,128,768]{2,1,0:T(8,128)(2,1)} %copy-done.6, bf16[2,128,768]{2,1,0:T(8,128)(2,1)} %copy-done.7, bf16[2,128,768]{2,1,0:T(8,128)(2,1)} %copy-done.8, ...), custom_call_target="tpu_custom_call" | custom-call | flops 4000000000 | bytes 6291456 | tf_op jit(solution)/shard_map/col_heads/pallas_call | solution.py:342
  71.3 0.0 collective-permute-done.5.refs_1_
  71.3 0.0 collective-permute-done.6.refs_2_
  71.3 5.2 %all-to-all-start.1 = ((bf16[32,32,512]{2,1,0:T(8,128)(2,1)}), bf16[32,32,512]{2,1,0:T(8,128)(2,1)}, u32[]{:S(2)}, u32[]{:S(2)}) async-start(bf16[32,32,512]{2,1,0:T(8,128)(2,1)} %col_heads.1), calls=%async_computation.1 | async-start | bytes 2097152 | tf_op jit(solution)/shard_map/all_to_all | solution.py:394
  76.5 0.4 collective-permute-start.15
  76.8 0.2 collective-permute-start.16
  77.0 0.3 collective-permute-start.17
  77.4 0.2 collective-permute-start.18
  77.6 1.3 %collective-permute-start.12 = (bf16[2,128,512]{2,1,0:T(8,128)(2,1)S(1)}, bf16[2,128,512]{2,1,0:T(8,128)(2,1)S(1)}, u32[]{:S(2)}, u32[]{:S(2)}) collective-permute-start(bf16[2,128,512]{2,1,0:T(8,128)(2,1)S(1)} %slice.7.refs_0_), channel_id=1, source_target_pairs={{0,1},{1,2},{2,3},{3,0},{4,5},{5,6},{6,7},{7,4},{8,9},{9,10},{10,1... | collective-permute-start | bytes 786440 | tf_op jit(solution)/shard_map/ppermute | solution.py:46
  78.9 2.4 %collective-permute-start.13 = (bf16[2,128,512]{2,1,0:T(8,128)(2,1)S(1)}, bf16[2,128,512]{2,1,0:T(8,128)(2,1)S(1)}, u32[]{:S(2)}, u32[]{:S(2)}) collective-permute-start(bf16[2,128,512]{2,1,0:T(8,128)(2,1)S(1)} %slice.7.refs_0_), channel_id=1, source_target_pairs={{0,2},{1,3},{2,0},{3,1},{4,6},{5,7},{6,4},{7,5},{8,10},{9,11},{10,... | collective-permute-start | bytes 786440 | tf_op jit(solution)/shard_map/ppermute | solution.py:46
  81.3 0.8 copy-done.13
  82.1 1.2 %collective-permute-start.14 = (bf16[2,128,512]{2,1,0:T(8,128)(2,1)S(1)}, bf16[2,128,512]{2,1,0:T(8,128)(2,1)}, u32[]{:S(2)}, u32[]{:S(2)}) collective-permute-start(bf16[2,128,512]{2,1,0:T(8,128)(2,1)S(1)} %slice.7.refs_0_), channel_id=1, source_target_pairs={{0,3},{1,0},{2,1},{3,2},{4,7},{5,4},{6,5},{7,6},{8,11},{9,8},{10,9... | collective-permute-start | bytes 786440 | tf_op jit(solution)/shard_map/ppermute | solution.py:46
  83.3 13.7 %row_heads.1.row_hbm = bf16[1024,512]{1,0:T(8,128)(2,1)} custom-call(bf16[1024,1024]{1,0:T(8,128)(2,1)} %bitcast.11, bf16[2,128,768]{2,1,0:T(8,128)(2,1)} %slice.6.refs_0_, bf16[2,128,768]{2,1,0:T(8,128)(2,1)} %collective-permute-done.5.refs_1_, bf16[2,128,768]{2,1,0:T(8,128)(2,1)} %collective-permute-done.6.refs_2_, ...), custom_call_target="tpu_custom_call" | custom-call | flops 6000000000 | bytes 6291456 | tf_op jit(solution)/shard_map/row_heads/pallas_call | solution.py:316
  97.0 1.2 %collective-permute-start.19 = (bf16[2,128,512]{2,1,0:T(8,128)(2,1)S(1)}, bf16[2,128,512]{2,1,0:T(8,128)(2,1)S(1)}, u32[]{:S(2)}, u32[]{:S(2)}) collective-permute-start(bf16[2,128,512]{2,1,0:T(8,128)(2,1)S(1)} %slice.7.refs_0_), channel_id=1, source_target_pairs={{0,8},{1,9},{2,10},{3,11},{4,12},{5,13},{6,14},{7,15},{8,0},{9,1},... | collective-permute-start | bytes 786440 | tf_op jit(solution)/shard_map/ppermute | solution.py:46
  98.3 0.1 collective-permute-start.20
  98.4 0.4 collective-permute-start.21
  98.8 0.1 collective-permute-start.22
  98.9 0.6 collective-permute-done.19.refs_4_
  99.4 0.4 collective-permute-done.20.refs_5_
  99.8 0.7 collective-permute-done.21.refs_6_
  100.6 0.7 copy-done.18
  101.3 2.1 %all-to-all-done.1 = bf16[32,32,512]{2,1,0:T(8,128)(2,1)} async-done(((bf16[32,32,512]{2,1,0:T(8,128)(2,1)}), bf16[32,32,512]{2,1,0:T(8,128)(2,1)}, u32[]{:S(2)}, u32[]{:S(2)}) %all-to-all-start.1) | async-done | bytes 1048608 | tf_op jit(solution)/shard_map/all_to_all | solution.py:394
  103.4 6.0 %project_out.1 = bf16[1024,1024]{1,0:T(8,128)(2,1)} custom-call(bf16[1024,512]{1,0:T(8,128)(2,1)} %row_heads.1.row_hbm, bf16[1024,512]{1,0:T(8,128)(2,1)} %bitcast.6.col_hbm, bf16[2,128,512]{2,1,0:T(8,128)(2,1)} %copy-done.5, bf16[2,128,512]{2,1,0:T(8,128)(2,1)} %copy-done.14, bf16[2,128,512]{2,1,0:T(8,128)(2,1)} %copy-done.15, ...), custom_call_target="tpu_custom_call" | custom-call | flops 2000000000 | bytes 6291456 | tf_op jit(solution)/shard_map/project_out/pallas_call | solution.py:367
  (48 shorter events, 0.2 us)
Async XLA Ops:
  0.0 12.0 %copy-start = (bf16[128,3072]{1,0:T(8,128)(2,1)S(1)}, bf16[128,3072]{1,0:T(8,128)(2,1)}, u32[]{:S(2)}) copy-start(bf16[128,3072]{1,0:T(8,128)(2,1)} %qb_ref.1) | copy-start | bytes 2359300
  0.0 12.0 %copy-start.1 = (bf16[128,3072]{1,0:T(8,128)(2,1)S(1)}, bf16[128,3072]{1,0:T(8,128)(2,1)}, u32[]{:S(2)}) copy-start(bf16[128,3072]{1,0:T(8,128)(2,1)} %qd_ref.1) | copy-start | bytes 2359300
  0.0 12.0 %copy-start.2 = (bf16[128,1024]{1,0:T(8,128)(2,1)S(1)}, bf16[128,1024]{1,0:T(8,128)(2,1)}, u32[]{:S(2)}) copy-start(bf16[128,1024]{1,0:T(8,128)(2,1)} %ob_ref.1) | copy-start | bytes 786436
  0.0 12.0 %copy-start.3 = (bf16[128,1024]{1,0:T(8,128)(2,1)S(1)}, bf16[128,1024]{1,0:T(8,128)(2,1)}, u32[]{:S(2)}) copy-start(bf16[128,1024]{1,0:T(8,128)(2,1)} %od_ref.1) | copy-start | bytes 786436
  0.0 61.2 %all-to-all-start = ((bf16[32,32,1024]{2,1,0:T(8,128)(2,1)}), bf16[32,32,1024]{2,1,0:T(8,128)(2,1)}, u32[]{:S(2)}, u32[]{:S(2)}) async-start(bf16[32,32,1024]{2,1,0:T(8,128)(2,1)} %bitcast.10), calls=%async_computation | async-start | bytes 4194304 | tf_op jit(solution)/shard_map/all_to_all | solution.py:394
  12.2 7.9 %collective-permute-start.1 = (bf16[128,768]{1,0:T(8,128)(2,1)S(1)}, bf16[128,768]{1,0:T(8,128)(2,1)S(1)}, u32[]{:S(2)}, u32[]{:S(2)}) collective-permute-start(bf16[128,768]{1,0:T(8,128)(2,1)S(1)} %get-tuple-element.24), channel_id=1, source_target_pairs={{0,132},{1,133},{2,134},{3,135},{4,128},{5,129},{6,130},{7,131},{8... | collective-permute-start | bytes 589832 | tf_op jit(solution)/shard_map/ppermute | solution.py:46
  15.1 12.0 %collective-permute-start = (bf16[128,1280]{1,0:T(8,128)(2,1)S(1)}, bf16[128,1280]{1,0:T(8,128)(2,1)S(1)}, u32[]{:S(2)}, u32[]{:S(2)}) collective-permute-start(bf16[128,1280]{1,0:T(8,128)(2,1)S(1)} %get-tuple-element.23), channel_id=1, source_target_pairs={{0,132},{1,133},{2,134},{3,135},{4,128},{5,129},{6,130},{7,131},{8... | collective-permute-start | bytes 983048 | tf_op jit(solution)/shard_map/ppermute | solution.py:46
  20.2 22.4 %copy-start.4 = (bf16[2,128,768]{2,1,0:T(8,128)(2,1)}, bf16[2,128,768]{2,1,0:T(8,128)(2,1)S(1)}, u32[]{:S(2)}) copy-start(bf16[2,128,768]{2,1,0:T(8,128)(2,1)S(1)} %pad_maximum_fusion.1.refs_0_) | copy-start | bytes 1179652
  20.2 10.6 %collective-permute-start.2 = (bf16[2,128,768]{2,1,0:T(8,128)(2,1)S(1)}, bf16[2,128,768]{2,1,0:T(8,128)(2,1)S(1)}, u32[]{:S(2)}, u32[]{:S(2)}) collective-permute-start(bf16[2,128,768]{2,1,0:T(8,128)(2,1)S(1)} %pad_maximum_fusion.1.refs_0_), channel_id=1, source_target_pairs={{0,1},{1,2},{2,3},{3,0},{4,5},{5,6},{6,7},{7,4},{8,9},{9,10},{10,1... | collective-permute-start | bytes 1179656 | tf_op jit(solution)/shard_map/ppermute | solution.py:46
  21.5 18.7 %collective-permute-start.3 = (bf16[2,128,768]{2,1,0:T(8,128)(2,1)S(1)}, bf16[2,128,768]{2,1,0:T(8,128)(2,1)S(1)}, u32[]{:S(2)}, u32[]{:S(2)}) collective-permute-start(bf16[2,128,768]{2,1,0:T(8,128)(2,1)S(1)} %pad_maximum_fusion.1.refs_0_), channel_id=1, source_target_pairs={{0,2},{1,3},{2,0},{3,1},{4,6},{5,7},{6,4},{7,5},{8,10},{9,11},{10,... | collective-permute-start | bytes 1179656 | tf_op jit(solution)/shard_map/ppermute | solution.py:46
  23.9 16.6 %collective-permute-start.4 = (bf16[2,128,768]{2,1,0:T(8,128)(2,1)S(1)}, bf16[2,128,768]{2,1,0:T(8,128)(2,1)S(1)}, u32[]{:S(2)}, u32[]{:S(2)}) collective-permute-start(bf16[2,128,768]{2,1,0:T(8,128)(2,1)S(1)} %pad_maximum_fusion.1.refs_0_), channel_id=1, source_target_pairs={{0,3},{1,0},{2,1},{3,2},{4,7},{5,4},{6,5},{7,6},{8,11},{9,8},{10,9... | collective-permute-start | bytes 1179656 | tf_op jit(solution)/shard_map/ppermute | solution.py:46
  30.8 17.4 %copy-start.6 = (bf16[2,128,768]{2,1,0:T(8,128)(2,1)}, bf16[2,128,768]{2,1,0:T(8,128)(2,1)S(1)}, u32[]{:S(2)}) copy-start(bf16[2,128,768]{2,1,0:T(8,128)(2,1)S(1)} %collective-permute-done.2.refs_1_) | copy-start | bytes 1179652
  40.2 8.0 %copy-start.7 = (bf16[2,128,768]{2,1,0:T(8,128)(2,1)}, bf16[2,128,768]{2,1,0:T(8,128)(2,1)S(1)}, u32[]{:S(2)}) copy-start(bf16[2,128,768]{2,1,0:T(8,128)(2,1)S(1)} %collective-permute-done.3.refs_2_) | copy-start | bytes 1179652
  40.5 7.7 %copy-start.8 = (bf16[2,128,768]{2,1,0:T(8,128)(2,1)}, bf16[2,128,768]{2,1,0:T(8,128)(2,1)S(1)}, u32[]{:S(2)}) copy-start(bf16[2,128,768]{2,1,0:T(8,128)(2,1)S(1)} %collective-permute-done.4.refs_3_) | copy-start | bytes 1179652
  40.5 4.3 %collective-permute-start.10 = (bf16[2,128,768]{2,1,0:T(8,128)(2,1)S(1)}, bf16[2,128,768]{2,1,0:T(8,128)(2,1)S(1)}, u32[]{:S(2)}, u32[]{:S(2)}) collective-permute-start(bf16[2,128,768]{2,1,0:T(8,128)(2,1)S(1)} %collective-permute-done.3.refs_2_), channel_id=1, source_target_pairs={{0,8},{1,9},{2,10},{3,11},{4,12},{5,13},{6,14},{7,15},{8,0},{9,1},... | collective-permute-start | bytes 1179656 | tf_op jit(solution)/shard_map/ppermute | solution.py:46
  42.5 4.5 %collective-permute-start.11 = (bf16[2,128,768]{2,1,0:T(8,128)(2,1)S(1)}, bf16[2,128,768]{2,1,0:T(8,128)(2,1)S(1)}, u32[]{:S(2)}, u32[]{:S(2)}) collective-permute-start(bf16[2,128,768]{2,1,0:T(8,128)(2,1)S(1)} %collective-permute-done.4.refs_3_), channel_id=1, source_target_pairs={{0,8},{1,9},{2,10},{3,11},{4,12},{5,13},{6,14},{7,15},{8,0},{9,1},... | collective-permute-start | bytes 1179656 | tf_op jit(solution)/shard_map/ppermute | solution.py:46
  42.6 5.6 %collective-permute-start.8 = (bf16[2,128,768]{2,1,0:T(8,128)(2,1)S(1)}, bf16[2,128,768]{2,1,0:T(8,128)(2,1)S(1)}, u32[]{:S(2)}, u32[]{:S(2)}) collective-permute-start(bf16[2,128,768]{2,1,0:T(8,128)(2,1)S(1)} %pad_maximum_fusion.1.refs_0_), channel_id=1, source_target_pairs={{0,8},{1,9},{2,10},{3,11},{4,12},{5,13},{6,14},{7,15},{8,0},{9,1},... | collective-permute-start | bytes 1179656 | tf_op jit(solution)/shard_map/ppermute | solution.py:46
  43.0 6.0 %collective-permute-start.9 = (bf16[2,128,768]{2,1,0:T(8,128)(2,1)S(1)}, bf16[2,128,768]{2,1,0:T(8,128)(2,1)}, u32[]{:S(2)}, u32[]{:S(2)}) collective-permute-start(bf16[2,128,768]{2,1,0:T(8,128)(2,1)S(1)} %collective-permute-done.2.refs_1_), channel_id=1, source_target_pairs={{0,8},{1,9},{2,10},{3,11},{4,12},{5,13},{6,14},{7,15},{8,0},{9,1},... | collective-permute-start | bytes 1179656 | tf_op jit(solution)/shard_map/ppermute | solution.py:46
  43.9 27.3 %collective-permute-start.5 = (bf16[2,128,768]{2,1,0:T(8,128)(2,1)}, bf16[2,128,768]{2,1,0:T(8,128)(2,1)}, u32[]{:S(2)}, u32[]{:S(2)}) collective-permute-start(bf16[2,128,768]{2,1,0:T(8,128)(2,1)} %slice.6.refs_0_), channel_id=1, source_target_pairs={{0,1},{1,2},{2,3},{3,0},{4,5},{5,6},{6,7},{7,4},{8,9},{9,10},{10,1... | collective-permute-start | bytes 1179656 | tf_op jit(solution)/shard_map/ppermute | solution.py:46
  44.8 3.4 %copy-start.9 = (bf16[2,128,768]{2,1,0:T(8,128)(2,1)}, bf16[2,128,768]{2,1,0:T(8,128)(2,1)S(1)}, u32[]{:S(2)}) copy-start(bf16[2,128,768]{2,1,0:T(8,128)(2,1)S(1)} %collective-permute-done.10.refs_6_) | copy-start | bytes 1179652
  44.8 26.5 %collective-permute-start.6 = (bf16[2,128,768]{2,1,0:T(8,128)(2,1)}, bf16[2,128,768]{2,1,0:T(8,128)(2,1)}, u32[]{:S(2)}, u32[]{:S(2)}) collective-permute-start(bf16[2,128,768]{2,1,0:T(8,128)(2,1)} %slice.6.refs_0_), channel_id=1, source_target_pairs={{0,2},{1,3},{2,0},{3,1},{4,6},{5,7},{6,4},{7,5},{8,10},{9,11},{10,... | collective-permute-start | bytes 1179656 | tf_op jit(solution)/shard_map/ppermute | solution.py:46
  47.0 1.2 %copy-start.10 = (bf16[2,128,768]{2,1,0:T(8,128)(2,1)}, bf16[2,128,768]{2,1,0:T(8,128)(2,1)S(1)}, u32[]{:S(2)}) copy-start(bf16[2,128,768]{2,1,0:T(8,128)(2,1)S(1)} %collective-permute-done.11.refs_7_) | copy-start | bytes 1179652
  47.0 24.2 %collective-permute-start.7 = (bf16[2,128,768]{2,1,0:T(8,128)(2,1)}, bf16[2,128,768]{2,1,0:T(8,128)(2,1)}, u32[]{:S(2)}, u32[]{:S(2)}) collective-permute-start(bf16[2,128,768]{2,1,0:T(8,128)(2,1)} %slice.6.refs_0_), channel_id=1, source_target_pairs={{0,3},{1,0},{2,1},{3,2},{4,7},{5,4},{6,5},{7,6},{8,11},{9,8},{10,9... | collective-permute-start | bytes 1179656 | tf_op jit(solution)/shard_map/ppermute | solution.py:46
  48.2 0.8 copy-start.12
  71.3 32.1 %all-to-all-start.1 = ((bf16[32,32,512]{2,1,0:T(8,128)(2,1)}), bf16[32,32,512]{2,1,0:T(8,128)(2,1)}, u32[]{:S(2)}, u32[]{:S(2)}) async-start(bf16[32,32,512]{2,1,0:T(8,128)(2,1)} %col_heads.1), calls=%async_computation.1 | async-start | bytes 2097152 | tf_op jit(solution)/shard_map/all_to_all | solution.py:394
  76.5 2.4 %collective-permute-start.15 = (bf16[2,128,768]{2,1,0:T(8,128)(2,1)}, bf16[2,128,768]{2,1,0:T(8,128)(2,1)S(1)}, u32[]{:S(2)}, u32[]{:S(2)}) collective-permute-start(bf16[2,128,768]{2,1,0:T(8,128)(2,1)} %slice.6.refs_0_), channel_id=1, source_target_pairs={{0,8},{1,9},{2,10},{3,11},{4,12},{5,13},{6,14},{7,15},{8,0},{9,1},... | collective-permute-start | bytes 1179656 | tf_op jit(solution)/shard_map/ppermute | solution.py:46
  76.8 4.5 %collective-permute-start.16 = (bf16[2,128,768]{2,1,0:T(8,128)(2,1)}, bf16[2,128,768]{2,1,0:T(8,128)(2,1)S(1)}, u32[]{:S(2)}, u32[]{:S(2)}) collective-permute-start(bf16[2,128,768]{2,1,0:T(8,128)(2,1)} %collective-permute-done.5.refs_1_), channel_id=1, source_target_pairs={{0,8},{1,9},{2,10},{3,11},{4,12},{5,13},{6,14},{7,15},{8,0},{9,1},... | collective-permute-start | bytes 1179656 | tf_op jit(solution)/shard_map/ppermute | solution.py:46
  77.0 6.2 %collective-permute-start.17 = (bf16[2,128,768]{2,1,0:T(8,128)(2,1)}, bf16[2,128,768]{2,1,0:T(8,128)(2,1)}, u32[]{:S(2)}, u32[]{:S(2)}) collective-permute-start(bf16[2,128,768]{2,1,0:T(8,128)(2,1)} %collective-permute-done.6.refs_2_), channel_id=1, source_target_pairs={{0,8},{1,9},{2,10},{3,11},{4,12},{5,13},{6,14},{7,15},{8,0},{9,1},... | collective-permute-start | bytes 1179656 | tf_op jit(solution)/shard_map/ppermute | solution.py:46
  77.4 5.9 %collective-permute-start.18 = (bf16[2,128,768]{2,1,0:T(8,128)(2,1)}, bf16[2,128,768]{2,1,0:T(8,128)(2,1)}, u32[]{:S(2)}, u32[]{:S(2)}) collective-permute-start(bf16[2,128,768]{2,1,0:T(8,128)(2,1)} %collective-permute-done.7.refs_3_), channel_id=1, source_target_pairs={{0,8},{1,9},{2,10},{3,11},{4,12},{5,13},{6,14},{7,15},{8,0},{9,1},... | collective-permute-start | bytes 1179656 | tf_op jit(solution)/shard_map/ppermute | solution.py:46
  77.6 19.4 %copy-start.5 = (bf16[2,128,512]{2,1,0:T(8,128)(2,1)}, bf16[2,128,512]{2,1,0:T(8,128)(2,1)S(1)}, u32[]{:S(2)}) copy-start(bf16[2,128,512]{2,1,0:T(8,128)(2,1)S(1)} %slice.7.refs_0_) | copy-start | bytes 786436
  77.6 19.4 %collective-permute-start.12 = (bf16[2,128,512]{2,1,0:T(8,128)(2,1)S(1)}, bf16[2,128,512]{2,1,0:T(8,128)(2,1)S(1)}, u32[]{:S(2)}, u32[]{:S(2)}) collective-permute-start(bf16[2,128,512]{2,1,0:T(8,128)(2,1)S(1)} %slice.7.refs_0_), channel_id=1, source_target_pairs={{0,1},{1,2},{2,3},{3,0},{4,5},{5,6},{6,7},{7,4},{8,9},{9,10},{10,1... | collective-permute-start | bytes 786440 | tf_op jit(solution)/shard_map/ppermute | solution.py:46
  78.9 2.5 %copy-start.11 = (bf16[2,128,768]{2,1,0:T(8,128)(2,1)}, bf16[2,128,768]{2,1,0:T(8,128)(2,1)S(1)}, u32[]{:S(2)}) copy-start(bf16[2,128,768]{2,1,0:T(8,128)(2,1)S(1)} %collective-permute-done.15.refs_4_) | copy-start | bytes 1179652
  78.9 18.1 %collective-permute-start.13 = (bf16[2,128,512]{2,1,0:T(8,128)(2,1)S(1)}, bf16[2,128,512]{2,1,0:T(8,128)(2,1)S(1)}, u32[]{:S(2)}, u32[]{:S(2)}) collective-permute-start(bf16[2,128,512]{2,1,0:T(8,128)(2,1)S(1)} %slice.7.refs_0_), channel_id=1, source_target_pairs={{0,2},{1,3},{2,0},{3,1},{4,6},{5,7},{6,4},{7,5},{8,10},{9,11},{10,... | collective-permute-start | bytes 786440 | tf_op jit(solution)/shard_map/ppermute | solution.py:46
  81.3 0.8 copy-start.13
  82.1 14.9 %collective-permute-start.14 = (bf16[2,128,512]{2,1,0:T(8,128)(2,1)S(1)}, bf16[2,128,512]{2,1,0:T(8,128)(2,1)}, u32[]{:S(2)}, u32[]{:S(2)}) collective-permute-start(bf16[2,128,512]{2,1,0:T(8,128)(2,1)S(1)} %slice.7.refs_0_), channel_id=1, source_target_pairs={{0,3},{1,0},{2,1},{3,2},{4,7},{5,4},{6,5},{7,6},{8,11},{9,8},{10,9... | collective-permute-start | bytes 786440 | tf_op jit(solution)/shard_map/ppermute | solution.py:46
  97.0 6.5 %copy-start.14 = (bf16[2,128,512]{2,1,0:T(8,128)(2,1)}, bf16[2,128,512]{2,1,0:T(8,128)(2,1)S(1)}, u32[]{:S(2)}) copy-start(bf16[2,128,512]{2,1,0:T(8,128)(2,1)S(1)} %collective-permute-done.12.refs_1_) | copy-start | bytes 786436
  97.0 6.4 %copy-start.15 = (bf16[2,128,512]{2,1,0:T(8,128)(2,1)}, bf16[2,128,512]{2,1,0:T(8,128)(2,1)S(1)}, u32[]{:S(2)}) copy-start(bf16[2,128,512]{2,1,0:T(8,128)(2,1)S(1)} %collective-permute-done.13.refs_2_) | copy-start | bytes 786436
  97.0 2.4 %collective-permute-start.19 = (bf16[2,128,512]{2,1,0:T(8,128)(2,1)S(1)}, bf16[2,128,512]{2,1,0:T(8,128)(2,1)S(1)}, u32[]{:S(2)}, u32[]{:S(2)}) collective-permute-start(bf16[2,128,512]{2,1,0:T(8,128)(2,1)S(1)} %slice.7.refs_0_), channel_id=1, source_target_pairs={{0,8},{1,9},{2,10},{3,11},{4,12},{5,13},{6,14},{7,15},{8,0},{9,1},... | collective-permute-start | bytes 786440 | tf_op jit(solution)/shard_map/ppermute | solution.py:46
  98.3 1.5 %collective-permute-start.20 = (bf16[2,128,512]{2,1,0:T(8,128)(2,1)S(1)}, bf16[2,128,512]{2,1,0:T(8,128)(2,1)S(1)}, u32[]{:S(2)}, u32[]{:S(2)}) collective-permute-start(bf16[2,128,512]{2,1,0:T(8,128)(2,1)S(1)} %collective-permute-done.12.refs_1_), channel_id=1, source_target_pairs={{0,8},{1,9},{2,10},{3,11},{4,12},{5,13},{6,14},{7,15},{8,0},{9,1},... | collective-permute-start | bytes 786440 | tf_op jit(solution)/shard_map/ppermute | solution.py:46
  98.4 2.2 %collective-permute-start.21 = (bf16[2,128,512]{2,1,0:T(8,128)(2,1)S(1)}, bf16[2,128,512]{2,1,0:T(8,128)(2,1)S(1)}, u32[]{:S(2)}, u32[]{:S(2)}) collective-permute-start(bf16[2,128,512]{2,1,0:T(8,128)(2,1)S(1)} %collective-permute-done.13.refs_2_), channel_id=1, source_target_pairs={{0,8},{1,9},{2,10},{3,11},{4,12},{5,13},{6,14},{7,15},{8,0},{9,1},... | collective-permute-start | bytes 786440 | tf_op jit(solution)/shard_map/ppermute | solution.py:46
  98.8 2.5 %collective-permute-start.22 = (bf16[2,128,512]{2,1,0:T(8,128)(2,1)}, bf16[2,128,512]{2,1,0:T(8,128)(2,1)}, u32[]{:S(2)}, u32[]{:S(2)}) collective-permute-start(bf16[2,128,512]{2,1,0:T(8,128)(2,1)} %collective-permute-done.14.refs_3_), channel_id=1, source_target_pairs={{0,8},{1,9},{2,10},{3,11},{4,12},{5,13},{6,14},{7,15},{8,0},{9,1},... | collective-permute-start | bytes 786440 | tf_op jit(solution)/shard_map/ppermute | solution.py:46
  99.4 1.1 %copy-start.16 = (bf16[2,128,512]{2,1,0:T(8,128)(2,1)}, bf16[2,128,512]{2,1,0:T(8,128)(2,1)S(1)}, u32[]{:S(2)}) copy-start(bf16[2,128,512]{2,1,0:T(8,128)(2,1)S(1)} %collective-permute-done.19.refs_4_) | copy-start | bytes 786436
  99.8 0.8 copy-start.17
  100.6 0.7 copy-start.18
